TPU v7x, 32 devices: a whole 2x2x4 slice. The times are simulated.
32 devices in a mesh: tp: 2 (over y), dp: 4 (over z), rep: 4 (over x, core).
Axes of the slice: x: 2, y: 2, z: 4, core: 2. Of those that a mesh axis runs over, the one named last changes fastest.
Arguments:
- layer_input: bfloat16 [16, 1024, 768], P(('dp', 'rep'), 'tp'), may hold values from -6 to 6
- history: bfloat16 [4, 16, 1024, 768], P(None, ('dp', 'rep'), 'tp'), may hold values from -6 to 6
- cotangent: bfloat16 [16, 1024, 768], P(('dp', 'rep'), 'tp'), may hold values from -6 to 6
- lengths: int32 [16, 3], P(('dp', 'rep')), may hold values from 1 to 512, 1024 in all within a row
- dwa_weights: float32 [5], replicated, may hold values from 0.2 to 1
- gain_one: float32 [768], replicated, may hold values from 0.1 to 1.9
- bias_one: float32 [768], replicated, may hold values from -3 to 3
- w_qkv: bfloat16 [3, 768, 768], P(None, None, 'tp'), may hold values from -0.21875 to 0.21875
- w_out: bfloat16 [768, 768], P('tp'), may hold values from -1.75 to 1.75
- gain_two: float32 [768], replicated, may hold values from 0.1 to 1.9
- bias_two: float32 [768], replicated, may hold values from -3 to 3
- w_up: bfloat16 [768, 3072], P(None, 'tp'), may hold values from -0.21875 to 0.21875
- w_down: bfloat16 [3072, 768], P('tp'), may hold values from -0.109375 to 0.109375
Outputs:
- output: bfloat16 [16, 1024, 768], P(('dp', 'rep'), 'tp')
- grad_input: bfloat16 [16, 1024, 768], P(('dp', 'rep'), 'tp')
- grad_history: bfloat16 [4, 16, 1024, 768], P(None, ('dp', 'rep'), 'tp')
- grad_dwa: float32 [5], replicated
- grad_gain_one: float32 [768], replicated
- grad_bias_one: float32 [768], replicated
- grad_w_qkv: float32 [3, 768, 768], P(None, 'dp', 'tp')
- grad_w_out: float32 [768, 768], P('tp', 'dp')
- grad_gain_two: float32 [768], replicated
- grad_bias_two: float32 [768], replicated
- grad_w_up: float32 [768, 3072], P('dp', 'tp')
- grad_w_down: float32 [3072, 768], P('tp', 'dp')
Inputs may be any that keep to these rules, and one draw needn't show every extreme that they name: Row g lists in order the lengths of the 3 sequences packed into group g; they sum to 1024 and the largest of each row is 512.
All inputs are finite; a program needn't handle non-finite values.
Results may differ from a plain program's by a relative error of at most 0.02.
Values may be sent and summed in bfloat16 or wider, within the bound.
No kernel may reach another device: no remote copies, remote signals or barrier semaphores. Data moves between devices by JAX's collectives and lax.ppermute only.
A program may use at most 128 MiB of HBM per device.

v0:
```python
import functools
import math

import jax
import jax.numpy as jnp
from jax import lax
from jax.experimental import pallas as pl
from jax.experimental.pallas import tpu as pltpu
from jax.sharding import PartitionSpec as P

HEAD_DIM = 64
LONGEST = 512
NEG_FILL = -1e30
NORM_EPS = 1e-05
BLOCK = 256
LANES = 128
NT = (((1,), (1,)), ((), ()))


def dot(a, b, dims=(((1,), (0,)), ((), ()))):
    return lax.dot_general(a, b, dims, preferred_element_type=jnp.float32)


def spans(whole, reach):
    back = -(-(reach - 1) // BLOCK)
    runs = []
    for i in range(whole // BLOCK):
        count = min(i, back) + 1
        if runs and runs[-1][2] == count:
            runs[-1][1] = i + 1
        else:
            runs.append([i, i + 1, count])
    return runs


def each_block(whole, reach, body):
    for first, last, count in spans(whole, reach):
        def step(at, carry, first=first, count=count):
            i = first + at // 2
            body(i, i + 1 - count, count * BLOCK, at % 2)
            return carry
        lax.fori_loop(0, 2 * (last - first), step, 0)


def attend_kernel(reach, start_ref, q_ref, k_ref, v_ref, out_ref, acc_ref):
    whole = q_ref.shape[0]
    lane = lax.broadcasted_iota(jnp.int32, (BLOCK, LANES), 1) // HEAD_DIM

    def body(i, first, count, head):
        at = pl.ds(pl.multiple_of(i * BLOCK, BLOCK), BLOCK)
        keys = pl.ds(pl.multiple_of(first * BLOCK, BLOCK), count)
        query = q_ref[at, :] * (HEAD_DIM**-0.5)
        query = jnp.where(lane == head, query, jnp.zeros_like(query))
        scores = dot(query, k_ref[keys, :], NT)
        key_at = first * BLOCK + lax.broadcasted_iota(jnp.int32, scores.shape, 1)
        query_at = i * BLOCK + lax.broadcasted_iota(jnp.int32, scores.shape, 0)
        allowed = (key_at >= start_ref[at, :1]) & (key_at <= query_at)
        scores = jnp.where(allowed, scores, NEG_FILL)
        exponent = jnp.exp(scores - jnp.max(scores, axis=1, keepdims=True))
        row_sum = jnp.sum(exponent, axis=1, keepdims=True)
        probs = (exponent * (1.0 / row_sum)).astype(jnp.bfloat16)
        mixed = dot(probs, v_ref[keys, :])

        @pl.when(head == 0)
        def _():
            acc_ref[...] = mixed

        @pl.when(head == 1)
        def _():
            out_ref[at, :] = jnp.where(lane == 0, acc_ref[...], mixed).astype(out_ref.dtype)

    each_block(whole, reach, body)


def attend(start_column, queries, keys, values, reach):
    whole, width = queries.shape
    block = pl.BlockSpec((whole, LANES), lambda p: (0, p))
    return pl.pallas_call(
        functools.partial(attend_kernel, reach),
        grid=(width // LANES,),
        in_specs=[pl.BlockSpec((whole, LANES), lambda p: (0, 0)), block, block, block],
        out_specs=block,
        out_shape=jax.ShapeDtypeStruct((whole, width), jnp.bfloat16),
        scratch_shapes=[pltpu.VMEM((BLOCK, LANES), jnp.float32)],
        compiler_params=pltpu.CompilerParams(vmem_limit_bytes=40 << 20),
        cost_estimate=pl.CostEstimate(
            flops=4 * whole * width * 640, transcendentals=whole * 640 * 6, bytes_accessed=8 * whole * width
        ),
    )(start_column, queries, keys, values)


def turn_back(field, cos, sin):
    half = HEAD_DIM // 2
    lane = lax.broadcasted_iota(jnp.int32, field.shape, 1) % HEAD_DIM
    crossed = jnp.where(lane < half, pltpu.roll(field, LANES - half, 1), pltpu.roll(field, half, 1))
    return field * cos - crossed * sin


def attend_back_kernel(
    reach, start_ref, cos_ref, sin_ref, q_ref, k_ref, v_ref, g_ref, dq_ref, dk_ref, dv_ref,
    key_acc, value_acc, query_acc,
):
    whole = q_ref.shape[0]
    lane = lax.broadcasted_iota(jnp.int32, (BLOCK, LANES), 1) // HEAD_DIM
    key_acc[...] = jnp.zeros_like(key_acc)
    value_acc[...] = jnp.zeros_like(value_acc)

    def body(i, first, count, head):
        at = pl.ds(pl.multiple_of(i * BLOCK, BLOCK), BLOCK)
        span = pl.ds(pl.multiple_of(first * BLOCK, BLOCK), count)
        query = q_ref[at, :] * (HEAD_DIM**-0.5)
        query = jnp.where(lane == head, query, jnp.zeros_like(query))
        grad = g_ref[at, :]
        grad = jnp.where(lane == head, grad, jnp.zeros_like(grad))
        keys = k_ref[span, :]
        scores = dot(keys, query, NT)
        key_at = first * BLOCK + lax.broadcasted_iota(jnp.int32, scores.shape, 0)
        query_at = i * BLOCK + lax.broadcasted_iota(jnp.int32, scores.shape, 1)
        allowed = (key_at >= start_ref[:1, at]) & (key_at <= query_at)
        scores = jnp.where(allowed, scores, NEG_FILL)
        exponent = jnp.exp(scores - jnp.max(scores, axis=0, keepdims=True))
        probs = exponent * (1.0 / jnp.sum(exponent, axis=0, keepdims=True))
        value_acc[span, :] += dot(probs.astype(jnp.bfloat16), grad)
        grad_probs = dot(v_ref[span, :], grad, NT)
        weighted = probs * grad_probs
        grad_scores = (weighted - probs * jnp.sum(weighted, axis=0, keepdims=True)).astype(jnp.bfloat16)
        key_acc[span, :] += dot(grad_scores, query)
        here = dot(grad_scores, keys, (((0,), (0,)), ((), ())))

        @pl.when(head == 0)
        def _():
            query_acc[...] = here

        @pl.when(head == 1)
        def _():
            both = jnp.where(lane == 0, query_acc[...], here) * (HEAD_DIM**-0.5)
            dq_ref[at, :] = turn_back(both, cos_ref[at, :], sin_ref[at, :]).astype(dq_ref.dtype)

    each_block(whole, reach, body)

    def finish(i, carry):
        at = pl.ds(pl.multiple_of(i * BLOCK, BLOCK), BLOCK)
        dk_ref[at, :] = turn_back(key_acc[at, :], cos_ref[at, :], sin_ref[at, :]).astype(dk_ref.dtype)
        dv_ref[at, :] = value_acc[at, :].astype(dv_ref.dtype)
        return carry

    lax.fori_loop(0, whole // BLOCK, finish, 0)


def attend_back(start_row, cos, sin, queries, keys, values, grad_mixed, reach):
    whole, width = queries.shape
    block = pl.BlockSpec((whole, LANES), lambda p: (0, p))
    table = pl.BlockSpec((whole, LANES), lambda p: (0, 0))
    return pl.pallas_call(
        functools.partial(attend_back_kernel, reach),
        grid=(width // LANES,),
        in_specs=[pl.BlockSpec((8, whole), lambda p: (0, 0)), table, table, block, block, block, block],
        out_specs=[block] * 3,
        out_shape=[jax.ShapeDtypeStruct((whole, width), jnp.bfloat16)] * 3,
        scratch_shapes=[
            pltpu.VMEM((whole, LANES), jnp.float32),
            pltpu.VMEM((whole, LANES), jnp.float32),
            pltpu.VMEM((BLOCK, LANES), jnp.float32),
        ],
        compiler_params=pltpu.CompilerParams(vmem_limit_bytes=40 << 20),
        cost_estimate=pl.CostEstimate(
            flops=10 * whole * width * 640, transcendentals=whole * 640 * 6, bytes_accessed=14 * whole * width
        ),
    )(start_row, cos, sin, queries, keys, values, grad_mixed)


ROWS = 256


def norm_parts(field):
    centered = field - jnp.mean(field, axis=-1, keepdims=True)
    scale = lax.rsqrt(jnp.mean(centered * centered, axis=-1, keepdims=True) + NORM_EPS)
    return centered * scale, scale


def wide(ref, at):
    return ref[at, :].astype(jnp.float32)


def row_blocks(count, body):
    def step(i, carry):
        body(i, pl.ds(pl.multiple_of(i * ROWS, ROWS), ROWS))
        return carry

    lax.fori_loop(0, count // ROWS, step, 0)


def whole_spec(shape):
    return pl.BlockSpec(shape, lambda *at: (0,) * len(shape))


def turn(field, cos, sin):
    half = HEAD_DIM // 2
    lane = lax.broadcasted_iota(jnp.int32, field.shape, 1) % HEAD_DIM
    crossed = jnp.where(lane < half, pltpu.roll(field, LANES - half, 1), pltpu.roll(field, half, 1))
    return field * cos + crossed * sin


def project_kernel(
    flags, rows_ref, gain_ref, shift_ref, cos_ref, sin_ref, w_own, w_got, out_ref, turned_ref, norm_ref
):
    whole = rows_ref.shape[0]
    step = pl.program_id(0)

    @pl.when(step == 0)
    def _():
        def body(i, at):
            unit, unused = norm_parts(wide(rows_ref, at))
            norm = unit * gain_ref[...] + shift_ref[...]
            norm_ref[at, :] = norm.astype(jnp.bfloat16)
            turned_ref[:, at] = norm.T.astype(jnp.bfloat16)

        row_blocks(whole, body)

    weight = jnp.where(flags[0] == 1, w_own[0], w_got[0])

    def body(i, at):
        field = dot(norm_ref[at, :], weight)

        @pl.when(step < 2)
        def _():
            for p in range(field.shape[1] // LANES):
                lanes = slice(p * LANES, (p + 1) * LANES)
                out_ref[0, at, lanes] = turn(field[:, lanes], cos_ref[at, :], sin_ref[at, :]).astype(
                    jnp.bfloat16
                )

        @pl.when(step == 2)
        def _():
            out_ref[0, at, :] = field.astype(jnp.bfloat16)

    row_blocks(whole, body)


def project(flags, rows, gain, shift, cos, sin, w_own, w_got):
    whole, width = rows.shape
    count, unused, columns = w_own.shape
    weight = pl.BlockSpec((1, width, columns), lambda c, flags: (c, 0, 0))
    return pl.pallas_call(
        project_kernel,
        grid_spec=pltpu.PrefetchScalarGridSpec(
            num_scalar_prefetch=1,
            grid=(count,),
            in_specs=[
                whole_spec((whole, width)),
                whole_spec((1, width)),
                whole_spec((1, width)),
                whole_spec((whole, LANES)),
                whole_spec((whole, LANES)),
                weight,
                weight,
            ],
            out_specs=[
                pl.BlockSpec((1, whole, columns), lambda c, flags: (c, 0, 0)),
                whole_spec((width, whole)),
            ],
            scratch_shapes=[pltpu.VMEM((whole, width), jnp.bfloat16)],
        ),
        out_shape=[
            jax.ShapeDtypeStruct((count, whole, columns), jnp.bfloat16),
            jax.ShapeDtypeStruct((width, whole), jnp.bfloat16),
        ],
        compiler_params=pltpu.CompilerParams(vmem_limit_bytes=40 << 20),
        cost_estimate=pl.CostEstimate(
            flops=2 * whole * width * columns * count,
            transcendentals=0,
            bytes_accessed=12 * whole * width,
        ),
    )(flags, rows, gain, shift, cos, sin, w_own, w_got)


HIDDEN = 256


def gelu_both(up):
    root = math.sqrt(2.0 / math.pi)
    square = up * up
    bent = jnp.tanh(root * up * (1.0 + 0.044715 * square))
    half = 0.5 * (1.0 + bent)
    slope = half + 0.5 * up * (1.0 - bent * bent) * (root * (1.0 + 3.0 * 0.044715 * square))
    return up * half, slope


def feed_kernel(
    flags, weight_ref, rows_ref, own_ref, got_ref, cot_ref, gain_ref, shift_ref, up_own, up_got,
    down_own, down_got, down_ref, back_ref, gup_ref, gdown_ref,
    norm, norm_t, grad, grad_t, act, slope, up_w, down_w,
):
    whole, width = rows_ref.shape
    step = pl.program_id(0)
    last = pl.num_programs(0) - 1

    @pl.when(step == 0)
    def _():
        def body(i, at):
            unit, unused = norm_parts(wide(rows_ref, at) + wide(own_ref, at) + wide(got_ref, at))
            field = unit * gain_ref[...] + shift_ref[...]
            norm[at, :] = field.astype(jnp.bfloat16)
            norm_t[:, at] = field.T.astype(jnp.bfloat16)
            field = wide(cot_ref, at) * weight_ref[0]
            grad[at, :] = field.astype(jnp.bfloat16)
            grad_t[:, at] = field.T.astype(jnp.bfloat16)

        row_blocks(whole, body)

    same = flags[0] == 1
    hidden = pl.ds(pl.multiple_of(step * HIDDEN, HIDDEN), HIDDEN)
    up_block = jnp.where(same, up_own[...], up_got[...])
    down_block = jnp.where(same, down_own[...], down_got[...])
    up_w[:, hidden] = up_block
    down_w[hidden, :] = down_block

    def body(i, at):
        value, rise = gelu_both(dot(norm[at, :], up_block))
        act[at, hidden] = value.astype(jnp.bfloat16)
        slope[at, hidden] = (dot(grad[at, :], down_block, NT) * rise).astype(jnp.bfloat16)

    row_blocks(whole, body)

    def grads(i, at):
        gdown_ref[0, at, :] = dot(grad_t[at, :], act[:, hidden]).astype(jnp.bfloat16)
        gup_ref[0, at, :] = dot(norm_t[at, :], slope[:, hidden]).astype(jnp.bfloat16)

    row_blocks(width, grads)

    @pl.when(step == last)
    def _():
        def body(i, at):
            back_ref[at, :] = dot(slope[at, :], up_w[...], NT).astype(jnp.bfloat16)
            down_ref[at, :] = dot(act[at, :], down_w[...]).astype(jnp.bfloat16)

        row_blocks(whole, body)


def feed(flags, weight, rows, own, got, cot, gain, shift, up_own, up_got, down_own, down_got):
    whole, width = rows.shape
    hidden = up_own.shape[1]
    steps = hidden // HIDDEN
    half = steps // 2
    tokens = whole_spec((whole, width))
    vector = whole_spec((1, width))

    def at(j, flags):
        return lax.rem(flags[2] * half + j, steps)

    up_spec = pl.BlockSpec((width, HIDDEN), lambda j, flags: (0, at(j, flags)))
    down_spec = pl.BlockSpec((HIDDEN, width), lambda j, flags: (at(j, flags), 0))
    piece = pl.BlockSpec((1, width, HIDDEN), lambda j, flags: (j // half, 0, j % half))
    wide_bf16 = jax.ShapeDtypeStruct((whole, width), jnp.bfloat16)
    pieces = jax.ShapeDtypeStruct((2, width, hidden // 2), jnp.bfloat16)
    return pl.pallas_call(
        feed_kernel,
        grid_spec=pltpu.PrefetchScalarGridSpec(
            num_scalar_prefetch=1,
            grid=(steps,),
            in_specs=[
                pl.BlockSpec(memory_space=pltpu.SMEM),
                tokens,
                tokens,
                tokens,
                tokens,
                vector,
                vector,
                up_spec,
                up_spec,
                down_spec,
                down_spec,
            ],
            out_specs=[tokens, tokens, piece, piece],
            scratch_shapes=[
                pltpu.VMEM((whole, width), jnp.bfloat16),
                pltpu.VMEM((width, whole), jnp.bfloat16),
                pltpu.VMEM((whole, width), jnp.bfloat16),
                pltpu.VMEM((width, whole), jnp.bfloat16),
                pltpu.VMEM((whole, hidden), jnp.bfloat16),
                pltpu.VMEM((whole, hidden), jnp.bfloat16),
                pltpu.VMEM((width, hidden), jnp.bfloat16),
                pltpu.VMEM((hidden, width), jnp.bfloat16),
            ],
        ),
        out_shape=[wide_bf16, wide_bf16, pieces, pieces],
        compiler_params=pltpu.CompilerParams(vmem_limit_bytes=56 << 20),
        cost_estimate=pl.CostEstimate(
            flops=12 * whole * width * hidden, transcendentals=whole * hidden, bytes_accessed=32 * whole * width
        ),
    )(flags, weight, rows, own, got, cot, gain, shift, up_own, up_got, down_own, down_got)


def middle_kernel(
    flags, weight_ref, rows_ref, own_ref, got_ref, cot_ref, back_own, back_got, gain_ref, mixed_ref,
    w_own, w_got, grad_ref, gmixed_ref, gout_ref, sums_ref, turned,
):
    whole, width = rows_ref.shape
    weight = jnp.where(flags[0] == 1, w_own[...], w_got[...])
    gain = gain_ref[...]
    sums_ref[...] = jnp.zeros_like(sums_ref)

    def body(i, at):
        unit, scale = norm_parts(wide(rows_ref, at) + wide(own_ref, at) + wide(got_ref, at))
        back = wide(back_own, at) + wide(back_got, at)
        inner = back * gain
        mean = jnp.mean(inner, axis=-1, keepdims=True)
        slant = jnp.mean(inner * unit, axis=-1, keepdims=True)
        grad = wide(cot_ref, at) * weight_ref[0] + scale * (inner - mean - unit * slant)
        low = grad.astype(jnp.bfloat16)
        grad_ref[at, :] = low
        turned[:, at] = grad.T.astype(jnp.bfloat16)
        gmixed_ref[at, :] = dot(low, weight, NT).astype(jnp.bfloat16)

        @pl.when((i * ROWS) // (whole // 2) == flags[1])
        def _():
            sums_ref[0:1, :] += jnp.sum(back * unit, axis=0, keepdims=True)
            sums_ref[1:2, :] += jnp.sum(back, axis=0, keepdims=True)

    row_blocks(whole, body)

    def grads(i, at):
        gout_ref[at, :] = dot(turned[at, :], mixed_ref[...]).astype(jnp.bfloat16)

    row_blocks(width, grads)


def middle(flags, weight, rows, own, got, cot, back_own, back_got, gain, mixed, w_own, w_got):
    whole, width = rows.shape
    columns = mixed.shape[1]
    tokens = whole_spec((whole, width))
    narrow = whole_spec((whole, columns))
    projection = whole_spec((columns, width))
    return pl.pallas_call(
        middle_kernel,
        grid_spec=pltpu.PrefetchScalarGridSpec(
            num_scalar_prefetch=1,
            grid=(1,),
            in_specs=[pl.BlockSpec(memory_space=pltpu.SMEM)]
            + [tokens] * 6
            + [whole_spec((1, width)), narrow, projection, projection],
            out_specs=[tokens, narrow, whole_spec((width, columns)), whole_spec((8, width))],
            scratch_shapes=[pltpu.VMEM((width, whole), jnp.bfloat16)],
        ),
        out_shape=[
            jax.ShapeDtypeStruct((whole, width), jnp.bfloat16),
            jax.ShapeDtypeStruct((whole, columns), jnp.bfloat16),
            jax.ShapeDtypeStruct((width, columns), jnp.bfloat16),
            jax.ShapeDtypeStruct((8, width), jnp.float32),
        ],
        compiler_params=pltpu.CompilerParams(vmem_limit_bytes=56 << 20),
        cost_estimate=pl.CostEstimate(
            flops=4 * whole * width * columns, transcendentals=0, bytes_accessed=18 * whole * width
        ),
    )(flags, weight, rows, own, got, cot, back_own, back_got, gain, mixed, w_own, w_got)


def unproject_kernel(flags, gq_ref, gk_ref, gv_ref, turned_ref, w_own, w_got, keep_ref, send_ref, gw_ref, weight):
    whole = gq_ref.shape[0]
    width = turned_ref.shape[0]
    weight[...] = jnp.where(flags[0] == 1, w_own[...], w_got[...])
    half = whole // 2

    def side(near, out_ref):
        def body(i, at):
            from_rows = pl.ds(pl.multiple_of(near * half + i * ROWS, ROWS), ROWS)
            total = dot(gq_ref[from_rows, :], weight[0], NT)
            total = total + dot(gk_ref[from_rows, :], weight[1], NT)
            total = total + dot(gv_ref[from_rows, :], weight[2], NT)
            out_ref[at, :] = total.astype(out_ref.dtype)

        row_blocks(half, body)

    side(1 - flags[1], send_ref)
    side(flags[1], keep_ref)

    def grads(i, at):
        for c, ref in enumerate((gq_ref, gk_ref, gv_ref)):
            gw_ref[c, at, :] = dot(turned_ref[at, :], ref[...]).astype(jnp.bfloat16)

    row_blocks(width, grads)


def unproject(flags, gq, gk, gv, turned, w_own, w_got):
    whole, columns = gq.shape
    width = turned.shape[0]
    narrow = whole_spec((whole, columns))
    weights = whole_spec((3, width, columns))
    half = whole_spec((whole // 2, width))
    return pl.pallas_call(
        unproject_kernel,
        grid_spec=pltpu.PrefetchScalarGridSpec(
            num_scalar_prefetch=1,
            grid=(1,),
            in_specs=[narrow, narrow, narrow, whole_spec((width, whole)), weights, weights],
            out_specs=[half, half, weights],
            scratch_shapes=[pltpu.VMEM((3, width, columns), jnp.bfloat16)],
        ),
        out_shape=[
            jax.ShapeDtypeStruct((whole // 2, width), jnp.float32),
            jax.ShapeDtypeStruct((whole // 2, width), jnp.bfloat16),
            jax.ShapeDtypeStruct((3, width, columns), jnp.bfloat16),
        ],
        compiler_params=pltpu.CompilerParams(vmem_limit_bytes=56 << 20),
        cost_estimate=pl.CostEstimate(
            flops=12 * whole * width * columns, transcendentals=0, bytes_accessed=12 * whole * width
        ),
    )(flags, gq, gk, gv, turned, w_own, w_got)


def first_norm_kernel(flags, rows_ref, keep_ref, got_ref, resid_ref, gain_ref, out_ref, sums_ref):
    sums_ref[...] = jnp.zeros_like(sums_ref)

    def body(i, at):
        unit, scale = norm_parts(wide(rows_ref, at))
        back = keep_ref[at, :] + wide(got_ref, at)
        inner = back * gain_ref[...]
        mean = jnp.mean(inner, axis=-1, keepdims=True)
        slant = jnp.mean(inner * unit, axis=-1, keepdims=True)
        grad = wide(resid_ref, at) + scale * (inner - mean - unit * slant)
        out_ref[at, :] = grad.astype(jnp.bfloat16)
        sums_ref[0:1, :] += jnp.sum(back * unit, axis=0, keepdims=True)
        sums_ref[1:2, :] += jnp.sum(back, axis=0, keepdims=True)

    row_blocks(rows_ref.shape[0], body)


def first_norm_back(flags, rows, keep, got, resid, gain):
    half, width = keep.shape
    mine = pl.BlockSpec((half, width), lambda i, flags: (flags[1], 0))
    tokens = whole_spec((half, width))
    return pl.pallas_call(
        first_norm_kernel,
        grid_spec=pltpu.PrefetchScalarGridSpec(
            num_scalar_prefetch=1,
            grid=(1,),
            in_specs=[mine, tokens, tokens, mine, whole_spec((1, width))],
            out_specs=[tokens, whole_spec((8, width))],
        ),
        out_shape=[
            jax.ShapeDtypeStruct((half, width), jnp.bfloat16),
            jax.ShapeDtypeStruct((8, width), jnp.float32),
        ],
        compiler_params=pltpu.CompilerParams(vmem_limit_bytes=40 << 20),
        cost_estimate=pl.CostEstimate(flops=20 * half * width, transcendentals=0, bytes_accessed=12 * half * width),
    )(flags, rows, keep, got, resid, gain)


AXES = ("tp", "dp", "rep")


def pairs_of(move):
    tps, dps, reps = (lax.axis_size(name) for name in AXES)
    index = lambda t, d, r: (t * dps + d) * reps + r
    every = [(t, d, r) for t in range(tps) for d in range(dps) for r in range(reps)]
    return [(index(*at), index(*move(*at))) for at in every if move(*at) != at]


def swap_diagonal(field):
    return lax.ppermute(field, AXES, pairs_of(lambda t, d, r: (r % 2, d, r - r % 2 + t)))


def swap_near(field):
    return lax.ppermute(field, "rep", [(r, r ^ 1) for r in range(lax.axis_size("rep"))])


def swap_far(field):
    return lax.ppermute(field, "rep", [(r, r ^ 2) for r in range(lax.axis_size("rep"))])


def ordered(own, other, first):
    return jnp.where(
        first, jnp.concatenate([own, other], axis=0), jnp.concatenate([other, own], axis=0)
    )


def take(field, index):
    return lax.dynamic_index_in_dim(field, index, 0, keepdims=False)


def half_columns(field, index):
    size = field.shape[-1] // 2
    return lax.dynamic_slice_in_dim(field, index * size, size, field.ndim - 1)


def sum_rows(block):
    dps = lax.axis_size("dp")
    rows = block.shape[0] // dps
    low = block.astype(jnp.bfloat16)
    if dps <= 8:
        place = lax.axis_index("dp")
        total = lax.dynamic_slice_in_dim(block, place * rows, rows, 0)
        for step in range(1, dps):
            sent = lax.dynamic_slice_in_dim(low, lax.rem(place + step, dps) * rows, rows, 0)
            total = total + lax.ppermute(
                sent, "dp", [(d, (d + step) % dps) for d in range(dps)]
            ).astype(jnp.float32)
    else:
        total = lax.psum_scatter(low, "dp", scatter_dimension=0, tiled=True)
    return lax.all_gather(total.astype(jnp.bfloat16), "rep", axis=0).astype(jnp.float32)


def sum_far_first(mine, theirs, same, near):
    pair = (mine.astype(jnp.float32) + swap_far(theirs).astype(jnp.float32)).astype(jnp.bfloat16)
    pair = jnp.where(same, pair, swap_diagonal(pair))
    keep, send = half_columns(pair, near), half_columns(pair, 1 - near)
    return sum_rows(keep.astype(jnp.float32) + swap_near(send).astype(jnp.float32))


def sum_diagonal_first(pieces, same, near):
    pieces = jnp.where(same, pieces, swap_diagonal(pieces))
    keep, send = half_columns(pieces, near), half_columns(pieces, 1 - near)
    pair = keep.astype(jnp.float32) + swap_near(send).astype(jnp.float32)
    return sum_rows(pair[0] + swap_far(pair[1].astype(jnp.bfloat16)).astype(jnp.float32))


def local(
    layer_input,
    history,
    cotangent,
    lengths,
    dwa_weights,
    gain_one,
    bias_one,
    w_qkv,
    w_out,
    gain_two,
    bias_two,
    w_up,
    w_down,
):
    rows = layer_input.shape[1]
    whole = rows * lax.axis_size("tp")
    hist_count = history.shape[0]
    part, slot = lax.axis_index("tp"), lax.axis_index("rep")
    near, far = slot % 2, slot // 2
    same = near == part
    flags = jnp.stack([same.astype(jnp.int32), near, far])
    own_weight = dwa_weights[hist_count:]

    input_half = jnp.where(same, layer_input[0], swap_diagonal(layer_input[0]))
    got_qkv = swap_diagonal(w_qkv)
    got_out = swap_diagonal(w_out)
    got_up = swap_diagonal(w_up)
    cot_half = jnp.where(same, cotangent[0], swap_diagonal(cotangent[0]))
    got_down = swap_diagonal(w_down)
    own_lengths = jnp.where(same, lengths, swap_near(lengths))[0]
    seq_owner, token_place = positions(own_lengths, whole)
    seq_begin = jnp.arange(whole, dtype=jnp.int32) - token_place
    start_column = jnp.broadcast_to(seq_begin[:, None], (whole, LANES))
    start_row = jnp.broadcast_to(seq_begin[None, :], (8, whole))
    half_dim = HEAD_DIM // 2
    lane = jnp.arange(LANES, dtype=jnp.int32)
    frequency = jnp.exp((lane % half_dim).astype(jnp.float32) * (-math.log(10000.0) / half_dim))
    angles = token_place.astype(jnp.float32)[:, None] * frequency[None, :]
    cos_table = jnp.cos(angles)
    sin_table = jnp.sin(angles) * jnp.where(lane % HEAD_DIM < half_dim, -1.0, 1.0)[None, :]
    layer_rows = ordered(input_half, swap_near(input_half), near == 0)
    cot_rows = ordered(cot_half, swap_near(cot_half), near == 0)
    gain_one, bias_one = gain_one[None], bias_one[None]
    gain_two, bias_two = gain_two[None], bias_two[None]

    projected, norm_one_t = project(
        flags, layer_rows, gain_one, bias_one, cos_table, sin_table, w_qkv, got_qkv
    )
    queries, keys, values = projected[0], projected[1], projected[2]
    mixed = attend(start_column, queries, keys, values, LONGEST)
    attn = jnp.dot(
        mixed, jnp.where(same, w_out, got_out), preferred_element_type=jnp.float32
    ).astype(jnp.bfloat16)
    attn_got = swap_near(attn)
    down, back, grad_up, grad_down = feed(
        flags,
        own_weight,
        layer_rows,
        attn,
        attn_got,
        cot_rows,
        gain_two,
        bias_two,
        w_up,
        got_up,
        w_down,
        got_down,
    )
    back_got = swap_near(back)
    grad_attn, grad_mixed, grad_out, sums_two = middle(
        flags,
        own_weight,
        layer_rows,
        attn,
        attn_got,
        cot_rows,
        back,
        back_got,
        gain_two,
        mixed,
        w_out,
        got_out,
    )
    grad_w_up = sum_far_first(grad_up[0], grad_up[1], same, near)
    grad_w_down = sum_diagonal_first(grad_down, same, near)

    def half_of(field, index):
        return lax.dynamic_slice_in_dim(field, index * rows, rows, 0)

    block_half = sum(
        half_of(field, near).astype(jnp.float32) for field in (layer_rows, attn, attn_got, down)
    ) + swap_near(half_of(down, 1 - near)).astype(jnp.float32)
    block_half = block_half.astype(jnp.bfloat16)
    block_out = jnp.where(same, block_half, swap_diagonal(block_half)).astype(jnp.float32)
    hist_rows = history[:, 0].astype(jnp.float32)
    output = (
        jnp.sum(dwa_weights[:hist_count, None, None] * hist_rows, axis=0)
        + dwa_weights[hist_count] * block_out
    )
    grad_block = cotangent[0].astype(jnp.float32)
    grad_history = (dwa_weights[:hist_count, None, None] * grad_block[None]).astype(jnp.bfloat16)[
        :, None
    ]
    dwa_terms = jnp.concatenate(
        [jnp.sum(hist_rows * grad_block[None], axis=(1, 2)), jnp.sum(block_out * grad_block)[None]]
    )

    grad_queries, grad_keys, grad_values = attend_back(
        start_row, cos_table, sin_table, queries, keys, values, grad_mixed, LONGEST
    )
    keep, send, grad_qkv = unproject(
        flags, grad_queries, grad_keys, grad_values, norm_one_t, w_qkv, got_qkv
    )
    input_grad, sums_one = first_norm_back(flags, layer_rows, keep, swap_near(send), grad_attn, gain_one)
    grad_input = jnp.where(same, input_grad, swap_diagonal(input_grad))
    attn_pieces = jnp.concatenate([grad_qkv, grad_out[None]], axis=0)
    mine = lax.dynamic_slice_in_dim(attn_pieces, 2 * far, 2, 0)
    theirs = lax.dynamic_slice_in_dim(attn_pieces, 2 - 2 * far, 2, 0)
    pair = (mine.astype(jnp.float32) + swap_far(theirs).astype(jnp.float32)).astype(jnp.bfloat16)
    pair = jnp.where(same, pair, swap_diagonal(pair))
    grad_w_attn = sum_rows(
        take(pair, near).astype(jnp.float32) + swap_near(take(pair, 1 - near)).astype(jnp.float32)
    )

    small = jnp.concatenate(
        [sums_one[:2], sums_two[:2], jnp.pad(dwa_terms, (0, gain_one.shape[1] - hist_count - 1))[None]]
    )
    small = jnp.sum(lax.all_gather(small, AXES, axis=0), axis=0)

    def columns_of(pieces):
        return pieces.transpose(1, 0, 2).reshape(pieces.shape[1], -1)

    return (
        output.astype(jnp.bfloat16)[None],
        grad_input[None],
        grad_history,
        small[4, : hist_count + 1],
        small[0],
        small[1],
        grad_w_attn[:3],
        grad_w_attn[3].T,
        small[2],
        small[3],
        columns_of(grad_w_up),
        columns_of(grad_w_down).T,
    )


def positions(seq_lengths, token_count):
    seq_ends = jnp.cumsum(seq_lengths)
    seq_starts = seq_ends - seq_lengths
    token_index = jnp.arange(token_count, dtype=jnp.int32)
    seq_owner = jnp.sum((token_index[:, None] >= seq_ends[None, :]).astype(jnp.int32), axis=1)
    picked = (
        seq_owner[:, None] == jnp.arange(seq_lengths.shape[0], dtype=jnp.int32)[None, :]
    ).astype(jnp.int32)
    seq_begin = jnp.sum(picked * seq_starts[None, :], axis=1)
    return (seq_owner, token_index - seq_begin)


def solution(mesh):
    in_specs = (
        P(("dp", "rep"), "tp", None),
        P(None, ("dp", "rep"), "tp", None),
        P(("dp", "rep"), "tp", None),
        P(("dp", "rep"), None),
        P(),
        P(),
        P(),
        P(None, None, "tp"),
        P("tp", None),
        P(),
        P(),
        P(None, "tp"),
        P("tp", None),
    )
    out_specs = (
        P(("dp", "rep"), "tp", None),
        P(("dp", "rep"), "tp", None),
        P(None, ("dp", "rep"), "tp", None),
        P(),
        P(),
        P(),
        P(None, "dp", "tp"),
        P("tp", "dp"),
        P(),
        P(),
        P("dp", "tp"),
        P("tp", "dp"),
    )
    return jax.shard_map(local, mesh=mesh, in_specs=in_specs, out_specs=out_specs, check_vma=False)
```

profile of v0, /device:TPU:9, one launch (start us, length us, event | category | flops | bytes accessed | tf_op | source)
XLA Modules:
  0.0 388.9 jit_solution(16132128492148356982)
XLA Ops:
  0.7 3.7 collective-permute-start
  4.5 1.9 collective-permute-start.3
  6.4 3.6 collective-permute-start.4
  10.0 1.9 collective-permute-start.6
  13.5 3.6 collective-permute-start.8
  17.4 1.2 broadcast_select_fusion.5
  18.8 1.9 fusion.13
  21.0 2.2 collective-permute-start.9
  23.9 9.4 %collective-permute-done.3.w_got = bf16[3,768,384]{2,1,0:T(8,128)(2,1)} collective-permute-done((bf16[3,768,384]{2,1,0:T(8,128)(2,1)}, bf16[3,768,384]{2,1,0:T(8,128)(2,1)}, u32[]{:S(2)}, u32[]{:S(2)}) %collective-permute-start.3) | collective-permute-done | bytes 1769504 | tf_op jit(solution)/shard_map/ppermute | solution.py:560
  33.3 10.4 %shard_map.220 = (bf16[3,1024,384]{2,1,0:T(8,128)(2,1)S(1)}, bf16[768,1024]{1,0:T(8,128)(2,1)S(1)}) custom-call(s32[3]{0:T(128)S(1)} %pad_add_fusion.flags, bf16[1024,768]{1,0:T(8,128)(2,1)S(1)} %maximum_select_fusion.rows_ref, f32[1,768]{1,0:T(1,128)S(1)} %broadcast_in_dim.31.gain_ref, f32[1,768]{1,0:T(1,128)S(1)} %broadcast_in_dim.32.shift_ref, ...), custom_call_target="tpu_custom_call" | custom-call | flops 1811939328 | bytes 9437184 | tf_op jit(solution)/shard_map/pallas_call | solution.py:244
  43.7 1.1 copy-done.18
  45.3 17.2 %shard_map.221.mixed_ref = bf16[1024,384]{1,0:T(8,128)(2,1)S(1)} custom-call(s32[1024,128]{1,0:T(8,128)S(1)} %broadcast_in_dim.30.start_ref, bf16[1024,384]{1,0:T(8,128)(2,1)S(1)} %get-tuple-element.62.q_ref, bf16[1024,384]{1,0:T(8,128)(2,1)S(1)} %get-tuple-element.61.k_ref, bf16[1024,384]{1,0:T(8,128)(2,1)S(1)} %get-tuple-element.60.v_ref), custom_call_target="tpu_custom_call" | custom-call | flops 1006632960 | bytes 3145728 | tf_op jit(solution)/shard_map/pallas_call | solution.py:78
  62.6 2.4 convolution_convert_fusion.own_ref
  65.1 2.6 broadcast_select_fusion.4
  70.3 3.4 maximum_select_fusion.1.cot_ref
  73.8 24.8 %collective-permute-done.9.down_got = bf16[1536,768]{1,0:T(8,128)(2,1)} collective-permute-done((bf16[1536,768]{1,0:T(8,128)(2,1)}, bf16[1536,768]{1,0:T(8,128)(2,1)}, u32[]{:S(2)}, u32[]{:S(2)}) %collective-permute-start.9) | collective-permute-done | bytes 2359328 | tf_op jit(solution)/shard_map/ppermute | solution.py:560
  98.6 35.5 %shard_map.222 = (bf16[1024,768]{1,0:T(8,128)(2,1)}, bf16[1024,768]{1,0:T(8,128)(2,1)}, bf16[2,768,768]{2,1,0:T(8,128)(2,1)}, bf16[2,768,768]{2,1,0:T(8,128)(2,1)}) custom-call(s32[3]{0:T(128)} %copy-done.14, f32[1]{0:T(128)} %slice.58.weight_ref, bf16[1024,768]{1,0:T(8,128)(2,1)} %copy-done, bf16[1024,768]{1,0:T(8,128)(2,1)} %copy-done.22, ...), custom_call_target="tpu_custom_call" | custom-call | flops 14495514624 | bytes 25165824 | tf_op jit(solution)/shard_map/pallas_call | solution.py:356
  134.2 2.5 slice_bitcast_fusion.1
  136.7 1.2 collective-permute-start.21
  137.9 0.9 constant_dynamic-slice_fusion.10
  139.7 5.4 %fusion.1 = (f32[4]{0:T(128)S(1)}, f32[512,768]{1,0:T(8,128)}) fusion(bf16[4,1,512,768]{3,2,1,0:T(8,128)(2,1)} %param.14, f32[512,768]{1,0:T(8,128)S(1)} %bitcast_convert_fusion, f32[4]{0:T(128)S(1)} %bitcast.86), kind=kLoop, calls=%fused_computation.3 | loop fusion | flops 7471100 | bytes 6291488 | tf_op jit(solution)/shard_map/reduce_sum | solution.py:722
  145.1 3.5 collective-permute-start.27
  148.6 2.8 add_convert_fusion.1
  151.4 2.2 collective-permute-start.11
  153.6 10.6 %collective-permute-done.21 = bf16[768,768]{1,0:T(8,128)(2,1)} collective-permute-done((bf16[768,768]{1,0:T(8,128)(2,1)}, bf16[768,768]{1,0:T(8,128)(2,1)}, u32[]{:S(2)}, u32[]{:S(2)}) %collective-permute-start.21) | collective-permute-done | bytes 1179680 | tf_op jit(solution)/shard_map/ppermute | solution.py:568
  164.2 2.6 fusion.2
  166.8 5.1 %collective-permute-start.22 = (bf16[768,768]{1,0:T(8,128)(2,1)}, bf16[768,768]{1,0:T(8,128)(2,1)}, u32[]{:S(2)}, u32[]{:S(2)}) collective-permute-start(bf16[768,768]{1,0:T(8,128)(2,1)} %fusion.2), channel_id=1, source_target_pairs={{1,16},{3,18},{5,20},{7,22},{9,24},{11,26},{13,28},{15,30},{16,1},... | collective-permute-start | bytes 3538952 | tf_op jit(solution)/shard_map/ppermute | solution.py:560
  171.9 12.5 %shard_map.223 = (bf16[1024,768]{1,0:T(8,128)(2,1)}, bf16[1024,384]{1,0:T(8,128)(2,1)}, bf16[768,384]{1,0:T(8,128)(2,1)}, f32[8,768]{1,0:T(8,128)}) custom-call(s32[3]{0:T(128)} %copy-done.14, f32[1]{0:T(128)} %slice.58.weight_ref, bf16[1024,768]{1,0:T(8,128)(2,1)} %copy-done, bf16[1024,768]{1,0:T(8,128)(2,1)} %copy-done.22, ...), custom_call_target="tpu_custom_call" | custom-call | flops 1207959552 | bytes 14155776 | tf_op jit(solution)/shard_map/pallas_call | solution.py:434
  184.5 1.1 copy-done.17
  185.6 28.6 %shard_map.224 = (bf16[1024,384]{1,0:T(8,128)(2,1)S(1)}, bf16[1024,384]{1,0:T(8,128)(2,1)S(1)}, bf16[1024,384]{1,0:T(8,128)(2,1)S(1)}) custom-call(s32[8,1024]{1,0:T(8,128)S(1)} %broadcast_in_dim.68.start_ref, f32[1024,128]{1,0:T(8,128)S(1)} %copy-done.13, f32[1024,128]{1,0:T(8,128)S(1)} %copy-done.11, bf16[1024,384]{1,0:T(8,128)(2,1)S(1)} %copy-done.9, ...), custom_call_target="tpu_custom_call" | custom-call | flops 2516582400 | bytes 5505024 | tf_op jit(solution)/shard_map/pallas_call | solution.py:154
  215.1 0.9 copy-done.20
  216.0 0.9 copy-done.21
  216.9 11.5 %shard_map.225 = (f32[512,768]{1,0:T(8,128)}, bf16[512,768]{1,0:T(8,128)(2,1)}, bf16[3,768,384]{2,1,0:T(8,128)(2,1)}) custom-call(s32[3]{0:T(128)} %copy-done.14, bf16[1024,384]{1,0:T(8,128)(2,1)} %copy-done.19, bf16[1024,384]{1,0:T(8,128)(2,1)} %copy-done.20, bf16[1024,384]{1,0:T(8,128)(2,1)} %copy-done.21, bf16[768,1024]{1,0:T(8,128)(2,1)} %copy-done.18, ...), custom_call_target="tpu_custom_call" | custom-call | flops 3623878656 | bytes 9437184 | tf_op jit(solution)/shard_map/pallas_call | solution.py:490
  228.3 2.5 multiply_convert_fusion
  230.9 1.4 fusion.6
  232.3 1.2 collective-permute-start.15
  234.3 4.3 %fusion.5 = (f32[]{:T(128)}, bf16[1,512,768]{2,1,0:T(8,128)(2,1)}) fusion(bf16[512,768]{1,0:T(8,128)(2,1)} %add_convert_fusion.1, bf16[512,768]{1,0:T(8,128)(2,1)} %collective-permute-done.11, pred[]{:T(512)S(6)} %eq.25, bf16[1,512,768]{2,1,0:T(8,128)(2,1)S(1)} %copy-done.26, f32[512,768]{1,0:T(8,128)S(1)} %copy-done.27, f32[]{:T(128)} %bitcast.1), kind=kLoop, calls=%fused_computation.19 | loop fusion | flops 3145727 | bytes 4718601 | tf_op jit(solution)/shard_map/reduce_sum | solution.py:722
  239.4 1.9 shard_map.226
  241.3 51.6 %all-gather.4 = f32[32,5,768]{2,1,0:T(8,128)S(1)} all-gather(f32[1,5,768]{2,1,0:T(8,128)S(1)} %maximum_bitcast_fusion), channel_id=2, replica_groups=mesh['tp'=2,'dp'=4,'rep'=4] {'tp','dp','rep'}, dimensions={0}, use_global_device_ids=true | all-gather | bytes 506880 | tf_op jit(solution)/shard_map/all_gather | solution.py:745
  293.5 1.4 broadcast_select_fusion.1
  295.2 1.9 broadcast_select_fusion
  298.3 3.3 collective-permute-start.14
  301.9 5.9 %collective-permute-start.25 = (bf16[192,384]{1,0:T(8,128)(2,1)S(1)}, bf16[192,384]{1,0:T(8,128)(2,1)S(1)}, u32[]{:S(2)}, u32[]{:S(2)}) collective-permute-start(bf16[192,384]{1,0:T(8,128)(2,1)S(1)} %get-tuple-element.70), channel_id=1, source_target_pairs={{0,8},{4,12},{8,0},{12,4},{1,9},{5,13},{9,1},{13,5},{2,10},{6,14},... | collective-permute-start | bytes 442376 | tf_op jit(solution)/shard_map/ppermute | solution.py:595
  307.9 1.9 add_convert_fusion
  310.3 2.9 collective-permute-start.16
  313.2 2.1 collective-permute-done.25
  315.3 3.5 collective-permute-done.26
  318.8 7.6 %all-gather.2 = bf16[768,384]{1,0:T(8,128)(2,1)S(1)} all-gather(bf16[192,384]{1,0:T(8,128)(2,1)S(1)} %add_convert_fusion.3), channel_id=4, replica_groups=mesh['tp'=2,'dp'=4,'rep'=4] {'rep'}, dimensions={0}, use_global_device_ids=true | all-gather | bytes 737280 | tf_op jit(solution)/shard_map/all_gather | solution.py:600
  327.0 1.2 copy.31
  328.9 12.8 %collective-permute-done.29 = bf16[768,384]{1,0:T(8,128)(2,1)S(1)} collective-permute-done((bf16[768,384]{1,0:T(8,128)(2,1)S(1)}, bf16[768,384]{1,0:T(8,128)(2,1)S(1)}, u32[]{:S(2)}, u32[]{:S(2)}) %collective-permute-start.29) | collective-permute-done | bytes 589856 | tf_op jit(solution)/shard_map/ppermute | solution.py:568
  342.1 1.4 collective-permute-start.32
  343.4 1.0 select_bitcast_fusion
  344.4 1.9 collective-permute-done.30
  346.4 7.5 %collective-permute-done.31 = bf16[192,384]{1,0:T(8,128)(2,1)S(1)} collective-permute-done((bf16[192,384]{1,0:T(8,128)(2,1)S(1)}, bf16[192,384]{1,0:T(8,128)(2,1)S(1)}, u32[]{:S(2)}, u32[]{:S(2)}) %collective-permute-start.31) | collective-permute-done | bytes 147488 | tf_op jit(solution)/shard_map/ppermute | solution.py:595
  353.8 1.7 collective-permute-done.32
  355.6 7.9 %all-gather.3 = bf16[768,384]{1,0:T(8,128)(2,1)S(1)} all-gather(bf16[192,384]{1,0:T(8,128)(2,1)S(1)} %add_convert_fusion.2), channel_id=5, replica_groups=mesh['tp'=2,'dp'=4,'rep'=4] {'rep'}, dimensions={0}, use_global_device_ids=true | all-gather | bytes 737280 | tf_op jit(solution)/shard_map/all_gather | solution.py:600
  363.9 1.7 collective-permute-start.19
  365.6 1.4 collective-permute-start.20
  367.1 1.2 copy.32
  368.2 0.9 collective-permute-done.18
  369.2 7.5 %collective-permute-done.19 = bf16[192,384]{1,0:T(8,128)(2,1)S(1)} collective-permute-done((bf16[192,384]{1,0:T(8,128)(2,1)S(1)}, bf16[192,384]{1,0:T(8,128)(2,1)S(1)}, u32[]{:S(2)}, u32[]{:S(2)}) %collective-permute-start.19) | collective-permute-done | bytes 147488 | tf_op jit(solution)/shard_map/ppermute | solution.py:595
  376.7 2.6 collective-permute-done.20
  379.4 7.7 %all-gather.1 = bf16[768,384]{1,0:T(8,128)(2,1)S(1)} all-gather(bf16[192,384]{1,0:T(8,128)(2,1)S(1)} %add_convert_fusion.4), channel_id=3, replica_groups=mesh['tp'=2,'dp'=4,'rep'=4] {'rep'}, dimensions={0}, use_global_device_ids=true | all-gather | bytes 737280 | tf_op jit(solution)/shard_map/all_gather | solution.py:600
  387.2 1.0 slice.80
  (152 shorter events, 15.2 us)
Async XLA Ops:
  0.6 18.1 %copy-start.35 = (s32[1,3]{1,0:T(1,128)S(1)}, s32[1,3]{1,0:T(1,128)}, u32[]{:S(2)}) copy-start(s32[1,3]{1,0:T(1,128)} %param.16) | copy-start | bytes 40
  0.7 16.8 %collective-permute-start = (bf16[512,768]{1,0:T(8,128)(2,1)}, bf16[512,768]{1,0:T(8,128)(2,1)S(1)}, u32[]{:S(2)}, u32[]{:S(2)}) collective-permute-start(bf16[512,768]{1,0:T(8,128)(2,1)} %bitcast.84), channel_id=1, source_target_pairs={{1,16},{3,18},{5,20},{7,22},{9,24},{11,26},{13,28},{15,30},{16,1},... | collective-permute-start | bytes 2359304 | tf_op jit(solution)/shard_map/ppermute | solution.py:560
  4.4 9.1 %collective-permute-start.2 = (s32[1,3]{1,0:T(1,128)}, s32[1,3]{1,0:T(1,128)S(1)}, u32[]{:S(2)}, u32[]{:S(2)}) collective-permute-start(s32[1,3]{1,0:T(1,128)} %param.16), channel_id=1, source_target_pairs={{0,1},{1,0},{2,3},{3,2},{4,5},{5,4},{6,7},{7,6},{8,9},{9,8},{10,11... | collective-permute-start | bytes 44 | tf_op jit(solution)/shard_map/ppermute | solution.py:564
  4.5 28.9 %collective-permute-start.3 = (bf16[3,768,384]{2,1,0:T(8,128)(2,1)}, bf16[3,768,384]{2,1,0:T(8,128)(2,1)}, u32[]{:S(2)}, u32[]{:S(2)}) collective-permute-start(bf16[3,768,384]{2,1,0:T(8,128)(2,1)} %w_own.5), channel_id=1, source_target_pairs={{1,16},{3,18},{5,20},{7,22},{9,24},{11,26},{13,28},{15,30},{16,1},... | collective-permute-start | bytes 5308424 | tf_op jit(solution)/shard_map/ppermute | solution.py:560
  6.4 56.2 %collective-permute-start.4 = (bf16[384,768]{1,0:T(8,128)(2,1)}, bf16[384,768]{1,0:T(8,128)(2,1)}, u32[]{:S(2)}, u32[]{:S(2)}) collective-permute-start(bf16[384,768]{1,0:T(8,128)(2,1)} %w_own.4), channel_id=1, source_target_pairs={{1,16},{3,18},{5,20},{7,22},{9,24},{11,26},{13,28},{15,30},{16,1},... | collective-permute-start | bytes 1769480 | tf_op jit(solution)/shard_map/ppermute | solution.py:560
  10.0 55.1 %collective-permute-start.6 = (bf16[512,768]{1,0:T(8,128)(2,1)}, bf16[512,768]{1,0:T(8,128)(2,1)}, u32[]{:S(2)}, u32[]{:S(2)}) collective-permute-start(bf16[512,768]{1,0:T(8,128)(2,1)} %bitcast.76), channel_id=1, source_target_pairs={{1,16},{3,18},{5,20},{7,22},{9,24},{11,26},{13,28},{15,30},{16,1},... | collective-permute-start | bytes 2359304 | tf_op jit(solution)/shard_map/ppermute | solution.py:560
  13.5 19.9 %copy-start.14 = (s32[3]{0:T(128)}, s32[3]{0:T(128)S(1)}, u32[]{:S(2)}) copy-start(s32[3]{0:T(128)S(1)} %pad_add_fusion.flags) | copy-start | bytes 40
  13.5 60.3 %collective-permute-start.8 = (bf16[768,1536]{1,0:T(8,128)(2,1)}, bf16[768,1536]{1,0:T(8,128)(2,1)}, u32[]{:S(2)}, u32[]{:S(2)}) collective-permute-start(bf16[768,1536]{1,0:T(8,128)(2,1)} %up_own.1), channel_id=1, source_target_pairs={{1,16},{3,18},{5,20},{7,22},{9,24},{11,26},{13,28},{15,30},{16,1},... | collective-permute-start | bytes 7077896 | tf_op jit(solution)/shard_map/ppermute | solution.py:560
  18.6 2.4 collective-permute-start.1
  20.7 12.6 %copy-start.10 = (f32[1024,128]{1,0:T(8,128)}, f32[1024,128]{1,0:T(8,128)S(1)}, u32[]{:S(2)}) copy-start(f32[1024,128]{1,0:T(8,128)S(1)} %get-tuple-element.74.sin_ref) | copy-start | bytes 1572868
  20.8 12.6 %copy-start.12 = (f32[1024,128]{1,0:T(8,128)}, f32[1024,128]{1,0:T(8,128)S(1)}, u32[]{:S(2)}) copy-start(f32[1024,128]{1,0:T(8,128)S(1)} %get-tuple-element.75.cos_ref) | copy-start | bytes 1572868
  20.8 12.6 %copy-start.16 = (bf16[3,768,384]{2,1,0:T(8,128)(2,1)S(1)}, bf16[3,768,384]{2,1,0:T(8,128)(2,1)}, u32[]{:S(2)}) copy-start(bf16[3,768,384]{2,1,0:T(8,128)(2,1)} %w_own.5) | copy-start | bytes 5308420
  21.0 77.6 %collective-permute-start.9 = (bf16[1536,768]{1,0:T(8,128)(2,1)}, bf16[1536,768]{1,0:T(8,128)(2,1)}, u32[]{:S(2)}, u32[]{:S(2)}) collective-permute-start(bf16[1536,768]{1,0:T(8,128)(2,1)} %down_own.1), channel_id=1, source_target_pairs={{1,16},{3,18},{5,20},{7,22},{9,24},{11,26},{13,28},{15,30},{16,1},... | collective-permute-start | bytes 7077896 | tf_op jit(solution)/shard_map/ppermute | solution.py:560
  23.9 19.8 %copy-start = (bf16[1024,768]{1,0:T(8,128)(2,1)}, bf16[1024,768]{1,0:T(8,128)(2,1)S(1)}, u32[]{:S(2)}) copy-start(bf16[1024,768]{1,0:T(8,128)(2,1)S(1)} %maximum_select_fusion.rows_ref) | copy-start | bytes 4718596
  45.1 17.4 %copy-start.6 = (bf16[1024,384]{1,0:T(8,128)(2,1)}, bf16[1024,384]{1,0:T(8,128)(2,1)S(1)}, u32[]{:S(2)}) copy-start(bf16[1024,384]{1,0:T(8,128)(2,1)S(1)} %get-tuple-element.61.k_ref) | copy-start | bytes 2359300
  45.1 17.4 %copy-start.8 = (bf16[1024,384]{1,0:T(8,128)(2,1)}, bf16[1024,384]{1,0:T(8,128)(2,1)S(1)}, u32[]{:S(2)}) copy-start(bf16[1024,384]{1,0:T(8,128)(2,1)S(1)} %get-tuple-element.62.q_ref) | copy-start | bytes 2359300
  45.3 17.3 %copy-start.31 = (bf16[384,768]{1,0:T(8,128)(2,1)S(1)}, bf16[384,768]{1,0:T(8,128)(2,1)}, u32[]{:S(2)}) copy-start(bf16[384,768]{1,0:T(8,128)(2,1)} %w_own.4) | copy-start | bytes 1769476
  62.6 2.6 copy-start.25
  65.0 8.8 %copy-start.22 = (bf16[1024,768]{1,0:T(8,128)(2,1)}, bf16[1024,768]{1,0:T(8,128)(2,1)S(1)}, u32[]{:S(2)}) copy-start(bf16[1024,768]{1,0:T(8,128)(2,1)S(1)} %convolution_convert_fusion.own_ref) | copy-start | bytes 4718596
  65.0 2.7 copy-start.36
  65.0 3.3 copy-start.33
  65.0 3.9 copy-start.34
  65.0 33.6 %collective-permute-start.5 = (bf16[1024,768]{1,0:T(8,128)(2,1)S(1)}, bf16[1024,768]{1,0:T(8,128)(2,1)}, u32[]{:S(2)}, u32[]{:S(2)}) collective-permute-start(bf16[1024,768]{1,0:T(8,128)(2,1)S(1)} %convolution_convert_fusion.own_ref), channel_id=1, source_target_pairs={{0,1},{1,0},{2,3},{3,2},{4,5},{5,4},{6,7},{7,6},{8,9},{9,8},{10,11... | collective-permute-start | bytes 4718600 | tf_op jit(solution)/shard_map/ppermute | solution.py:564
  67.7 2.6 collective-permute-start.7
  134.2 3.8 copy-start.32
  134.2 37.7 %collective-permute-start.12 = (bf16[1024,768]{1,0:T(8,128)(2,1)}, bf16[1024,768]{1,0:T(8,128)(2,1)}, u32[]{:S(2)}, u32[]{:S(2)}) collective-permute-start(bf16[1024,768]{1,0:T(8,128)(2,1)} %get-tuple-element.32.back_own), channel_id=1, source_target_pairs={{0,1},{1,0},{2,3},{3,2},{4,5},{5,4},{6,7},{7,6},{8,9},{9,8},{10,11... | collective-permute-start | bytes 4718600 | tf_op jit(solution)/shard_map/ppermute | solution.py:564
  136.7 27.5 %collective-permute-start.21 = (bf16[768,768]{1,0:T(8,128)(2,1)}, bf16[768,768]{1,0:T(8,128)(2,1)}, u32[]{:S(2)}, u32[]{:S(2)}) collective-permute-start(bf16[768,768]{1,0:T(8,128)(2,1)} %slice_bitcast_fusion.1), channel_id=1, source_target_pairs={{0,2},{1,3},{2,0},{3,1},{4,6},{5,7},{6,4},{7,5},{8,10},{9,11},{10,... | collective-permute-start | bytes 3538952 | tf_op jit(solution)/shard_map/ppermute | solution.py:568
  138.9 9.7 %collective-permute-start.10 = (bf16[512,768]{1,0:T(8,128)(2,1)}, bf16[512,768]{1,0:T(8,128)(2,1)}, u32[]{:S(2)}, u32[]{:S(2)}) collective-permute-start(bf16[512,768]{1,0:T(8,128)(2,1)} %constant_dynamic-slice_fusion.10), channel_id=1, source_target_pairs={{0,1},{1,0},{2,3},{3,2},{4,5},{5,4},{6,7},{7,6},{8,9},{9,8},{10,11... | collective-permute-start | bytes 2359304 | tf_op jit(solution)/shard_map/ppermute | solution.py:564
  139.6 8.9 %copy-start.1 = (bf16[1024,768]{1,0:T(8,128)(2,1)S(1)}, bf16[1024,768]{1,0:T(8,128)(2,1)}, u32[]{:S(2)}) copy-start(bf16[1024,768]{1,0:T(8,128)(2,1)} %copy-done) | copy-start | bytes 4718596
  139.7 8.9 %copy-start.23 = (bf16[1024,768]{1,0:T(8,128)(2,1)S(1)}, bf16[1024,768]{1,0:T(8,128)(2,1)}, u32[]{:S(2)}) copy-start(bf16[1024,768]{1,0:T(8,128)(2,1)} %copy-done.22) | copy-start | bytes 4718596
  145.1 19.1 %copy-start.28 = (bf16[2,768,768]{2,1,0:T(8,128)(2,1)S(1)}, bf16[2,768,768]{2,1,0:T(8,128)(2,1)}, u32[]{:S(2)}) copy-start(bf16[2,768,768]{2,1,0:T(8,128)(2,1)} %get-tuple-element.46) | copy-start | bytes 7077892
  145.1 150.1 %collective-permute-start.27 = (bf16[2,768,768]{2,1,0:T(8,128)(2,1)}, bf16[2,768,768]{2,1,0:T(8,128)(2,1)}, u32[]{:S(2)}, u32[]{:S(2)}) collective-permute-start(bf16[2,768,768]{2,1,0:T(8,128)(2,1)} %get-tuple-element.47), channel_id=1, source_target_pairs={{1,16},{3,18},{5,20},{7,22},{9,24},{11,26},{13,28},{15,30},{16,1},... | collective-permute-start | bytes 7077896 | tf_op jit(solution)/shard_map/ppermute | solution.py:560
  151.4 82.9 %collective-permute-start.11 = (bf16[512,768]{1,0:T(8,128)(2,1)}, bf16[512,768]{1,0:T(8,128)(2,1)}, u32[]{:S(2)}, u32[]{:S(2)}) collective-permute-start(bf16[512,768]{1,0:T(8,128)(2,1)} %add_convert_fusion.1), channel_id=1, source_target_pairs={{1,16},{3,18},{5,20},{7,22},{9,24},{11,26},{13,28},{15,30},{16,1},... | collective-permute-start | bytes 2359304 | tf_op jit(solution)/shard_map/ppermute | solution.py:560
  166.8 17.6 %copy-start.7 = (bf16[1024,384]{1,0:T(8,128)(2,1)S(1)}, bf16[1024,384]{1,0:T(8,128)(2,1)}, u32[]{:S(2)}) copy-start(bf16[1024,384]{1,0:T(8,128)(2,1)} %copy-done.6) | copy-start | bytes 2359300
  166.8 17.6 %copy-start.9 = (bf16[1024,384]{1,0:T(8,128)(2,1)S(1)}, bf16[1024,384]{1,0:T(8,128)(2,1)}, u32[]{:S(2)}) copy-start(bf16[1024,384]{1,0:T(8,128)(2,1)} %copy-done.8) | copy-start | bytes 2359300
  166.8 17.7 %copy-start.11 = (f32[1024,128]{1,0:T(8,128)S(1)}, f32[1024,128]{1,0:T(8,128)}, u32[]{:S(2)}) copy-start(f32[1024,128]{1,0:T(8,128)} %copy-done.10) | copy-start | bytes 1572868
  166.8 17.7 %copy-start.13 = (f32[1024,128]{1,0:T(8,128)S(1)}, f32[1024,128]{1,0:T(8,128)}, u32[]{:S(2)}) copy-start(f32[1024,128]{1,0:T(8,128)} %copy-done.12) | copy-start | bytes 1572868
  166.8 126.7 %collective-permute-start.22 = (bf16[768,768]{1,0:T(8,128)(2,1)}, bf16[768,768]{1,0:T(8,128)(2,1)}, u32[]{:S(2)}, u32[]{:S(2)}) collective-permute-start(bf16[768,768]{1,0:T(8,128)(2,1)} %fusion.2), channel_id=1, source_target_pairs={{1,16},{3,18},{5,20},{7,22},{9,24},{11,26},{13,28},{15,30},{16,1},... | collective-permute-start | bytes 3538952 | tf_op jit(solution)/shard_map/ppermute | solution.py:560
  228.3 2.5 copy-start.24
  228.3 2.5 copy-start.29
  228.3 11.0 %collective-permute-start.13 = (bf16[512,768]{1,0:T(8,128)(2,1)}, bf16[512,768]{1,0:T(8,128)(2,1)S(1)}, u32[]{:S(2)}, u32[]{:S(2)}) collective-permute-start(bf16[512,768]{1,0:T(8,128)(2,1)} %get-tuple-element.39), channel_id=1, source_target_pairs={{0,1},{1,0},{2,3},{3,2},{4,5},{5,4},{6,7},{7,6},{8,9},{9,8},{10,11... | collective-permute-start | bytes 2359304 | tf_op jit(solution)/shard_map/ppermute | solution.py:564
  230.9 3.4 copy-start.26
  230.9 3.4 copy-start.27
  232.3 75.6 %collective-permute-start.15 = (bf16[2,768,384]{2,1,0:T(8,128)(2,1)}, bf16[2,768,384]{2,1,0:T(8,128)(2,1)}, u32[]{:S(2)}, u32[]{:S(2)}) collective-permute-start(bf16[2,768,384]{2,1,0:T(8,128)(2,1)} %fusion.6), channel_id=1, source_target_pairs={{0,2},{1,3},{2,0},{3,1},{4,6},{5,7},{6,4},{7,5},{8,10},{9,11},{10,... | collective-permute-start | bytes 3538952 | tf_op jit(solution)/shard_map/ppermute | solution.py:568
  234.3 5.1 %copy-start.2 = (bf16[1024,768]{1,0:T(8,128)(2,1)S(1)}, bf16[1024,768]{1,0:T(8,128)(2,1)}, u32[]{:S(2)}) copy-start(bf16[1024,768]{1,0:T(8,128)(2,1)} %copy-done) | copy-start | bytes 4718596
  234.3 5.1 %copy-start.4 = (bf16[1024,768]{1,0:T(8,128)(2,1)S(1)}, bf16[1024,768]{1,0:T(8,128)(2,1)}, u32[]{:S(2)}) copy-start(bf16[1024,768]{1,0:T(8,128)(2,1)} %get-tuple-element.40.resid_ref) | copy-start | bytes 4718596
  234.3 5.1 %copy-start.5 = (f32[512,768]{1,0:T(8,128)S(1)}, f32[512,768]{1,0:T(8,128)}, u32[]{:S(2)}) copy-start(f32[512,768]{1,0:T(8,128)} %get-tuple-element.38.keep_ref) | copy-start | bytes 4718596
  234.3 5.1 %copy-start.15 = (s32[3]{0:T(128)S(1)}, s32[3]{0:T(128)}, u32[]{:S(2)}) copy-start(s32[3]{0:T(128)} %copy-done.14) | copy-start | bytes 40
  294.9 6.7 %collective-permute-start.23 = (bf16[768,384]{1,0:T(8,128)(2,1)S(1)}, bf16[768,384]{1,0:T(8,128)(2,1)S(1)}, u32[]{:S(2)}, u32[]{:S(2)}) collective-permute-start(bf16[768,384]{1,0:T(8,128)(2,1)S(1)} %constant_dynamic-slice_fusion.6), channel_id=1, source_target_pairs={{0,1},{1,0},{2,3},{3,2},{4,5},{5,4},{6,7},{7,6},{8,9},{9,8},{10,11... | collective-permute-start | bytes 1769480 | tf_op jit(solution)/shard_map/ppermute | solution.py:564
  297.2 29.2 %collective-permute-start.28 = (bf16[2,768,384]{2,1,0:T(8,128)(2,1)S(1)}, bf16[2,768,384]{2,1,0:T(8,128)(2,1)S(1)}, u32[]{:S(2)}, u32[]{:S(2)}) collective-permute-start(bf16[2,768,384]{2,1,0:T(8,128)(2,1)S(1)} %constant_dynamic-slice_fusion.2), channel_id=1, source_target_pairs={{0,1},{1,0},{2,3},{3,2},{4,5},{5,4},{6,7},{7,6},{8,9},{9,8},{10,11... | collective-permute-start | bytes 3538952 | tf_op jit(solution)/shard_map/ppermute | solution.py:564
  298.3 9.6 %copy-start.30 = (bf16[768,384]{1,0:T(8,128)(2,1)S(1)}, bf16[768,384]{1,0:T(8,128)(2,1)}, u32[]{:S(2)}) copy-start(bf16[768,384]{1,0:T(8,128)(2,1)} %get-tuple-element.45) | copy-start | bytes 1769476
  298.3 45.2 %collective-permute-start.14 = (bf16[512,768]{1,0:T(8,128)(2,1)S(1)}, bf16[512,768]{1,0:T(8,128)(2,1)S(1)}, u32[]{:S(2)}, u32[]{:S(2)}) collective-permute-start(bf16[512,768]{1,0:T(8,128)(2,1)S(1)} %get-tuple-element.41), channel_id=1, source_target_pairs={{1,16},{3,18},{5,20},{7,22},{9,24},{11,26},{13,28},{15,30},{16,1},... | collective-permute-start | bytes 2359304 | tf_op jit(solution)/shard_map/ppermute | solution.py:560
  301.9 8.4 %collective-permute-start.24 = (bf16[192,384]{1,0:T(8,128)(2,1)S(1)}, bf16[192,384]{1,0:T(8,128)(2,1)S(1)}, u32[]{:S(2)}, u32[]{:S(2)}) collective-permute-start(bf16[192,384]{1,0:T(8,128)(2,1)S(1)} %get-tuple-element.68), channel_id=1, source_target_pairs={{0,4},{4,8},{8,12},{12,0},{1,5},{5,9},{9,13},{13,1},{2,6},{6,10},{... | collective-permute-start | bytes 442376 | tf_op jit(solution)/shard_map/ppermute | solution.py:595
  301.9 13.3 %collective-permute-start.25 = (bf16[192,384]{1,0:T(8,128)(2,1)S(1)}, bf16[192,384]{1,0:T(8,128)(2,1)S(1)}, u32[]{:S(2)}, u32[]{:S(2)}) collective-permute-start(bf16[192,384]{1,0:T(8,128)(2,1)S(1)} %get-tuple-element.70), channel_id=1, source_target_pairs={{0,8},{4,12},{8,0},{12,4},{1,9},{5,13},{9,1},{13,5},{2,10},{6,14},... | collective-permute-start | bytes 442376 | tf_op jit(solution)/shard_map/ppermute | solution.py:595
  307.9 10.9 %collective-permute-start.26 = (bf16[192,384]{1,0:T(8,128)(2,1)S(1)}, bf16[192,384]{1,0:T(8,128)(2,1)S(1)}, u32[]{:S(2)}, u32[]{:S(2)}) collective-permute-start(bf16[192,384]{1,0:T(8,128)(2,1)S(1)} %get-tuple-element.69), channel_id=1, source_target_pairs={{0,12},{4,0},{8,4},{12,8},{1,13},{5,1},{9,5},{13,9},{2,14},{6,2},{... | collective-permute-start | bytes 442376 | tf_op jit(solution)/shard_map/ppermute | solution.py:595
  310.3 17.9 %collective-permute-start.16 = (bf16[2,768,384]{2,1,0:T(8,128)(2,1)S(1)}, bf16[2,768,384]{2,1,0:T(8,128)(2,1)S(1)}, u32[]{:S(2)}, u32[]{:S(2)}) collective-permute-start(bf16[2,768,384]{2,1,0:T(8,128)(2,1)S(1)} %add_convert_fusion), channel_id=1, source_target_pairs={{1,16},{3,18},{5,20},{7,22},{9,24},{11,26},{13,28},{15,30},{16,1},... | collective-permute-start | bytes 3538952 | tf_op jit(solution)/shard_map/ppermute | solution.py:560
  326.9 14.8 %collective-permute-start.29 = (bf16[768,384]{1,0:T(8,128)(2,1)S(1)}, bf16[768,384]{1,0:T(8,128)(2,1)S(1)}, u32[]{:S(2)}, u32[]{:S(2)}) collective-permute-start(bf16[768,384]{1,0:T(8,128)(2,1)S(1)} %fusion.10), channel_id=1, source_target_pairs={{0,2},{1,3},{2,0},{3,1},{4,6},{5,7},{6,4},{7,5},{8,10},{9,11},{10,... | collective-permute-start | bytes 1769480 | tf_op jit(solution)/shard_map/ppermute | solution.py:568
  328.4 35.2 %collective-permute-start.17 = (bf16[768,384]{1,0:T(8,128)(2,1)S(1)}, bf16[768,384]{1,0:T(8,128)(2,1)S(1)}, u32[]{:S(2)}, u32[]{:S(2)}) collective-permute-start(bf16[768,384]{1,0:T(8,128)(2,1)S(1)} %dynamic-slice_bitcast_fusion), channel_id=1, source_target_pairs={{0,1},{1,0},{2,3},{3,2},{4,5},{5,4},{6,7},{7,6},{8,9},{9,8},{10,11... | collective-permute-start | bytes 1769480 | tf_op jit(solution)/shard_map/ppermute | solution.py:564
  341.9 4.4 %collective-permute-start.30 = (bf16[192,384]{1,0:T(8,128)(2,1)S(1)}, bf16[192,384]{1,0:T(8,128)(2,1)S(1)}, u32[]{:S(2)}, u32[]{:S(2)}) collective-permute-start(bf16[192,384]{1,0:T(8,128)(2,1)S(1)} %get-tuple-element.65), channel_id=1, source_target_pairs={{0,4},{4,8},{8,12},{12,0},{1,5},{5,9},{9,13},{13,1},{2,6},{6,10},{... | collective-permute-start | bytes 442376 | tf_op jit(solution)/shard_map/ppermute | solution.py:595
  342.0 11.8 %collective-permute-start.31 = (bf16[192,384]{1,0:T(8,128)(2,1)S(1)}, bf16[192,384]{1,0:T(8,128)(2,1)S(1)}, u32[]{:S(2)}, u32[]{:S(2)}) collective-permute-start(bf16[192,384]{1,0:T(8,128)(2,1)S(1)} %get-tuple-element.67), channel_id=1, source_target_pairs={{0,8},{4,12},{8,0},{12,4},{1,9},{5,13},{9,1},{13,5},{2,10},{6,14},... | collective-permute-start | bytes 442376 | tf_op jit(solution)/shard_map/ppermute | solution.py:595
  342.1 13.5 %collective-permute-start.32 = (bf16[192,384]{1,0:T(8,128)(2,1)S(1)}, bf16[192,384]{1,0:T(8,128)(2,1)S(1)}, u32[]{:S(2)}, u32[]{:S(2)}) collective-permute-start(bf16[192,384]{1,0:T(8,128)(2,1)S(1)} %get-tuple-element.66), channel_id=1, source_target_pairs={{0,12},{4,0},{8,4},{12,8},{1,13},{5,1},{9,5},{13,9},{2,14},{6,2},{... | collective-permute-start | bytes 442376 | tf_op jit(solution)/shard_map/ppermute | solution.py:595
  363.8 5.4 %collective-permute-start.18 = (bf16[192,384]{1,0:T(8,128)(2,1)S(1)}, bf16[192,384]{1,0:T(8,128)(2,1)S(1)}, u32[]{:S(2)}, u32[]{:S(2)}) collective-permute-start(bf16[192,384]{1,0:T(8,128)(2,1)S(1)} %get-tuple-element.71), channel_id=1, source_target_pairs={{0,4},{4,8},{8,12},{12,0},{1,5},{5,9},{9,13},{13,1},{2,6},{6,10},{... | collective-permute-start | bytes 442376 | tf_op jit(solution)/shard_map/ppermute | solution.py:595
  363.9 12.8 %collective-permute-start.19 = (bf16[192,384]{1,0:T(8,128)(2,1)S(1)}, bf16[192,384]{1,0:T(8,128)(2,1)S(1)}, u32[]{:S(2)}, u32[]{:S(2)}) collective-permute-start(bf16[192,384]{1,0:T(8,128)(2,1)S(1)} %get-tuple-element.73), channel_id=1, source_target_pairs={{0,8},{4,12},{8,0},{12,4},{1,9},{5,13},{9,1},{13,5},{2,10},{6,14},... | collective-permute-start | bytes 442376 | tf_op jit(solution)/shard_map/ppermute | solution.py:595
  365.6 13.7 %collective-permute-start.20 = (bf16[192,384]{1,0:T(8,128)(2,1)S(1)}, bf16[192,384]{1,0:T(8,128)(2,1)S(1)}, u32[]{:S(2)}, u32[]{:S(2)}) collective-permute-start(bf16[192,384]{1,0:T(8,128)(2,1)S(1)} %get-tuple-element.72), channel_id=1, source_target_pairs={{0,12},{4,0},{8,4},{12,8},{1,13},{5,1},{9,5},{13,9},{2,14},{6,2},{... | collective-permute-start | bytes 442376 | tf_op jit(solution)/shard_map/ppermute | solution.py:595
  (6 other events, 7.3 us)
where the time goes:
time: 390 us; the launch traced here: 389 us
  Pallas kernels  118 us (30%)
  waiting for transfers between devices  87 us (22%)
  blocking collectives  74.9 us (19%)
  starting transfers between devices  49.4 us (13%)
  other arithmetic  37.8 us (10%)
  local copies, waits for them, and re-layouts  18.4 us (5%)
    all_gather x1, blocking collectives, local(): small = jnp.sum(lax.all_gather(small, AXES, axis=0), axis=0)  51.6 us
    pallas_call x1, Pallas kernels, feed(): pl.pallas_call(feed_kernel, grid_spec=pltpu.PrefetchScalarGridSpec(num_sc...  35.5 us
    ppermute x11, waiting for transfers between devices, swap_diagonal(): lax.ppermute(field, AXES, pairs_of(lambda t, d, r: (r % 2, d, r - r % 2 +...  34.2 us
    ppermute x11, starting transfers between devices, swap_diagonal(): lax.ppermute(field, AXES, pairs_of(lambda t, d, r: (r % 2, d, r - r % 2 +...  34.1 us
    pallas_call x1, Pallas kernels, attend_back(): pl.pallas_call(functools.partial(attend_back_kernel, reach), grid=(width...  28.6 us
    ppermute x9, waiting for transfers between devices, sum_rows(): lax.ppermute(sent, 'dp', [(d, (d + step) % dps) for d in range(dps)])  28.3 us
    ppermute x3, waiting for transfers between devices, swap_far(): lax.ppermute(field, 'rep', [(r, r ^ 2) for r in range(lax.axis_size('rep'...  23.4 us
    all_gather x3, blocking collectives, sum_rows(): lax.all_gather(total.astype(jnp.bfloat16), 'rep', axis=0)  23.3 us
  transfers between devices with their start and end apart: 33, of which 15 were waited for; matrix products, arithmetic and copies ran while one was open for 13% of the time, Pallas kernels for 21%

commit v1 on v0

--- a/solution.py
+++ b/solution.py
@@ -194,6 +194,13 @@
     return pl.BlockSpec(shape, lambda *at: (0,) * len(shape))
 
 
+def join_rows(flags, own, near, far, out):
+    half = near.shape[0]
+    for index, got in ((flags[2], near), (1 - flags[2], far)):
+        at = pl.ds(pl.multiple_of(index * half, half), half)
+        out[at, :] = jnp.where(flags[0] == 1, own[at, :], got[...])
+
+
 def turn(field, cos, sin):
     half = HEAD_DIM // 2
     lane = lax.broadcasted_iota(jnp.int32, field.shape, 1) % HEAD_DIM
@@ -202,7 +209,8 @@
 
 
 def project_kernel(
-    flags, rows_ref, gain_ref, shift_ref, cos_ref, sin_ref, w_own, w_got, out_ref, turned_ref, norm_ref
+    flags, rows_ref, gain_ref, shift_ref, cos_ref, sin_ref, w_own, w_near, w_far, out_ref, turned_ref,
+    weight_ref, norm_ref,
 ):
     whole = rows_ref.shape[0]
     step = pl.program_id(0)
@@ -217,10 +225,10 @@
 
         row_blocks(whole, body)
 
-    weight = jnp.where(flags[0] == 1, w_own[0], w_got[0])
+    join_rows(flags, w_own.at[0], w_near.at[0], w_far.at[0], weight_ref.at[0])
 
     def body(i, at):
-        field = dot(norm_ref[at, :], weight)
+        field = dot(norm_ref[at, :], weight_ref[0])
 
         @pl.when(step < 2)
         def _():
@@ -237,10 +245,11 @@
     row_blocks(whole, body)
 
 
-def project(flags, rows, gain, shift, cos, sin, w_own, w_got):
+def project(flags, rows, gain, shift, cos, sin, w_own, w_near, w_far):
     whole, width = rows.shape
     count, unused, columns = w_own.shape
     weight = pl.BlockSpec((1, width, columns), lambda c, flags: (c, 0, 0))
+    part = pl.BlockSpec((1, width // 2, columns), lambda c, flags: (c, 0, 0))
     return pl.pallas_call(
         project_kernel,
         grid_spec=pltpu.PrefetchScalarGridSpec(
@@ -253,17 +262,20 @@
                 whole_spec((whole, LANES)),
                 whole_spec((whole, LANES)),
                 weight,
-                weight,
+                part,
+                part,
             ],
             out_specs=[
                 pl.BlockSpec((1, whole, columns), lambda c, flags: (c, 0, 0)),
                 whole_spec((width, whole)),
+                weight,
             ],
             scratch_shapes=[pltpu.VMEM((whole, width), jnp.bfloat16)],
         ),
         out_shape=[
             jax.ShapeDtypeStruct((count, whole, columns), jnp.bfloat16),
             jax.ShapeDtypeStruct((width, whole), jnp.bfloat16),
+            jax.ShapeDtypeStruct(w_own.shape, jnp.bfloat16),
         ],
         compiler_params=pltpu.CompilerParams(vmem_limit_bytes=40 << 20),
         cost_estimate=pl.CostEstimate(
@@ -271,7 +283,7 @@
             transcendentals=0,
             bytes_accessed=12 * whole * width,
         ),
-    )(flags, rows, gain, shift, cos, sin, w_own, w_got)
+    )(flags, rows, gain, shift, cos, sin, w_own, w_near, w_far)
 
 
 HIDDEN = 256
@@ -287,9 +299,8 @@
 
 
 def feed_kernel(
-    flags, weight_ref, rows_ref, own_ref, got_ref, cot_ref, gain_ref, shift_ref, up_own, up_got,
-    down_own, down_got, down_ref, back_ref, gup_ref, gdown_ref,
-    norm, norm_t, grad, grad_t, act, slope, up_w, down_w,
+    flags, weight_ref, rows_ref, own_ref, got_ref, cot_ref, gain_ref, shift_ref, up_own, up_near,
+    up_far, down_own, down_near, down_far, down_ref, back_ref, keep_ref, send_ref, gdown_ref, norm, norm_t, grad, grad_t, act, slope, up_w, down_w,
 ):
     whole, width = rows_ref.shape
     step = pl.program_id(0)
@@ -308,12 +319,14 @@
 
         row_blocks(whole, body)
 
-    same = flags[0] == 1
     hidden = pl.ds(pl.multiple_of(step * HIDDEN, HIDDEN), HIDDEN)
-    up_block = jnp.where(same, up_own[...], up_got[...])
-    down_block = jnp.where(same, down_own[...], down_got[...])
-    up_w[:, hidden] = up_block
-    down_w[hidden, :] = down_block
+    first = step < pl.num_programs(0) // 2
+    join_rows(flags, up_own, up_near, up_far, up_w.at[:, hidden])
+    down_w[hidden, :] = jnp.where(
+        flags[0] == 1, down_own[...], jnp.where(first, down_near[...], down_far[...])
+    )
+    up_block = up_w[:, hidden]
+    down_block = down_w[hidden, :]
 
     def body(i, at):
         value, rise = gelu_both(dot(norm[at, :], up_block))
@@ -324,7 +337,15 @@
 
     def grads(i, at):
         gdown_ref[0, at, :] = dot(grad_t[at, :], act[:, hidden]).astype(jnp.bfloat16)
-        gup_ref[0, at, :] = dot(norm_t[at, :], slope[:, hidden]).astype(jnp.bfloat16)
+        grad_up = dot(norm_t[at, :], slope[:, hidden]).astype(jnp.bfloat16)
+
+        @pl.when(first)
+        def _():
+            keep_ref[at, :] = grad_up
+
+        @pl.when(jnp.logical_not(first))
+        def _():
+            send_ref[at, :] = grad_up
 
     row_blocks(width, grads)
 
@@ -337,7 +358,7 @@
         row_blocks(whole, body)
 
 
-def feed(flags, weight, rows, own, got, cot, gain, shift, up_own, up_got, down_own, down_got):
+def feed(flags, weight, rows, own, got, cot, gain, shift, up_own, up_near, up_far, down_own, down_near, down_far):
     whole, width = rows.shape
     hidden = up_own.shape[1]
     steps = hidden // HIDDEN
@@ -348,10 +369,20 @@
     def at(j, flags):
         return lax.rem(flags[2] * half + j, steps)
 
+    def early(j):
+        return jnp.minimum(j, half - 1)
+
+    def late(j):
+        return jnp.maximum(j - half, 0)
+
     up_spec = pl.BlockSpec((width, HIDDEN), lambda j, flags: (0, at(j, flags)))
+    up_part = pl.BlockSpec((width // 2, HIDDEN), lambda j, flags: (0, at(j, flags)))
     down_spec = pl.BlockSpec((HIDDEN, width), lambda j, flags: (at(j, flags), 0))
-    piece = pl.BlockSpec((1, width, HIDDEN), lambda j, flags: (j // half, 0, j % half))
+    piece = pl.BlockSpec(
+        (1, width, HIDDEN), lambda j, flags: (at(j, flags) // half, 0, lax.rem(at(j, flags), half))
+    )
     wide_bf16 = jax.ShapeDtypeStruct((whole, width), jnp.bfloat16)
+    part = jax.ShapeDtypeStruct((width, hidden // 2), jnp.bfloat16)
     pieces = jax.ShapeDtypeStruct((2, width, hidden // 2), jnp.bfloat16)
     return pl.pallas_call(
         feed_kernel,
@@ -367,11 +398,19 @@
                 vector,
                 vector,
                 up_spec,
-                up_spec,
+                up_part,
+                up_part,
                 down_spec,
-                down_spec,
+                pl.BlockSpec((HIDDEN, width), lambda j, flags: (early(j), 0)),
+                pl.BlockSpec((HIDDEN, width), lambda j, flags: (late(j), 0)),
             ],
-            out_specs=[tokens, tokens, piece, piece],
+            out_specs=[
+                tokens,
+                tokens,
+                pl.BlockSpec((width, HIDDEN), lambda j, flags: (0, early(j))),
+                pl.BlockSpec((width, HIDDEN), lambda j, flags: (0, late(j))),
+                piece,
+            ],
             scratch_shapes=[
                 pltpu.VMEM((whole, width), jnp.bfloat16),
                 pltpu.VMEM((width, whole), jnp.bfloat16),
@@ -383,20 +422,20 @@
                 pltpu.VMEM((hidden, width), jnp.bfloat16),
             ],
         ),
-        out_shape=[wide_bf16, wide_bf16, pieces, pieces],
+        out_shape=[wide_bf16, wide_bf16, part, part, pieces],
         compiler_params=pltpu.CompilerParams(vmem_limit_bytes=56 << 20),
         cost_estimate=pl.CostEstimate(
             flops=12 * whole * width * hidden, transcendentals=whole * hidden, bytes_accessed=32 * whole * width
         ),
-    )(flags, weight, rows, own, got, cot, gain, shift, up_own, up_got, down_own, down_got)
+    )(flags, weight, rows, own, got, cot, gain, shift, up_own, up_near, up_far, down_own, down_near, down_far)
 
 
 def middle_kernel(
     flags, weight_ref, rows_ref, own_ref, got_ref, cot_ref, back_own, back_got, gain_ref, mixed_ref,
-    w_own, w_got, grad_ref, gmixed_ref, gout_ref, sums_ref, turned,
+    w_ref, grad_ref, gmixed_ref, gout_ref, sums_ref, turned,
 ):
     whole, width = rows_ref.shape
-    weight = jnp.where(flags[0] == 1, w_own[...], w_got[...])
+    weight = w_ref[...]
     gain = gain_ref[...]
     sums_ref[...] = jnp.zeros_like(sums_ref)
 
@@ -425,7 +464,7 @@
     row_blocks(width, grads)
 
 
-def middle(flags, weight, rows, own, got, cot, back_own, back_got, gain, mixed, w_own, w_got):
+def middle(flags, weight, rows, own, got, cot, back_own, back_got, gain, mixed, w_out):
     whole, width = rows.shape
     columns = mixed.shape[1]
     tokens = whole_spec((whole, width))
@@ -438,7 +477,7 @@
             grid=(1,),
             in_specs=[pl.BlockSpec(memory_space=pltpu.SMEM)]
             + [tokens] * 6
-            + [whole_spec((1, width)), narrow, projection, projection],
+            + [whole_spec((1, width)), narrow, projection],
             out_specs=[tokens, narrow, whole_spec((width, columns)), whole_spec((8, width))],
             scratch_shapes=[pltpu.VMEM((width, whole), jnp.bfloat16)],
         ),
@@ -452,14 +491,32 @@
         cost_estimate=pl.CostEstimate(
             flops=4 * whole * width * columns, transcendentals=0, bytes_accessed=18 * whole * width
         ),
-    )(flags, weight, rows, own, got, cot, back_own, back_got, gain, mixed, w_own, w_got)
-
-
-def unproject_kernel(flags, gq_ref, gk_ref, gv_ref, turned_ref, w_own, w_got, keep_ref, send_ref, gw_ref, weight):
-    whole = gq_ref.shape[0]
-    width = turned_ref.shape[0]
-    weight[...] = jnp.where(flags[0] == 1, w_own[...], w_got[...])
-    half = whole // 2
+    )(flags, weight, rows, own, got, cot, back_own, back_got, gain, mixed, w_out)
+
+
+def weigh_kernel(turned_ref, gq_ref, gk_ref, gv_ref, out_ref):
+    def grads(i, at):
+        for c, ref in enumerate((gq_ref, gk_ref, gv_ref)):
+            out_ref[c, at, :] = dot(turned_ref[at, :], ref[...]).astype(jnp.bfloat16)
+
+    row_blocks(turned_ref.shape[0], grads)
+
+
+def weigh(turned, gq, gk, gv):
+    width, whole = turned.shape
+    columns = gq.shape[1]
+    return pl.pallas_call(
+        weigh_kernel,
+        out_shape=jax.ShapeDtypeStruct((3, width, columns), jnp.bfloat16),
+        compiler_params=pltpu.CompilerParams(vmem_limit_bytes=40 << 20),
+        cost_estimate=pl.CostEstimate(
+            flops=6 * whole * width * columns, transcendentals=0, bytes_accessed=6 * whole * width
+        ),
+    )(turned, gq, gk, gv)
+
+
+def unproject_kernel(flags, gq_ref, gk_ref, gv_ref, weight, keep_ref, send_ref):
+    half = keep_ref.shape[0]
 
     def side(near, out_ref):
         def body(i, at):
@@ -474,38 +531,29 @@
     side(1 - flags[1], send_ref)
     side(flags[1], keep_ref)
 
-    def grads(i, at):
-        for c, ref in enumerate((gq_ref, gk_ref, gv_ref)):
-            gw_ref[c, at, :] = dot(turned_ref[at, :], ref[...]).astype(jnp.bfloat16)
-
-    row_blocks(width, grads)
-
-
-def unproject(flags, gq, gk, gv, turned, w_own, w_got):
+
+def unproject(flags, gq, gk, gv, weight):
     whole, columns = gq.shape
-    width = turned.shape[0]
+    width = weight.shape[1]
     narrow = whole_spec((whole, columns))
-    weights = whole_spec((3, width, columns))
     half = whole_spec((whole // 2, width))
     return pl.pallas_call(
         unproject_kernel,
         grid_spec=pltpu.PrefetchScalarGridSpec(
             num_scalar_prefetch=1,
             grid=(1,),
-            in_specs=[narrow, narrow, narrow, whole_spec((width, whole)), weights, weights],
-            out_specs=[half, half, weights],
-            scratch_shapes=[pltpu.VMEM((3, width, columns), jnp.bfloat16)],
+            in_specs=[narrow, narrow, narrow, whole_spec((3, width, columns))],
+            out_specs=[half, half],
         ),
         out_shape=[
             jax.ShapeDtypeStruct((whole // 2, width), jnp.float32),
             jax.ShapeDtypeStruct((whole // 2, width), jnp.bfloat16),
-            jax.ShapeDtypeStruct((3, width, columns), jnp.bfloat16),
         ],
-        compiler_params=pltpu.CompilerParams(vmem_limit_bytes=56 << 20),
+        compiler_params=pltpu.CompilerParams(vmem_limit_bytes=40 << 20),
         cost_estimate=pl.CostEstimate(
-            flops=12 * whole * width * columns, transcendentals=0, bytes_accessed=12 * whole * width
-        ),
-    )(flags, gq, gk, gv, turned, w_own, w_got)
+            flops=6 * whole * width * columns, transcendentals=0, bytes_accessed=8 * whole * width
+        ),
+    )(flags, gq, gk, gv, weight)
 
 
 def first_norm_kernel(flags, rows_ref, keep_ref, got_ref, resid_ref, gain_ref, out_ref, sums_ref):
@@ -546,18 +594,85 @@
     )(flags, rows, keep, got, resid, gain)
 
 
+def past_kernel(dwa_ref, hist_ref, cot_ref, grad_ref, part_ref, sums_ref):
+    @pl.when(pl.program_id(0) == 0)
+    def _():
+        sums_ref[...] = jnp.zeros_like(sums_ref)
+
+    grad = cot_ref[...].astype(jnp.float32)
+    total = jnp.zeros_like(grad)
+    for j in range(hist_ref.shape[0]):
+        field = hist_ref[j].astype(jnp.float32)
+        total += dwa_ref[j] * field
+        grad_ref[j] = (dwa_ref[j] * grad).astype(jnp.bfloat16)
+        sums_ref[j : j + 1, :] += jnp.sum(field * grad, axis=0, keepdims=True)
+    part_ref[...] = total
+
+
+def past(dwa, history, cot):
+    count, rows, width = history.shape
+    layers = pl.BlockSpec((count, ROWS, width), lambda i: (0, i, 0))
+    tokens = pl.BlockSpec((ROWS, width), lambda i: (i, 0))
+    return pl.pallas_call(
+        past_kernel,
+        grid=(rows // ROWS,),
+        in_specs=[pl.BlockSpec(memory_space=pltpu.SMEM), layers, tokens],
+        out_specs=[layers, tokens, whole_spec((8, width))],
+        out_shape=[
+            jax.ShapeDtypeStruct(history.shape, jnp.bfloat16),
+            jax.ShapeDtypeStruct((rows, width), jnp.float32),
+            jax.ShapeDtypeStruct((8, width), jnp.float32),
+        ],
+        compiler_params=pltpu.CompilerParams(vmem_limit_bytes=40 << 20),
+        cost_estimate=pl.CostEstimate(
+            flops=20 * rows * width, transcendentals=0, bytes_accessed=22 * rows * width
+        ),
+    )(dwa, history, cot)
+
+
+def present_kernel(flags, weight_ref, part_ref, cot_ref, own_ref, got_ref, out_ref, sums_ref):
+    field = jnp.where(flags[0] == 1, own_ref[...], got_ref[...]).astype(jnp.float32)
+    out_ref[...] = (part_ref[...] + weight_ref[0] * field).astype(jnp.bfloat16)
+    total = jnp.sum(field * cot_ref[...].astype(jnp.float32), axis=0, keepdims=True)
+    sums_ref[...] = jnp.broadcast_to(total, sums_ref.shape)
+
+
+def present(flags, weight, part, cot, own, got):
+    rows, width = part.shape
+    scalars = pl.BlockSpec(memory_space=pltpu.SMEM)
+    tokens = whole_spec((rows, width))
+    return pl.pallas_call(
+        present_kernel,
+        grid=(1,),
+        in_specs=[scalars, scalars] + [tokens] * 4,
+        out_specs=[tokens, whole_spec((8, width))],
+        out_shape=[
+            jax.ShapeDtypeStruct((rows, width), jnp.bfloat16),
+            jax.ShapeDtypeStruct((8, width), jnp.float32),
+        ],
+        compiler_params=pltpu.CompilerParams(vmem_limit_bytes=40 << 20),
+        cost_estimate=pl.CostEstimate(
+            flops=4 * rows * width, transcendentals=0, bytes_accessed=12 * rows * width
+        ),
+    )(flags, weight, part, cot, own, got)
+
+
 AXES = ("tp", "dp", "rep")
 
 
-def pairs_of(move):
+def crossing(move):
     tps, dps, reps = (lax.axis_size(name) for name in AXES)
     index = lambda t, d, r: (t * dps + d) * reps + r
     every = [(t, d, r) for t in range(tps) for d in range(dps) for r in range(reps)]
-    return [(index(*at), index(*move(*at))) for at in every if move(*at) != at]
+    return [(index(*at), index(*move(*at))) for at in every if at[0] != at[2] % 2]
 
 
 def swap_diagonal(field):
-    return lax.ppermute(field, AXES, pairs_of(lambda t, d, r: (r % 2, d, r - r % 2 + t)))
+    return lax.ppermute(field, AXES, crossing(lambda t, d, r: (r % 2, d, r - r % 2 + t)))
+
+
+def swap_far_crossing(field):
+    return lax.ppermute(field, AXES, crossing(lambda t, d, r: (t, d, r ^ 2)))
 
 
 def swap_near(field):
@@ -568,50 +683,50 @@
     return lax.ppermute(field, "rep", [(r, r ^ 2) for r in range(lax.axis_size("rep"))])
 
 
-def ordered(own, other, first):
+def after(field, *others):
+    return lax.optimization_barrier((field, *others))[0]
+
+
+def ordered(own, other, first, axis=0):
     return jnp.where(
-        first, jnp.concatenate([own, other], axis=0), jnp.concatenate([other, own], axis=0)
-    )
-
-
-def take(field, index):
-    return lax.dynamic_index_in_dim(field, index, 0, keepdims=False)
-
-
-def half_columns(field, index):
-    size = field.shape[-1] // 2
-    return lax.dynamic_slice_in_dim(field, index * size, size, field.ndim - 1)
-
-
-def sum_rows(block):
+        first, jnp.concatenate([own, other], axis=axis), jnp.concatenate([other, own], axis=axis)
+    )
+
+
+def take(field, index, axis=0):
+    return lax.dynamic_index_in_dim(field, index, axis, keepdims=False)
+
+
+def part_of(field, index, axis):
+    size = field.shape[axis] // 2
+    return lax.dynamic_slice_in_dim(field, index * size, size, axis)
+
+
+def add(*fields):
+    return sum(field.astype(jnp.float32) for field in fields).astype(jnp.bfloat16)
+
+
+def move_rows(block):
     dps = lax.axis_size("dp")
-    rows = block.shape[0] // dps
-    low = block.astype(jnp.bfloat16)
-    if dps <= 8:
-        place = lax.axis_index("dp")
-        total = lax.dynamic_slice_in_dim(block, place * rows, rows, 0)
-        for step in range(1, dps):
-            sent = lax.dynamic_slice_in_dim(low, lax.rem(place + step, dps) * rows, rows, 0)
-            total = total + lax.ppermute(
-                sent, "dp", [(d, (d + step) % dps) for d in range(dps)]
-            ).astype(jnp.float32)
-    else:
-        total = lax.psum_scatter(low, "dp", scatter_dimension=0, tiled=True)
-    return lax.all_gather(total.astype(jnp.bfloat16), "rep", axis=0).astype(jnp.float32)
-
-
-def sum_far_first(mine, theirs, same, near):
-    pair = (mine.astype(jnp.float32) + swap_far(theirs).astype(jnp.float32)).astype(jnp.bfloat16)
-    pair = jnp.where(same, pair, swap_diagonal(pair))
-    keep, send = half_columns(pair, near), half_columns(pair, 1 - near)
-    return sum_rows(keep.astype(jnp.float32) + swap_near(send).astype(jnp.float32))
-
-
-def sum_diagonal_first(pieces, same, near):
-    pieces = jnp.where(same, pieces, swap_diagonal(pieces))
-    keep, send = half_columns(pieces, near), half_columns(pieces, 1 - near)
-    pair = keep.astype(jnp.float32) + swap_near(send).astype(jnp.float32)
-    return sum_rows(pair[0] + swap_far(pair[1].astype(jnp.bfloat16)).astype(jnp.float32))
+    if dps > 8:
+        flat = block.reshape(-1, block.shape[2])
+        return [lax.psum_scatter(flat, "dp", scatter_dimension=0, tiled=True)]
+    place = lax.axis_index("dp")
+    moved = [take(block, place)]
+    for step in range(1, dps):
+        sent = take(block, lax.rem(place + step, dps))
+        moved.append(lax.ppermute(sent, "dp", [(d, (d + step) % dps) for d in range(dps)]))
+    return moved
+
+
+def sum_everywhere(field):
+    for name in ("rep", "tp", "dp"):
+        size = lax.axis_size(name)
+        bit = 1
+        while bit < size:
+            field = field + lax.ppermute(field, name, [(d, d ^ bit) for d in range(size)])
+            bit *= 2
+    return field
 
 
 def local(
@@ -638,12 +753,18 @@
     flags = jnp.stack([same.astype(jnp.int32), near, far])
     own_weight = dwa_weights[hist_count:]
 
-    input_half = jnp.where(same, layer_input[0], swap_diagonal(layer_input[0]))
-    got_qkv = swap_diagonal(w_qkv)
-    got_out = swap_diagonal(w_out)
-    got_up = swap_diagonal(w_up)
-    cot_half = jnp.where(same, cotangent[0], swap_diagonal(cotangent[0]))
-    got_down = swap_diagonal(w_down)
+    dps = lax.axis_size("dp")
+    input_got = swap_diagonal(layer_input[0])
+    qkv_near = swap_diagonal(part_of(w_qkv, far, 1))
+    out_near = swap_diagonal(part_of(w_out, far, 0))
+    up_near = swap_diagonal(part_of(w_up, far, 0))
+    cot_got = swap_diagonal(cotangent[0])
+    down_near = swap_diagonal(part_of(w_down, far, 0))
+    qkv_far = swap_far_crossing(qkv_near)
+    out_far = swap_far_crossing(out_near)
+    up_far = swap_far_crossing(up_near)
+    down_far = swap_far_crossing(down_near)
+
     own_lengths = jnp.where(same, lengths, swap_near(lengths))[0]
     seq_owner, token_place = positions(own_lengths, whole)
     seq_begin = jnp.arange(whole, dtype=jnp.int32) - token_place
@@ -655,21 +776,25 @@
     angles = token_place.astype(jnp.float32)[:, None] * frequency[None, :]
     cos_table = jnp.cos(angles)
     sin_table = jnp.sin(angles) * jnp.where(lane % HEAD_DIM < half_dim, -1.0, 1.0)[None, :]
+    grad_history, past_sum, sums_past = past(dwa_weights, history[:, 0], cotangent[0])
+
+    input_half = jnp.where(same, layer_input[0], input_got)
     layer_rows = ordered(input_half, swap_near(input_half), near == 0)
-    cot_rows = ordered(cot_half, swap_near(cot_half), near == 0)
+    layer_rows = after(layer_rows, past_sum, cos_table, sin_table, start_column, start_row)
     gain_one, bias_one = gain_one[None], bias_one[None]
     gain_two, bias_two = gain_two[None], bias_two[None]
 
-    projected, norm_one_t = project(
-        flags, layer_rows, gain_one, bias_one, cos_table, sin_table, w_qkv, got_qkv
+    projected, norm_one_t, weight_qkv = project(
+        flags, layer_rows, gain_one, bias_one, cos_table, sin_table, w_qkv, qkv_near, qkv_far
     )
     queries, keys, values = projected[0], projected[1], projected[2]
     mixed = attend(start_column, queries, keys, values, LONGEST)
-    attn = jnp.dot(
-        mixed, jnp.where(same, w_out, got_out), preferred_element_type=jnp.float32
-    ).astype(jnp.bfloat16)
+    weight_out = jnp.where(same, w_out, ordered(out_near, out_far, far == 0))
+    attn = jnp.dot(mixed, weight_out, preferred_element_type=jnp.float32).astype(jnp.bfloat16)
     attn_got = swap_near(attn)
-    down, back, grad_up, grad_down = feed(
+    cot_half = jnp.where(same, cotangent[0], after(cot_got, mixed))
+    cot_rows = ordered(cot_half, swap_near(cot_half), near == 0)
+    down, back, up_keep, up_send, grad_down = feed(
         flags,
         own_weight,
         layer_rows,
@@ -679,11 +804,15 @@
         gain_two,
         bias_two,
         w_up,
-        got_up,
+        up_near,
+        up_far,
         w_down,
-        got_down,
+        down_near,
+        down_far,
     )
     back_got = swap_near(back)
+    up_got = swap_far(up_send)
+    down_got = swap_diagonal(grad_down)
     grad_attn, grad_mixed, grad_out, sums_two = middle(
         flags,
         own_weight,
@@ -695,71 +824,85 @@
         back_got,
         gain_two,
         mixed,
-        w_out,
-        got_out,
-    )
-    grad_w_up = sum_far_first(grad_up[0], grad_up[1], same, near)
-    grad_w_down = sum_diagonal_first(grad_down, same, near)
+        weight_out,
+    )
+    grad_queries, grad_keys, grad_values = attend_back(
+        start_row, cos_table, sin_table, queries, keys, values, grad_mixed, LONGEST
+    )
+
+    def columns_of(pieces):
+        return pieces.transpose(1, 0, 2).reshape(pieces.shape[1], -1)
+
+    def by_dp(block):
+        return block.reshape(dps, block.shape[0] // dps, block.shape[1])
+
+    up_pair = add(up_keep, after(up_got, grad_keys))
+    up_moved = swap_diagonal(up_pair)
+    down_pair = jnp.where(same, grad_down, after(down_got, grad_keys))
+    down_other = swap_near(take(down_pair, 1 - near))
+    grad_qkv = weigh(norm_one_t, grad_queries, grad_keys, grad_values)
+    mine = take(grad_qkv, far)
+    attn_got_far = swap_far(take(grad_qkv, 1 - far))
+    late_pieces = jnp.stack([grad_qkv[2], grad_out])
+    late_got = swap_diagonal(late_pieces)
+    keep, send = unproject(flags, grad_queries, grad_keys, grad_values, weight_qkv)
+    send_got = swap_near(send)
+    down_one = add(take(down_pair, near), after(down_other, grad_qkv))
+    down_blocks = move_rows(by_dp(down_one))
+    input_grad, sums_one = first_norm_back(flags, layer_rows, keep, send_got, grad_attn, gain_one)
+    grad_input = swap_diagonal(input_grad)
+    up_pair = jnp.where(same, up_pair, after(up_moved, grad_qkv))
+    up_one = add(part_of(up_pair, near, 1), swap_near(part_of(up_pair, 1 - near, 1)))
+    up_blocks = move_rows(by_dp(up_one))
 
     def half_of(field, index):
         return lax.dynamic_slice_in_dim(field, index * rows, rows, 0)
 
-    block_half = sum(
-        half_of(field, near).astype(jnp.float32) for field in (layer_rows, attn, attn_got, down)
-    ) + swap_near(half_of(down, 1 - near)).astype(jnp.float32)
-    block_half = block_half.astype(jnp.bfloat16)
-    block_out = jnp.where(same, block_half, swap_diagonal(block_half)).astype(jnp.float32)
-    hist_rows = history[:, 0].astype(jnp.float32)
-    output = (
-        jnp.sum(dwa_weights[:hist_count, None, None] * hist_rows, axis=0)
-        + dwa_weights[hist_count] * block_out
-    )
-    grad_block = cotangent[0].astype(jnp.float32)
-    grad_history = (dwa_weights[:hist_count, None, None] * grad_block[None]).astype(jnp.bfloat16)[
-        :, None
-    ]
-    dwa_terms = jnp.concatenate(
-        [jnp.sum(hist_rows * grad_block[None], axis=(1, 2)), jnp.sum(block_out * grad_block)[None]]
-    )
-
-    grad_queries, grad_keys, grad_values = attend_back(
-        start_row, cos_table, sin_table, queries, keys, values, grad_mixed, LONGEST
-    )
-    keep, send, grad_qkv = unproject(
-        flags, grad_queries, grad_keys, grad_values, norm_one_t, w_qkv, got_qkv
-    )
-    input_grad, sums_one = first_norm_back(flags, layer_rows, keep, swap_near(send), grad_attn, gain_one)
-    grad_input = jnp.where(same, input_grad, swap_diagonal(input_grad))
-    attn_pieces = jnp.concatenate([grad_qkv, grad_out[None]], axis=0)
-    mine = lax.dynamic_slice_in_dim(attn_pieces, 2 * far, 2, 0)
-    theirs = lax.dynamic_slice_in_dim(attn_pieces, 2 - 2 * far, 2, 0)
-    pair = (mine.astype(jnp.float32) + swap_far(theirs).astype(jnp.float32)).astype(jnp.bfloat16)
-    pair = jnp.where(same, pair, swap_diagonal(pair))
-    grad_w_attn = sum_rows(
-        take(pair, near).astype(jnp.float32) + swap_near(take(pair, 1 - near)).astype(jnp.float32)
-    )
-
+    down_half = after(half_of(down, 1 - near), input_grad)
+    block_half = add(
+        *[half_of(field, near) for field in (layer_rows, attn, attn_got, down)], swap_near(down_half)
+    )
+    output, sums_now = present(
+        flags, own_weight, past_sum, cotangent[0], block_half, swap_diagonal(block_half)
+    )
     small = jnp.concatenate(
-        [sums_one[:2], sums_two[:2], jnp.pad(dwa_terms, (0, gain_one.shape[1] - hist_count - 1))[None]]
-    )
-    small = jnp.sum(lax.all_gather(small, AXES, axis=0), axis=0)
-
-    def columns_of(pieces):
-        return pieces.transpose(1, 0, 2).reshape(pieces.shape[1], -1)
+        [sums_one[:2], sums_two[:2], sums_past[:hist_count], sums_now[:1]], axis=0
+    )
+    small = sum_everywhere(small)
+
+    key_pair = add(mine, attn_got_far)
+    key_pair = by_dp(jnp.where(same, key_pair, swap_diagonal(key_pair)))
+    key_one = add(part_of(key_pair, near, 1), swap_near(part_of(key_pair, 1 - near, 1)))
+    late_pair = jnp.where(same, late_pieces, late_got)
+    late_one = add(take(late_pair, near), swap_near(take(late_pair, 1 - near)))
+    late_sum = add(*move_rows(by_dp(late_one)))
+    key_sum = add(*move_rows(key_one))
+    late_sum = add(late_sum, swap_far(late_sum))
+    grad_value_out = ordered(late_sum[None], swap_near(late_sum)[None], near == 0)
+    key_half = ordered(key_sum, swap_near(key_sum), near == 0)
+    grad_query_key = ordered(key_half[None], swap_far(key_half)[None], far == 0)
+
+    down_sum = add(*down_blocks)
+    down_sum = add(down_sum, swap_far(down_sum))
+    grad_w_down = ordered(down_sum[None], swap_near(down_sum)[None], near == 0)
+    up_sum = add(*up_blocks)
+    up_half = ordered(up_sum, swap_near(up_sum), near == 0, axis=1)
+    grad_w_up = ordered(up_half[None], swap_far(up_half)[None], far == 0)
+    grad_w_qkv = jnp.concatenate([grad_query_key, grad_value_out[:1]], axis=0)
 
     return (
-        output.astype(jnp.bfloat16)[None],
-        grad_input[None],
-        grad_history,
-        small[4, : hist_count + 1],
+        output[None],
+        jnp.where(same, input_grad, grad_input)[None],
+        grad_history[:, None],
+        jnp.sum(small[4:], axis=1),
         small[0],
         small[1],
-        grad_w_attn[:3],
-        grad_w_attn[3].T,
+        grad_w_qkv.astype(jnp.float32),
+        grad_value_out[1].astype(jnp.float32).T,
         small[2],
         small[3],
-        columns_of(grad_w_up),
-        columns_of(grad_w_down).T,
+        columns_of(grad_w_up).astype(jnp.float32),
+        columns_of(grad_w_down).astype(jnp.float32).T,
     )
 
 

time: 390 us -> 338 us (0.87)
  blocking collectives: 74.9 us -> 0 us
  starting transfers between devices: 49.4 us -> 86.2 us
  other arithmetic: 37.8 us -> 18.8 us
    all_gather x4 -> x0, blocking collectives: 74.9 us -> none  [the longest x1 51.6 us: local(): small = jnp.sum(lax.all_gather(small, AXES, axis=0), axis=0)]
    ppermute x20 -> x33, starting transfers between devices: 44.8 us -> 74.6 us  [the longest x12 43.3 us: swap_diagonal(): lax.ppermute(field, AXES, crossing(lambda t, d, r: (r % 2, d, r - r % 2 +...]
    ppermute x3 -> x6, waiting for transfers between devices: 23.4 us -> 2.24 us  [swap_far(): lax.ppermute(field, 'rep', [(r, r ^ 2) for r in range(lax.axis_size('rep'...]
    ppermute x20 -> x33, waiting for transfers between devices: 62.5 us -> 83.2 us  [the longest x12 35.2 us: move_rows(): lax.ppermute(sent, 'dp', [(d, (d + step) % dps) for d in range(dps)])]
    reduce_sum x3 -> x1, other arithmetic: 9.82 us -> 0.63 us  [local(): jnp.sum(small[4:], axis=1)]
    pallas_call x0 -> x3, Pallas kernels: none -> 8.19 us  [the longest x1 2.94 us: past(): pl.pallas_call(past_kernel, grid=(rows // ROWS,), in_specs=[pl.BlockSpec(...]
    pallas_call x1, Pallas kernels: 11.5 us -> 3.67 us  [unproject(): pl.pallas_call(unproject_kernel, grid_spec=pltpu.PrefetchScalarGridSpec(n...]
    convert_element_type x12 -> x14, other arithmetic: 10.5 us -> 4.54 us  [the longest x13 3.57 us: add(): sum((field.astype(jnp.float32) for field in fields)).astype(jnp.bfloat16)]
  transfers between devices with their start and end apart: 33 -> 54, of which waited for: 15 -> 24; matrix products, arithmetic and copies ran while one was open for 13% -> 9% of each run, Pallas kernels for 21% -> 24%
where the time goes in v1:
time: 338 us; the launch traced here: 333 us
  Pallas kernels  118 us (35%)
  starting transfers between devices  86.2 us (26%)
  waiting for transfers between devices  85.9 us (25%)
  local copies, waits for them, and re-layouts  21.6 us (6%)
  other arithmetic  18.8 us (6%)
    ppermute x12, starting transfers between devices, swap_diagonal(): lax.ppermute(field, AXES, crossing(lambda t, d, r: (r % 2, d, r - r % 2 +...  43.3 us
    pallas_call x1, Pallas kernels, feed(): pl.pallas_call(feed_kernel, grid_spec=pltpu.PrefetchScalarGridSpec(num_sc...  36.8 us
    ppermute x12, waiting for transfers between devices, move_rows(): lax.ppermute(sent, 'dp', [(d, (d + step) % dps) for d in range(dps)])  35.2 us
    pallas_call x1, Pallas kernels, attend_back(): pl.pallas_call(functools.partial(attend_back_kernel, reach), grid=(width...  28.5 us
    ppermute x12, waiting for transfers between devices, swap_diagonal(): lax.ppermute(field, AXES, crossing(lambda t, d, r: (r % 2, d, r - r % 2 +...  22.3 us
    ppermute x4, waiting for transfers between devices, swap_far_crossing(): return lax.ppermute(field, AXES, crossing(lambda t, d, r: (t, d, r ^ 2)))  21.7 us
    ppermute x12, starting transfers between devices, move_rows(): lax.ppermute(sent, 'dp', [(d, (d + step) % dps) for d in range(dps)])  18.3 us
    pallas_call x1, Pallas kernels, attend(): pl.pallas_call(functools.partial(attend_kernel, reach), grid=(width // LA...  17.2 us
  transfers between devices with their start and end apart: 54, of which 24 were waited for; matrix products, arithmetic and copies ran while one was open for 9% of the time, Pallas kernels for 24%

profile of v1, /device:TPU:9, one launch (start us, length us, event | category | flops | bytes accessed | tf_op | source)
XLA Modules:
  0.0 333.0 jit_solution(15498655866442137136)
XLA Ops:
  0.7 3.8 %collective-permute-start = (bf16[512,768]{1,0:T(8,128)(2,1)}, bf16[512,768]{1,0:T(8,128)(2,1)}, u32[]{:S(2)}, u32[]{:S(2)}) collective-permute-start(bf16[512,768]{1,0:T(8,128)(2,1)} %bitcast.132), channel_id=1, source_target_pairs={{1,16},{3,18},{5,20},{7,22},{9,24},{11,26},{13,28},{15,30},{16,1},... | collective-permute-start | bytes 2359304 | tf_op jit(solution)/shard_map/ppermute | solution.py:671
  4.6 1.3 constant_dynamic-slice_fusion.6
  5.9 1.9 collective-permute-start.3
  7.9 3.6 %collective-permute-start.8 = (bf16[512,768]{1,0:T(8,128)(2,1)S(1)}, bf16[512,768]{1,0:T(8,128)(2,1)}, u32[]{:S(2)}, u32[]{:S(2)}) collective-permute-start(bf16[512,768]{1,0:T(8,128)(2,1)S(1)} %bitcast.114), channel_id=1, source_target_pairs={{1,16},{3,18},{5,20},{7,22},{9,24},{11,26},{13,28},{15,30},{16,1},... | collective-permute-start | bytes 2359304 | tf_op jit(solution)/shard_map/ppermute | solution.py:671
  11.6 1.9 collective-permute-start.5
  13.6 1.9 copy-done.3
  15.5 2.9 shard_map.220
  19.6 2.5 constant_dynamic-slice_fusion.3
  23.3 3.6 %collective-permute-start.10 = (bf16[384,1536]{1,0:T(8,128)(2,1)}, bf16[384,1536]{1,0:T(8,128)(2,1)}, u32[]{:S(2)}, u32[]{:S(2)}) collective-permute-start(bf16[384,1536]{1,0:T(8,128)(2,1)} %constant_dynamic-slice_fusion.4), channel_id=1, source_target_pairs={{1,16},{3,18},{5,20},{7,22},{9,24},{11,26},{13,28},{15,30},{16,1},... | collective-permute-start | bytes 3538952 | tf_op jit(solution)/shard_map/ppermute | solution.py:671
  27.3 1.5 broadcast_select_fusion.4
  28.9 6.7 %collective-permute-done.5 = bf16[192,768]{1,0:T(8,128)(2,1)} collective-permute-done((bf16[192,768]{1,0:T(8,128)(2,1)S(1)}, bf16[192,768]{1,0:T(8,128)(2,1)}, u32[]{:S(2)}, u32[]{:S(2)}) %collective-permute-start.5) | collective-permute-done | bytes 294944 | tf_op jit(solution)/shard_map/ppermute | solution.py:671
  35.6 3.1 collective-permute-start.6
  38.7 2.2 collective-permute-start.4
  40.9 1.9 fusion.7
  43.3 4.8 %collective-permute-start.12 = (bf16[768,768]{1,0:T(8,128)(2,1)}, bf16[768,768]{1,0:T(8,128)(2,1)S(1)}, u32[]{:S(2)}, u32[]{:S(2)}) collective-permute-start(bf16[768,768]{1,0:T(8,128)(2,1)} %constant_dynamic-slice_fusion.3), channel_id=1, source_target_pairs={{1,16},{3,18},{5,20},{7,22},{9,24},{11,26},{13,28},{15,30},{16,1},... | collective-permute-start | bytes 3538952 | tf_op jit(solution)/shard_map/ppermute | solution.py:671
  48.0 1.3 fusion.3.w_ref
  50.3 2.5 collective-permute-done.4.w_far
  52.8 9.2 %shard_map.221 = (bf16[3,1024,384]{2,1,0:T(8,128)(2,1)S(1)}, bf16[768,1024]{1,0:T(8,128)(2,1)S(1)}, bf16[3,768,384]{2,1,0:T(8,128)(2,1)S(1)}) custom-call(s32[3]{0:T(128)S(1)} %pad_add_fusion.flags, bf16[1024,768]{1,0:T(8,128)(2,1)S(1)} %maximum_select_fusion.rows_ref, f32[1,768]{1,0:T(1,128)S(1)} %broadcast_in_dim.73.gain_ref, ...), custom_call_target="tpu_custom_call" | custom-call | flops 1811939328 | bytes 9437184 | tf_op jit(solution)/shard_map/pallas_call | solution.py:253
  63.7 17.2 %shard_map.222.mixed_ref = bf16[1024,384]{1,0:T(8,128)(2,1)S(1)} custom-call(s32[1024,128]{1,0:T(8,128)S(1)} %broadcast_in_dim.71.start_ref, bf16[1024,384]{1,0:T(8,128)(2,1)S(1)} %get-tuple-element.104.q_ref, bf16[1024,384]{1,0:T(8,128)(2,1)S(1)} %get-tuple-element.103.k_ref, bf16[1024,384]{1,0:T(8,128)(2,1)S(1)} %get-tuple-element.102.v_ref), custom_call_target="tpu_custom_call" | custom-call | flops 1006632960 | bytes 3145728 | tf_op jit(solution)/shard_map/pallas_call | solution.py:78
  82.0 3.1 collective-permute-start.11
  85.2 2.3 collective-permute-start.13
  87.5 1.2 broadcast_select_fusion.3
  91.1 1.9 maximum_select_fusion.1.cot_ref
  93.0 6.2 %collective-permute-done.11.up_far = bf16[384,1536]{1,0:T(8,128)(2,1)S(1)} collective-permute-done((bf16[384,1536]{1,0:T(8,128)(2,1)}, bf16[384,1536]{1,0:T(8,128)(2,1)S(1)}, u32[]{:S(2)}, u32[]{:S(2)}) %collective-permute-start.11) | collective-permute-done | bytes 1179680 | tf_op jit(solution)/shard_map/ppermute | solution.py:675
  99.2 12.6 %collective-permute-done.13.down_far = bf16[768,768]{1,0:T(8,128)(2,1)S(1)} collective-permute-done((bf16[768,768]{1,0:T(8,128)(2,1)S(1)}, bf16[768,768]{1,0:T(8,128)(2,1)S(1)}, u32[]{:S(2)}, u32[]{:S(2)}) %collective-permute-start.13) | collective-permute-done | bytes 1179680 | tf_op jit(solution)/shard_map/ppermute | solution.py:675
  114.0 36.8 %shard_map.223 = (bf16[1024,768]{1,0:T(8,128)(2,1)}, bf16[1024,768]{1,0:T(8,128)(2,1)}, bf16[768,768]{1,0:T(8,128)(2,1)}, bf16[768,768]{1,0:T(8,128)(2,1)}, bf16[2,768,768]{2,1,0:T(8,128)(2,1)}) custom-call(s32[3]{0:T(128)} %copy-done.13, f32[1]{0:T(128)} %slice.48.weight_ref, bf16[1024,768]{1,0:T(8,128)(2,1)} %copy-done, bf16[1024,768]{1,0:T(8,128)(2,1)} %copy-done.21, ...), custom_call_target="tpu_custom_call" | custom-call | flops 14495514624 | bytes 25165824 | tf_op jit(solution)/shard_map/pallas_call | solution.py:387
  150.9 6.0 %collective-permute-start.47 = (bf16[2,768,768]{2,1,0:T(8,128)(2,1)}, bf16[2,768,768]{2,1,0:T(8,128)(2,1)}, u32[]{:S(2)}, u32[]{:S(2)}) collective-permute-start(bf16[2,768,768]{2,1,0:T(8,128)(2,1)} %get-tuple-element.71), channel_id=1, source_target_pairs={{1,16},{3,18},{5,20},{7,22},{9,24},{11,26},{13,28},{15,30},{16,1},... | collective-permute-start | bytes 7077896 | tf_op jit(solution)/shard_map/ppermute | solution.py:671
  156.9 1.3 collective-permute-start.39
  158.1 12.3 %shard_map.224 = (bf16[1024,768]{1,0:T(8,128)(2,1)}, bf16[1024,384]{1,0:T(8,128)(2,1)}, bf16[768,384]{1,0:T(8,128)(2,1)}, f32[8,768]{1,0:T(8,128)}) custom-call(s32[3]{0:T(128)} %copy-done.13, f32[1]{0:T(128)} %slice.48.weight_ref, bf16[1024,768]{1,0:T(8,128)(2,1)} %copy-done, bf16[1024,768]{1,0:T(8,128)(2,1)} %copy-done.21, bf16[1024,768]{1,0:T(8,128)(2,1)} %copy-done.23, ...), custom_call_target="tpu_custom_call" | custom-call | flops 1207959552 | bytes 14155776 | tf_op jit(solution)/shard_map/pallas_call | solution.py:473
  171.6 28.5 %shard_map.225 = (bf16[1024,384]{1,0:T(8,128)(2,1)S(1)}, bf16[1024,384]{1,0:T(8,128)(2,1)S(1)}, bf16[1024,384]{1,0:T(8,128)(2,1)S(1)}) custom-call(s32[8,1024]{1,0:T(8,128)S(1)} %broadcast_in_dim.72.start_ref, f32[1024,128]{1,0:T(8,128)S(1)} %copy-done.11, f32[1024,128]{1,0:T(8,128)S(1)} %copy-done.9, bf16[1024,384]{1,0:T(8,128)(2,1)S(1)} %get-tuple-element.104.q_ref, ...), custom_call_target="tpu_custom_call" | custom-call | flops 2516582400 | bytes 5505024 | tf_op jit(solution)/shard_map/pallas_call | solution.py:154
  200.2 2.9 shard_map.229
  204.6 3.7 %shard_map.226 = (f32[512,768]{1,0:T(8,128)S(1)}, bf16[512,768]{1,0:T(8,128)(2,1)S(1)}) custom-call(s32[3]{0:T(128)S(1)} %copy-done.14, bf16[1024,384]{1,0:T(8,128)(2,1)S(1)} %get-tuple-element.50.gq_ref, bf16[1024,384]{1,0:T(8,128)(2,1)S(1)} %get-tuple-element.51.gk_ref, bf16[1024,384]{1,0:T(8,128)(2,1)S(1)} %get-tuple-element.52.gv_ref, ...), custom_call_target="tpu_custom_call" | custom-call | flops 1811939328 | bytes 6291456 | tf_op jit(solution)/shard_map/pallas_call | solution.py:540
  209.5 1.6 add_convert_fusion
  211.2 2.7 collective-permute-start.40
  213.9 1.8 collective-permute-done.24
  215.8 5.6 %collective-permute-start.25 = (bf16[768,384]{1,0:T(8,128)(2,1)S(1)}, bf16[768,384]{1,0:T(8,128)(2,1)S(1)}, u32[]{:S(2)}, u32[]{:S(2)}) collective-permute-start(bf16[768,384]{1,0:T(8,128)(2,1)S(1)} %fusion.2), channel_id=1, source_target_pairs={{1,16},{3,18},{5,20},{7,22},{9,24},{11,26},{13,28},{15,30},{16,1},... | collective-permute-start | bytes 1769480 | tf_op jit(solution)/shard_map/ppermute | solution.py:671
  221.6 2.1 collective-permute-start.32
  224.5 1.9 shard_map.227
  226.4 3.6 %collective-permute-start.18 = (bf16[512,768]{1,0:T(8,128)(2,1)S(1)}, bf16[512,768]{1,0:T(8,128)(2,1)S(1)}, u32[]{:S(2)}, u32[]{:S(2)}) collective-permute-start(bf16[512,768]{1,0:T(8,128)(2,1)S(1)} %get-tuple-element.57), channel_id=1, source_target_pairs={{1,16},{3,18},{5,20},{7,22},{9,24},{11,26},{13,28},{15,30},{16,1},... | collective-permute-start | bytes 2359304 | tf_op jit(solution)/shard_map/ppermute | solution.py:671
  230.1 1.9 broadcast_select_fusion
  232.2 3.0 collective-permute-done.25
  235.5 12.3 %collective-permute-done.32 = bf16[2,768,384]{2,1,0:T(8,128)(2,1)S(1)} collective-permute-done((bf16[2,768,384]{2,1,0:T(8,128)(2,1)S(1)}, bf16[2,768,384]{2,1,0:T(8,128)(2,1)S(1)}, u32[]{:S(2)}, u32[]{:S(2)}) %collective-permute-start.32) | collective-permute-done | bytes 1179680 | tf_op jit(solution)/shard_map/ppermute | solution.py:671
  248.2 1.4 collective-permute-start.27
  250.6 1.4 collective-permute-start.29
  252.2 1.6 collective-permute-done.28
  256.2 3.5 %collective-permute-start.17 = (bf16[512,768]{1,0:T(8,128)(2,1)S(1)}, bf16[512,768]{1,0:T(8,128)(2,1)S(1)}, u32[]{:S(2)}, u32[]{:S(2)}) collective-permute-start(bf16[512,768]{1,0:T(8,128)(2,1)S(1)} %add_convert_fusion.1.own_ref), channel_id=1, source_target_pairs={{1,16},{3,18},{5,20},{7,22},{9,24},{11,26},{13,28},{15,30},{16,1},... | collective-permute-start | bytes 2359304 | tf_op jit(solution)/shard_map/ppermute | solution.py:671
  262.6 2.6 collective-permute-start.43
  266.6 5.6 %collective-permute-done.42 = bf16[192,384]{1,0:T(8,128)(2,1)S(1)} collective-permute-done((bf16[192,384]{1,0:T(8,128)(2,1)S(1)}, bf16[192,384]{1,0:T(8,128)(2,1)S(1)}, u32[]{:S(2)}, u32[]{:S(2)}) %collective-permute-start.42) | collective-permute-done | bytes 147488 | tf_op jit(solution)/shard_map/ppermute | solution.py:718
  272.2 2.6 collective-permute-start.34
  275.6 2.8 collective-permute-start.35
  278.4 3.8 %collective-permute-done.44 = bf16[192,384]{1,0:T(8,128)(2,1)S(1)} collective-permute-done((bf16[192,384]{1,0:T(8,128)(2,1)S(1)}, bf16[192,384]{1,0:T(8,128)(2,1)S(1)}, u32[]{:S(2)}, u32[]{:S(2)}) %collective-permute-start.44) | collective-permute-done | bytes 147488 | tf_op jit(solution)/shard_map/ppermute | solution.py:718
  282.3 1.9 collective-permute-done.34
  284.2 2.4 collective-permute-done.35
  286.6 1.8 collective-permute-done.36
  290.2 3.4 %collective-permute-start.50 = (bf16[192,768]{1,0:T(8,128)(2,1)S(1)}, bf16[192,768]{1,0:T(8,128)(2,1)S(1)}, u32[]{:S(2)}, u32[]{:S(2)}) collective-permute-start(bf16[192,768]{1,0:T(8,128)(2,1)S(1)} %get-tuple-element.109), channel_id=1, source_target_pairs={{0,8},{4,12},{8,0},{12,4},{1,9},{5,13},{9,1},{13,5},{2,10},{6,14},... | collective-permute-start | bytes 884744 | tf_op jit(solution)/shard_map/ppermute | solution.py:718
  293.6 1.3 collective-permute-start.51
  294.9 1.6 collective-permute-start.38
  296.8 1.2 collective-permute-start.46
  298.0 2.3 shard_map.228
  302.1 12.8 %collective-permute-done.50 = bf16[192,768]{1,0:T(8,128)(2,1)S(1)} collective-permute-done((bf16[192,768]{1,0:T(8,128)(2,1)S(1)}, bf16[192,768]{1,0:T(8,128)(2,1)S(1)}, u32[]{:S(2)}, u32[]{:S(2)}) %collective-permute-start.50) | collective-permute-done | bytes 294944 | tf_op jit(solution)/shard_map/ppermute | solution.py:718
  314.9 3.6 %collective-permute-done.51 = bf16[192,768]{1,0:T(8,128)(2,1)S(1)} collective-permute-done((bf16[192,768]{1,0:T(8,128)(2,1)S(1)}, bf16[192,768]{1,0:T(8,128)(2,1)S(1)}, u32[]{:S(2)}, u32[]{:S(2)}) %collective-permute-start.51) | collective-permute-done | bytes 294944 | tf_op jit(solution)/shard_map/ppermute | solution.py:718
  319.0 1.4 collective-permute-start.21
  323.1 2.2 collective-permute-done.22
  325.9 3.3 collective-permute-start.53
  (214 shorter events, 37.6 us)
Async XLA Ops:
  0.7 12.9 %copy-start.32 = (f32[768]{0:T(1024)S(1)}, f32[768]{0:T(1024)}, u32[]{:S(2)}) copy-start(f32[768]{0:T(1024)} %param.18) | copy-start | bytes 9220
  0.7 12.9 %copy-start.33 = (f32[768]{0:T(1024)S(1)}, f32[768]{0:T(1024)}, u32[]{:S(2)}) copy-start(f32[768]{0:T(1024)} %param.19) | copy-start | bytes 9220
  0.7 12.9 %copy-start.15 = (f32[5]{0:T(128)S(1)}, f32[5]{0:T(128)}, u32[]{:S(2)}) copy-start(f32[5]{0:T(128)} %dwa_ref.1) | copy-start | bytes 64
  0.7 26.6 %collective-permute-start = (bf16[512,768]{1,0:T(8,128)(2,1)}, bf16[512,768]{1,0:T(8,128)(2,1)}, u32[]{:S(2)}, u32[]{:S(2)}) collective-permute-start(bf16[512,768]{1,0:T(8,128)(2,1)} %bitcast.132), channel_id=1, source_target_pairs={{1,16},{3,18},{5,20},{7,22},{9,24},{11,26},{13,28},{15,30},{16,1},... | collective-permute-start | bytes 2359304 | tf_op jit(solution)/shard_map/ppermute | solution.py:671
  4.5 18.8 %collective-permute-start.2 = (s32[1,3]{1,0:T(1,128)}, s32[1,3]{1,0:T(1,128)S(1)}, u32[]{:S(2)}, u32[]{:S(2)}) collective-permute-start(s32[1,3]{1,0:T(1,128)} %param.16), channel_id=1, source_target_pairs={{0,1},{1,0},{2,3},{3,2},{4,5},{5,4},{6,7},{7,6},{8,9},{9,8},{10,11... | collective-permute-start | bytes 44 | tf_op jit(solution)/shard_map/ppermute | solution.py:679
  5.9 32.8 %collective-permute-start.3 = (bf16[3,384,384]{2,1,0:T(8,128)(2,1)S(1)}, bf16[3,384,384]{2,1,0:T(8,128)(2,1)S(1)}, u32[]{:S(2)}, u32[]{:S(2)}) collective-permute-start(bf16[3,384,384]{2,1,0:T(8,128)(2,1)S(1)} %constant_dynamic-slice_fusion.6), channel_id=1, source_target_pairs={{1,16},{3,18},{5,20},{7,22},{9,24},{11,26},{13,28},{15,30},{16,1},... | collective-permute-start | bytes 2654216 | tf_op jit(solution)/shard_map/ppermute | solution.py:671
  7.9 79.7 %collective-permute-start.8 = (bf16[512,768]{1,0:T(8,128)(2,1)S(1)}, bf16[512,768]{1,0:T(8,128)(2,1)}, u32[]{:S(2)}, u32[]{:S(2)}) collective-permute-start(bf16[512,768]{1,0:T(8,128)(2,1)S(1)} %bitcast.114), channel_id=1, source_target_pairs={{1,16},{3,18},{5,20},{7,22},{9,24},{11,26},{13,28},{15,30},{16,1},... | collective-permute-start | bytes 2359304 | tf_op jit(solution)/shard_map/ppermute | solution.py:671
  11.6 24.0 %collective-permute-start.5 = (bf16[192,768]{1,0:T(8,128)(2,1)S(1)}, bf16[192,768]{1,0:T(8,128)(2,1)}, u32[]{:S(2)}, u32[]{:S(2)}) collective-permute-start(bf16[192,768]{1,0:T(8,128)(2,1)S(1)} %constant_dynamic-slice_fusion.5), channel_id=1, source_target_pairs={{1,16},{3,18},{5,20},{7,22},{9,24},{11,26},{13,28},{15,30},{16,1},... | collective-permute-start | bytes 884744 | tf_op jit(solution)/shard_map/ppermute | solution.py:671
  22.2 30.5 %copy-start.13 = (s32[3]{0:T(128)}, s32[3]{0:T(128)S(1)}, u32[]{:S(2)}) copy-start(s32[3]{0:T(128)S(1)} %pad_add_fusion.flags) | copy-start | bytes 40
  23.3 58.7 %collective-permute-start.10 = (bf16[384,1536]{1,0:T(8,128)(2,1)}, bf16[384,1536]{1,0:T(8,128)(2,1)}, u32[]{:S(2)}, u32[]{:S(2)}) collective-permute-start(bf16[384,1536]{1,0:T(8,128)(2,1)} %constant_dynamic-slice_fusion.4), channel_id=1, source_target_pairs={{1,16},{3,18},{5,20},{7,22},{9,24},{11,26},{13,28},{15,30},{16,1},... | collective-permute-start | bytes 3538952 | tf_op jit(solution)/shard_map/ppermute | solution.py:671
  28.8 20.6 %collective-permute-start.1 = (bf16[512,768]{1,0:T(8,128)(2,1)S(1)}, bf16[512,768]{1,0:T(8,128)(2,1)S(1)}, u32[]{:S(2)}, u32[]{:S(2)}) collective-permute-start(bf16[512,768]{1,0:T(8,128)(2,1)S(1)} %broadcast_select_fusion.4), channel_id=1, source_target_pairs={{0,1},{1,0},{2,3},{3,2},{4,5},{5,4},{6,7},{7,6},{8,9},{9,8},{10,11... | collective-permute-start | bytes 2359304 | tf_op jit(solution)/shard_map/ppermute | solution.py:679
  35.6 7.7 %collective-permute-start.6 = (bf16[192,768]{1,0:T(8,128)(2,1)}, bf16[192,768]{1,0:T(8,128)(2,1)S(1)}, u32[]{:S(2)}, u32[]{:S(2)}) collective-permute-start(bf16[192,768]{1,0:T(8,128)(2,1)} %collective-permute-done.5), channel_id=1, source_target_pairs={{1,3},{3,1},{5,7},{7,5},{9,11},{11,9},{13,15},{15,13},{16,18},{18,... | collective-permute-start | bytes 884744 | tf_op jit(solution)/shard_map/ppermute | solution.py:675
  38.7 14.0 %collective-permute-start.4 = (bf16[3,384,384]{2,1,0:T(8,128)(2,1)S(1)}, bf16[3,384,384]{2,1,0:T(8,128)(2,1)S(1)}, u32[]{:S(2)}, u32[]{:S(2)}) collective-permute-start(bf16[3,384,384]{2,1,0:T(8,128)(2,1)S(1)} %collective-permute-done.3.w_near), channel_id=1, source_target_pairs={{1,3},{3,1},{5,7},{7,5},{9,11},{11,9},{13,15},{15,13},{16,18},{18,... | collective-permute-start | bytes 2654216 | tf_op jit(solution)/shard_map/ppermute | solution.py:675
  43.3 41.9 %collective-permute-start.12 = (bf16[768,768]{1,0:T(8,128)(2,1)}, bf16[768,768]{1,0:T(8,128)(2,1)S(1)}, u32[]{:S(2)}, u32[]{:S(2)}) collective-permute-start(bf16[768,768]{1,0:T(8,128)(2,1)} %constant_dynamic-slice_fusion.3), channel_id=1, source_target_pairs={{1,16},{3,18},{5,20},{7,22},{9,24},{11,26},{13,28},{15,30},{16,1},... | collective-permute-start | bytes 3538952 | tf_op jit(solution)/shard_map/ppermute | solution.py:671
  49.3 31.6 %copy-start.25 = (bf16[384,768]{1,0:T(8,128)(2,1)}, bf16[384,768]{1,0:T(8,128)(2,1)S(1)}, u32[]{:S(2)}) copy-start(bf16[384,768]{1,0:T(8,128)(2,1)S(1)} %fusion.3.w_ref) | copy-start | bytes 1769476
  50.0 12.0 %copy-start = (bf16[1024,768]{1,0:T(8,128)(2,1)}, bf16[1024,768]{1,0:T(8,128)(2,1)S(1)}, u32[]{:S(2)}) copy-start(bf16[1024,768]{1,0:T(8,128)(2,1)S(1)} %maximum_select_fusion.rows_ref) | copy-start | bytes 4718596
  81.9 30.9 %collective-permute-start.7 = (bf16[1024,768]{1,0:T(8,128)(2,1)S(1)}, bf16[1024,768]{1,0:T(8,128)(2,1)S(1)}, u32[]{:S(2)}, u32[]{:S(2)}) collective-permute-start(bf16[1024,768]{1,0:T(8,128)(2,1)S(1)} %convolution_convert_fusion.own_ref), channel_id=1, source_target_pairs={{0,1},{1,0},{2,3},{3,2},{4,5},{5,4},{6,7},{7,6},{8,9},{9,8},{10,11... | collective-permute-start | bytes 4718600 | tf_op jit(solution)/shard_map/ppermute | solution.py:679
  82.0 17.2 %collective-permute-start.11 = (bf16[384,1536]{1,0:T(8,128)(2,1)}, bf16[384,1536]{1,0:T(8,128)(2,1)S(1)}, u32[]{:S(2)}, u32[]{:S(2)}) collective-permute-start(bf16[384,1536]{1,0:T(8,128)(2,1)} %collective-permute-done.10.up_near), channel_id=1, source_target_pairs={{1,3},{3,1},{5,7},{7,5},{9,11},{11,9},{13,15},{15,13},{16,18},{18,... | collective-permute-start | bytes 3538952 | tf_op jit(solution)/shard_map/ppermute | solution.py:675
  85.2 26.6 %collective-permute-start.13 = (bf16[768,768]{1,0:T(8,128)(2,1)S(1)}, bf16[768,768]{1,0:T(8,128)(2,1)S(1)}, u32[]{:S(2)}, u32[]{:S(2)}) collective-permute-start(bf16[768,768]{1,0:T(8,128)(2,1)S(1)} %collective-permute-done.12.down_near), channel_id=1, source_target_pairs={{1,3},{3,1},{5,7},{7,5},{9,11},{11,9},{13,15},{15,13},{16,18},{18,... | collective-permute-start | bytes 3538952 | tf_op jit(solution)/shard_map/ppermute | solution.py:675
  88.8 2.4 collective-permute-start.9
  99.2 12.6 %copy-start.38 = (bf16[384,1536]{1,0:T(8,128)(2,1)}, bf16[384,1536]{1,0:T(8,128)(2,1)S(1)}, u32[]{:S(2)}) copy-start(bf16[384,1536]{1,0:T(8,128)(2,1)S(1)} %collective-permute-done.11.up_far) | copy-start | bytes 3538948
  150.8 7.3 %collective-permute-start.14 = (bf16[1024,768]{1,0:T(8,128)(2,1)}, bf16[1024,768]{1,0:T(8,128)(2,1)}, u32[]{:S(2)}, u32[]{:S(2)}) collective-permute-start(bf16[1024,768]{1,0:T(8,128)(2,1)} %get-tuple-element.48.back_own), channel_id=1, source_target_pairs={{0,1},{1,0},{2,3},{3,2},{4,5},{5,4},{6,7},{7,6},{8,9},{9,8},{10,11... | collective-permute-start | bytes 4718600 | tf_op jit(solution)/shard_map/ppermute | solution.py:679
  150.9 79.2 %collective-permute-start.47 = (bf16[2,768,768]{2,1,0:T(8,128)(2,1)}, bf16[2,768,768]{2,1,0:T(8,128)(2,1)}, u32[]{:S(2)}, u32[]{:S(2)}) collective-permute-start(bf16[2,768,768]{2,1,0:T(8,128)(2,1)} %get-tuple-element.71), channel_id=1, source_target_pairs={{1,16},{3,18},{5,20},{7,22},{9,24},{11,26},{13,28},{15,30},{16,1},... | collective-permute-start | bytes 7077896 | tf_op jit(solution)/shard_map/ppermute | solution.py:671
  156.9 51.6 %collective-permute-start.39 = (bf16[768,768]{1,0:T(8,128)(2,1)}, bf16[768,768]{1,0:T(8,128)(2,1)}, u32[]{:S(2)}, u32[]{:S(2)}) collective-permute-start(bf16[768,768]{1,0:T(8,128)(2,1)} %get-tuple-element.68), channel_id=1, source_target_pairs={{0,2},{1,3},{2,0},{3,1},{4,6},{5,7},{6,4},{7,5},{8,10},{9,11},{10,... | collective-permute-start | bytes 3538952 | tf_op jit(solution)/shard_map/ppermute | solution.py:683
  158.1 12.3 %copy-start.9 = (f32[1024,128]{1,0:T(8,128)S(1)}, f32[1024,128]{1,0:T(8,128)}, u32[]{:S(2)}) copy-start(f32[1024,128]{1,0:T(8,128)} %copy-done.8) | copy-start | bytes 1572868
  158.1 12.3 %copy-start.11 = (f32[1024,128]{1,0:T(8,128)S(1)}, f32[1024,128]{1,0:T(8,128)}, u32[]{:S(2)}) copy-start(f32[1024,128]{1,0:T(8,128)} %copy-done.10) | copy-start | bytes 1572868
  171.6 28.6 %copy-start.20 = (bf16[768,1024]{1,0:T(8,128)(2,1)S(1)}, bf16[768,1024]{1,0:T(8,128)(2,1)}, u32[]{:S(2)}) copy-start(bf16[768,1024]{1,0:T(8,128)(2,1)} %copy-done.19) | copy-start | bytes 4718596
  203.3 12.4 %collective-permute-start.24 = (bf16[768,384]{1,0:T(8,128)(2,1)S(1)}, bf16[768,384]{1,0:T(8,128)(2,1)S(1)}, u32[]{:S(2)}, u32[]{:S(2)}) collective-permute-start(bf16[768,384]{1,0:T(8,128)(2,1)S(1)} %get-tuple-element.105), channel_id=1, source_target_pairs={{0,2},{1,3},{2,0},{3,1},{4,6},{5,7},{6,4},{7,5},{8,10},{9,11},{10,... | collective-permute-start | bytes 1769480 | tf_op jit(solution)/shard_map/ppermute | solution.py:683
  208.3 16.2 %collective-permute-start.15 = (bf16[512,768]{1,0:T(8,128)(2,1)S(1)}, bf16[512,768]{1,0:T(8,128)(2,1)S(1)}, u32[]{:S(2)}, u32[]{:S(2)}) collective-permute-start(bf16[512,768]{1,0:T(8,128)(2,1)S(1)} %get-tuple-element.55), channel_id=1, source_target_pairs={{0,1},{1,0},{2,3},{3,2},{4,5},{5,4},{6,7},{7,6},{8,9},{9,8},{10,11... | collective-permute-start | bytes 2359304 | tf_op jit(solution)/shard_map/ppermute | solution.py:679
  211.2 24.2 %collective-permute-start.40 = (bf16[768,768]{1,0:T(8,128)(2,1)S(1)}, bf16[768,768]{1,0:T(8,128)(2,1)S(1)}, u32[]{:S(2)}, u32[]{:S(2)}) collective-permute-start(bf16[768,768]{1,0:T(8,128)(2,1)S(1)} %add_convert_fusion), channel_id=1, source_target_pairs={{1,16},{3,18},{5,20},{7,22},{9,24},{11,26},{13,28},{15,30},{16,1},... | collective-permute-start | bytes 3538952 | tf_op jit(solution)/shard_map/ppermute | solution.py:671
  215.8 19.3 %collective-permute-start.25 = (bf16[768,384]{1,0:T(8,128)(2,1)S(1)}, bf16[768,384]{1,0:T(8,128)(2,1)S(1)}, u32[]{:S(2)}, u32[]{:S(2)}) collective-permute-start(bf16[768,384]{1,0:T(8,128)(2,1)S(1)} %fusion.2), channel_id=1, source_target_pairs={{1,16},{3,18},{5,20},{7,22},{9,24},{11,26},{13,28},{15,30},{16,1},... | collective-permute-start | bytes 1769480 | tf_op jit(solution)/shard_map/ppermute | solution.py:671
  221.6 26.2 %collective-permute-start.32 = (bf16[2,768,384]{2,1,0:T(8,128)(2,1)S(1)}, bf16[2,768,384]{2,1,0:T(8,128)(2,1)S(1)}, u32[]{:S(2)}, u32[]{:S(2)}) collective-permute-start(bf16[2,768,384]{2,1,0:T(8,128)(2,1)S(1)} %pad_maximum_fusion), channel_id=1, source_target_pairs={{1,16},{3,18},{5,20},{7,22},{9,24},{11,26},{13,28},{15,30},{16,1},... | collective-permute-start | bytes 3538952 | tf_op jit(solution)/shard_map/ppermute | solution.py:671
  226.4 29.8 %collective-permute-start.18 = (bf16[512,768]{1,0:T(8,128)(2,1)S(1)}, bf16[512,768]{1,0:T(8,128)(2,1)S(1)}, u32[]{:S(2)}, u32[]{:S(2)}) collective-permute-start(bf16[512,768]{1,0:T(8,128)(2,1)S(1)} %get-tuple-element.57), channel_id=1, source_target_pairs={{1,16},{3,18},{5,20},{7,22},{9,24},{11,26},{13,28},{15,30},{16,1},... | collective-permute-start | bytes 2359304 | tf_op jit(solution)/shard_map/ppermute | solution.py:671
  230.1 24.7 %collective-permute-start.16 = (bf16[512,768]{1,0:T(8,128)(2,1)S(1)}, bf16[512,768]{1,0:T(8,128)(2,1)S(1)}, u32[]{:S(2)}, u32[]{:S(2)}) collective-permute-start(bf16[512,768]{1,0:T(8,128)(2,1)S(1)} %constant_dynamic-slice_fusion.2), channel_id=1, source_target_pairs={{0,1},{1,0},{2,3},{3,2},{4,5},{5,4},{6,7},{7,6},{8,9},{9,8},{10,11... | collective-permute-start | bytes 2359304 | tf_op jit(solution)/shard_map/ppermute | solution.py:679
  235.3 12.8 %collective-permute-start.26 = (bf16[4,96,384]{2,1,0:T(8,128)(2,1)S(1)}, bf16[4,96,384]{2,1,0:T(8,128)(2,1)S(1)}, u32[]{:S(2)}, u32[]{:S(2)}) collective-permute-start(bf16[4,96,384]{2,1,0:T(8,128)(2,1)S(1)} %constant_dynamic-slice_fusion.1), channel_id=1, source_target_pairs={{0,1},{1,0},{2,3},{3,2},{4,5},{5,4},{6,7},{7,6},{8,9},{9,8},{10,11... | collective-permute-start | bytes 884744 | tf_op jit(solution)/shard_map/ppermute | solution.py:679
  248.2 3.9 %collective-permute-start.27 = (bf16[96,384]{1,0:T(8,128)(2,1)S(1)}, bf16[96,384]{1,0:T(8,128)(2,1)S(1)}, u32[]{:S(2)}, u32[]{:S(2)}) collective-permute-start(bf16[96,384]{1,0:T(8,128)(2,1)S(1)} %get-tuple-element.118), channel_id=1, source_target_pairs={{0,4},{4,8},{8,12},{12,0},{1,5},{5,9},{9,13},{13,1},{2,6},{6,10},{... | collective-permute-start | bytes 221192 | tf_op jit(solution)/shard_map/ppermute | solution.py:718
  249.5 4.2 %collective-permute-start.28 = (bf16[96,384]{1,0:T(8,128)(2,1)S(1)}, bf16[96,384]{1,0:T(8,128)(2,1)S(1)}, u32[]{:S(2)}, u32[]{:S(2)}) collective-permute-start(bf16[96,384]{1,0:T(8,128)(2,1)S(1)} %get-tuple-element.120), channel_id=1, source_target_pairs={{0,8},{4,12},{8,0},{12,4},{1,9},{5,13},{9,1},{13,5},{2,10},{6,14},... | collective-permute-start | bytes 221192 | tf_op jit(solution)/shard_map/ppermute | solution.py:718
  250.6 4.0 %collective-permute-start.29 = (bf16[96,384]{1,0:T(8,128)(2,1)S(1)}, bf16[96,384]{1,0:T(8,128)(2,1)S(1)}, u32[]{:S(2)}, u32[]{:S(2)}) collective-permute-start(bf16[96,384]{1,0:T(8,128)(2,1)S(1)} %get-tuple-element.119), channel_id=1, source_target_pairs={{0,12},{4,0},{8,4},{12,8},{1,13},{5,1},{9,5},{13,9},{2,14},{6,2},{... | collective-permute-start | bytes 221192 | tf_op jit(solution)/shard_map/ppermute | solution.py:718
  252.1 37.6 %collective-permute-start.48 = (bf16[768,768]{1,0:T(8,128)(2,1)S(1)}, bf16[768,768]{1,0:T(8,128)(2,1)S(1)}, u32[]{:S(2)}, u32[]{:S(2)}) collective-permute-start(bf16[768,768]{1,0:T(8,128)(2,1)S(1)} %dynamic-slice_bitcast_fusion), channel_id=1, source_target_pairs={{0,1},{1,0},{2,3},{3,2},{4,5},{5,4},{6,7},{7,6},{8,9},{9,8},{10,11... | collective-permute-start | bytes 3538952 | tf_op jit(solution)/shard_map/ppermute | solution.py:679
  253.8 8.0 %collective-permute-start.41 = (bf16[768,384]{1,0:T(8,128)(2,1)S(1)}, bf16[768,384]{1,0:T(8,128)(2,1)S(1)}, u32[]{:S(2)}, u32[]{:S(2)}) collective-permute-start(bf16[768,384]{1,0:T(8,128)(2,1)S(1)} %constant_dynamic-slice_fusion), channel_id=1, source_target_pairs={{0,1},{1,0},{2,3},{3,2},{4,5},{5,4},{6,7},{7,6},{8,9},{9,8},{10,11... | collective-permute-start | bytes 1769480 | tf_op jit(solution)/shard_map/ppermute | solution.py:679
  254.7 7.9 %collective-permute-start.33 = (bf16[768,384]{1,0:T(8,128)(2,1)S(1)}, bf16[768,384]{1,0:T(8,128)(2,1)S(1)}, u32[]{:S(2)}, u32[]{:S(2)}) collective-permute-start(bf16[768,384]{1,0:T(8,128)(2,1)S(1)} %dynamic-slice_bitcast_fusion.1), channel_id=1, source_target_pairs={{0,1},{1,0},{2,3},{3,2},{4,5},{5,4},{6,7},{7,6},{8,9},{9,8},{10,11... | collective-permute-start | bytes 1769480 | tf_op jit(solution)/shard_map/ppermute | solution.py:679
  254.7 5.9 %collective-permute-start.30 = (bf16[96,384]{1,0:T(8,128)(2,1)S(1)}, bf16[96,384]{1,0:T(8,128)(2,1)S(1)}, u32[]{:S(2)}, u32[]{:S(2)}) collective-permute-start(bf16[96,384]{1,0:T(8,128)(2,1)S(1)} %fusion.16), channel_id=1, source_target_pairs={{0,1},{1,0},{2,3},{3,2},{4,5},{5,4},{6,7},{7,6},{8,9},{9,8},{10,11... | collective-permute-start | bytes 221192 | tf_op jit(solution)/shard_map/ppermute | solution.py:679
  256.2 40.6 %collective-permute-start.17 = (bf16[512,768]{1,0:T(8,128)(2,1)S(1)}, bf16[512,768]{1,0:T(8,128)(2,1)S(1)}, u32[]{:S(2)}, u32[]{:S(2)}) collective-permute-start(bf16[512,768]{1,0:T(8,128)(2,1)S(1)} %add_convert_fusion.1.own_ref), channel_id=1, source_target_pairs={{1,16},{3,18},{5,20},{7,22},{9,24},{11,26},{13,28},{15,30},{16,1},... | collective-permute-start | bytes 2359304 | tf_op jit(solution)/shard_map/ppermute | solution.py:671
  260.7 4.7 %collective-permute-start.31 = (bf16[192,384]{1,0:T(8,128)(2,1)S(1)}, bf16[192,384]{1,0:T(8,128)(2,1)S(1)}, u32[]{:S(2)}, u32[]{:S(2)}) collective-permute-start(bf16[192,384]{1,0:T(8,128)(2,1)S(1)} %maximum_select_fusion.10), channel_id=1, source_target_pairs={{0,2},{1,3},{2,0},{3,1},{4,6},{5,7},{6,4},{7,5},{8,10},{9,11},{10,... | collective-permute-start | bytes 442376 | tf_op jit(solution)/shard_map/ppermute | solution.py:683
  262.0 10.2 %collective-permute-start.42 = (bf16[192,384]{1,0:T(8,128)(2,1)S(1)}, bf16[192,384]{1,0:T(8,128)(2,1)S(1)}, u32[]{:S(2)}, u32[]{:S(2)}) collective-permute-start(bf16[192,384]{1,0:T(8,128)(2,1)S(1)} %get-tuple-element.110), channel_id=1, source_target_pairs={{0,4},{4,8},{8,12},{12,0},{1,5},{5,9},{9,13},{13,1},{2,6},{6,10},{... | collective-permute-start | bytes 442376 | tf_op jit(solution)/shard_map/ppermute | solution.py:718
  262.6 12.9 %collective-permute-start.43 = (bf16[192,384]{1,0:T(8,128)(2,1)S(1)}, bf16[192,384]{1,0:T(8,128)(2,1)S(1)}, u32[]{:S(2)}, u32[]{:S(2)}) collective-permute-start(bf16[192,384]{1,0:T(8,128)(2,1)S(1)} %get-tuple-element.112), channel_id=1, source_target_pairs={{0,8},{4,12},{8,0},{12,4},{1,9},{5,13},{9,1},{13,5},{2,10},{6,14},... | collective-permute-start | bytes 442376 | tf_op jit(solution)/shard_map/ppermute | solution.py:718
  265.4 16.8 %collective-permute-start.44 = (bf16[192,384]{1,0:T(8,128)(2,1)S(1)}, bf16[192,384]{1,0:T(8,128)(2,1)S(1)}, u32[]{:S(2)}, u32[]{:S(2)}) collective-permute-start(bf16[192,384]{1,0:T(8,128)(2,1)S(1)} %get-tuple-element.111), channel_id=1, source_target_pairs={{0,12},{4,0},{8,4},{12,8},{1,13},{5,1},{9,5},{13,9},{2,14},{6,2},{... | collective-permute-start | bytes 442376 | tf_op jit(solution)/shard_map/ppermute | solution.py:718
  272.2 12.0 %collective-permute-start.34 = (bf16[192,384]{1,0:T(8,128)(2,1)S(1)}, bf16[192,384]{1,0:T(8,128)(2,1)S(1)}, u32[]{:S(2)}, u32[]{:S(2)}) collective-permute-start(bf16[192,384]{1,0:T(8,128)(2,1)S(1)} %get-tuple-element.113), channel_id=1, source_target_pairs={{0,4},{4,8},{8,12},{12,0},{1,5},{5,9},{9,13},{13,1},{2,6},{6,10},{... | collective-permute-start | bytes 442376 | tf_op jit(solution)/shard_map/ppermute | solution.py:718
  275.6 11.1 %collective-permute-start.35 = (bf16[192,384]{1,0:T(8,128)(2,1)S(1)}, bf16[192,384]{1,0:T(8,128)(2,1)S(1)}, u32[]{:S(2)}, u32[]{:S(2)}) collective-permute-start(bf16[192,384]{1,0:T(8,128)(2,1)S(1)} %get-tuple-element.115), channel_id=1, source_target_pairs={{0,8},{4,12},{8,0},{12,4},{1,9},{5,13},{9,1},{13,5},{2,10},{6,14},... | collective-permute-start | bytes 442376 | tf_op jit(solution)/shard_map/ppermute | solution.py:718
  282.2 6.2 %collective-permute-start.36 = (bf16[192,384]{1,0:T(8,128)(2,1)S(1)}, bf16[192,384]{1,0:T(8,128)(2,1)S(1)}, u32[]{:S(2)}, u32[]{:S(2)}) collective-permute-start(bf16[192,384]{1,0:T(8,128)(2,1)S(1)} %get-tuple-element.114), channel_id=1, source_target_pairs={{0,12},{4,0},{8,4},{12,8},{1,13},{5,1},{9,5},{13,9},{2,14},{6,2},{... | collective-permute-start | bytes 442376 | tf_op jit(solution)/shard_map/ppermute | solution.py:718
  284.2 10.7 %collective-permute-start.45 = (bf16[192,384]{1,0:T(8,128)(2,1)S(1)}, bf16[192,384]{1,0:T(8,128)(2,1)S(1)}, u32[]{:S(2)}, u32[]{:S(2)}) collective-permute-start(bf16[192,384]{1,0:T(8,128)(2,1)S(1)} %fusion.10), channel_id=1, source_target_pairs={{0,1},{1,0},{2,3},{3,2},{4,5},{5,4},{6,7},{7,6},{8,9},{9,8},{10,11... | collective-permute-start | bytes 442376 | tf_op jit(solution)/shard_map/ppermute | solution.py:679
  288.5 5.1 %collective-permute-start.37 = (bf16[192,384]{1,0:T(8,128)(2,1)S(1)}, bf16[192,384]{1,0:T(8,128)(2,1)S(1)}, u32[]{:S(2)}, u32[]{:S(2)}) collective-permute-start(bf16[192,384]{1,0:T(8,128)(2,1)S(1)} %fusion.13), channel_id=1, source_target_pairs={{0,2},{1,3},{2,0},{3,1},{4,6},{5,7},{6,4},{7,5},{8,10},{9,11},{10,... | collective-permute-start | bytes 442376 | tf_op jit(solution)/shard_map/ppermute | solution.py:683
  290.1 11.9 %collective-permute-start.49 = (bf16[192,768]{1,0:T(8,128)(2,1)S(1)}, bf16[192,768]{1,0:T(8,128)(2,1)S(1)}, u32[]{:S(2)}, u32[]{:S(2)}) collective-permute-start(bf16[192,768]{1,0:T(8,128)(2,1)S(1)} %get-tuple-element.107), channel_id=1, source_target_pairs={{0,4},{4,8},{8,12},{12,0},{1,5},{5,9},{9,13},{13,1},{2,6},{6,10},{... | collective-permute-start | bytes 884744 | tf_op jit(solution)/shard_map/ppermute | solution.py:718
  290.2 24.7 %collective-permute-start.50 = (bf16[192,768]{1,0:T(8,128)(2,1)S(1)}, bf16[192,768]{1,0:T(8,128)(2,1)S(1)}, u32[]{:S(2)}, u32[]{:S(2)}) collective-permute-start(bf16[192,768]{1,0:T(8,128)(2,1)S(1)} %get-tuple-element.109), channel_id=1, source_target_pairs={{0,8},{4,12},{8,0},{12,4},{1,9},{5,13},{9,1},{13,5},{2,10},{6,14},... | collective-permute-start | bytes 884744 | tf_op jit(solution)/shard_map/ppermute | solution.py:718
  293.6 24.8 %collective-permute-start.51 = (bf16[192,768]{1,0:T(8,128)(2,1)S(1)}, bf16[192,768]{1,0:T(8,128)(2,1)S(1)}, u32[]{:S(2)}, u32[]{:S(2)}) collective-permute-start(bf16[192,768]{1,0:T(8,128)(2,1)S(1)} %get-tuple-element.108), channel_id=1, source_target_pairs={{0,12},{4,0},{8,4},{12,8},{1,13},{5,1},{9,5},{13,9},{2,14},{6,2},{... | collective-permute-start | bytes 884744 | tf_op jit(solution)/shard_map/ppermute | solution.py:718
  294.9 5.4 %collective-permute-start.38 = (bf16[192,384]{1,0:T(8,128)(2,1)S(1)}, bf16[192,384]{1,0:T(8,128)(2,1)S(1)}, u32[]{:S(2)}, u32[]{:S(2)}) collective-permute-start(bf16[192,384]{1,0:T(8,128)(2,1)S(1)} %add_convert_fusion.5), channel_id=1, source_target_pairs={{0,1},{1,0},{2,3},{3,2},{4,5},{5,4},{6,7},{7,6},{8,9},{9,8},{10,11... | collective-permute-start | bytes 442376 | tf_op jit(solution)/shard_map/ppermute | solution.py:679
  296.8 32.4 %collective-permute-start.46 = (bf16[192,768]{1,0:T(8,128)(2,1)S(1)}, bf16[192,768]{1,0:T(8,128)(2,1)S(1)}, u32[]{:S(2)}, u32[]{:S(2)}) collective-permute-start(bf16[192,768]{1,0:T(8,128)(2,1)S(1)} %maximum_select_fusion.8), channel_id=1, source_target_pairs={{0,2},{1,3},{2,0},{3,1},{4,6},{5,7},{6,4},{7,5},{8,10},{9,11},{10,... | collective-permute-start | bytes 884744 | tf_op jit(solution)/shard_map/ppermute | solution.py:683
  300.3 1.3 collective-permute-start.19
  301.7 17.3 %collective-permute-start.20 = (f32[9,768]{1,0:T(8,128)S(1)}, f32[9,768]{1,0:T(8,128)S(1)}, u32[]{:S(2)}, u32[]{:S(2)}) collective-permute-start(f32[9,768]{1,0:T(8,128)S(1)} %fusion.23), channel_id=1, source_target_pairs={{0,2},{1,3},{2,0},{3,1},{4,6},{5,7},{6,4},{7,5},{8,10},{9,11},{10,... | collective-permute-start | bytes 82952 | tf_op jit(solution)/shard_map/ppermute | solution.py:727
  318.6 7.2 %collective-permute-start.52 = (bf16[192,768]{1,0:T(8,128)(2,1)S(1)}, bf16[192,768]{1,0:T(8,128)(2,1)S(1)}, u32[]{:S(2)}, u32[]{:S(2)}) collective-permute-start(bf16[192,768]{1,0:T(8,128)(2,1)S(1)} %fusion.6), channel_id=1, source_target_pairs={{0,2},{1,3},{2,0},{3,1},{4,6},{5,7},{6,4},{7,5},{8,10},{9,11},{10,... | collective-permute-start | bytes 884744 | tf_op jit(solution)/shard_map/ppermute | solution.py:683
  319.0 3.0 collective-permute-start.21
  322.0 3.3 collective-permute-start.22
  325.3 5.1 %collective-permute-start.23 = (f32[9,768]{1,0:T(8,128)S(1)}, f32[9,768]{1,0:T(8,128)S(1)}, u32[]{:S(2)}, u32[]{:S(2)}) collective-permute-start(f32[9,768]{1,0:T(8,128)S(1)} %add.220), channel_id=1, source_target_pairs={{0,8},{4,12},{8,0},{12,4},{1,9},{5,13},{9,1},{13,5},{2,10},{6,14},... | collective-permute-start | bytes 82952 | tf_op jit(solution)/shard_map/ppermute | solution.py:727
  325.9 5.8 %collective-permute-start.53 = (bf16[192,768]{1,0:T(8,128)(2,1)S(1)}, bf16[192,768]{1,0:T(8,128)(2,1)S(1)}, u32[]{:S(2)}, u32[]{:S(2)}) collective-permute-start(bf16[192,768]{1,0:T(8,128)(2,1)S(1)} %add_convert_fusion.3), channel_id=1, source_target_pairs={{0,1},{1,0},{2,3},{3,2},{4,5},{5,4},{6,7},{7,6},{8,9},{9,8},{10,11... | collective-permute-start | bytes 884744 | tf_op jit(solution)/shard_map/ppermute | solution.py:679
  (30 other events, 163.7 us)

commit v2 on v1

--- a/solution.py
+++ b/solution.py
@@ -72,21 +72,28 @@
     each_block(whole, reach, body)
 
 
-def attend(start_column, queries, keys, values, reach):
-    whole, width = queries.shape
-    block = pl.BlockSpec((whole, LANES), lambda p: (0, p))
-    return pl.pallas_call(
-        functools.partial(attend_kernel, reach),
-        grid=(width // LANES,),
-        in_specs=[pl.BlockSpec((whole, LANES), lambda p: (0, 0)), block, block, block],
-        out_specs=block,
+def attend(pair, start_column, projected, so_far, reach):
+    count, whole, width = projected.shape
+
+    def block(c):
+        return pl.BlockSpec((None, whole, LANES), lambda i: (c, 0, pair))
+
+    begun = [] if so_far is None else [so_far]
+    kernel = attend_kernel if so_far is None else lambda reach, unused, *refs: attend_kernel(reach, *refs)
+    return pl.pallas_call(
+        functools.partial(kernel, reach),
+        grid=(1,),
+        in_specs=[pl.BlockSpec(memory_space=pl.ANY)] * len(begun)
+        + [pl.BlockSpec((whole, LANES), lambda i: (0, 0)), block(0), block(1), block(2)],
+        out_specs=pl.BlockSpec((whole, LANES), lambda i: (0, pair)),
         out_shape=jax.ShapeDtypeStruct((whole, width), jnp.bfloat16),
         scratch_shapes=[pltpu.VMEM((BLOCK, LANES), jnp.float32)],
+        input_output_aliases={0: 0} if begun else {},
         compiler_params=pltpu.CompilerParams(vmem_limit_bytes=40 << 20),
         cost_estimate=pl.CostEstimate(
-            flops=4 * whole * width * 640, transcendentals=whole * 640 * 6, bytes_accessed=8 * whole * width
-        ),
-    )(start_column, queries, keys, values)
+            flops=4 * whole * LANES * 640, transcendentals=whole * 640 * 2, bytes_accessed=8 * whole * LANES
+        ),
+    )(*begun, start_column, projected, projected, projected)
 
 
 def turn_back(field, cos, sin):
@@ -97,7 +104,7 @@
 
 
 def attend_back_kernel(
-    reach, start_ref, cos_ref, sin_ref, q_ref, k_ref, v_ref, g_ref, dq_ref, dk_ref, dv_ref,
+    reach, start_ref, cos_ref, sin_ref, q_ref, k_ref, v_ref, g_ref, out_ref,
     key_acc, value_acc, query_acc,
 ):
     whole = q_ref.shape[0]
@@ -134,39 +141,54 @@
         @pl.when(head == 1)
         def _():
             both = jnp.where(lane == 0, query_acc[...], here) * (HEAD_DIM**-0.5)
-            dq_ref[at, :] = turn_back(both, cos_ref[at, :], sin_ref[at, :]).astype(dq_ref.dtype)
+            out_ref[0, at, :] = turn_back(both, cos_ref[at, :], sin_ref[at, :]).astype(out_ref.dtype)
 
     each_block(whole, reach, body)
 
     def finish(i, carry):
         at = pl.ds(pl.multiple_of(i * BLOCK, BLOCK), BLOCK)
-        dk_ref[at, :] = turn_back(key_acc[at, :], cos_ref[at, :], sin_ref[at, :]).astype(dk_ref.dtype)
-        dv_ref[at, :] = value_acc[at, :].astype(dv_ref.dtype)
+        out_ref[1, at, :] = turn_back(key_acc[at, :], cos_ref[at, :], sin_ref[at, :]).astype(out_ref.dtype)
+        out_ref[2, at, :] = value_acc[at, :].astype(out_ref.dtype)
         return carry
 
     lax.fori_loop(0, whole // BLOCK, finish, 0)
 
 
-def attend_back(start_row, cos, sin, queries, keys, values, grad_mixed, reach):
-    whole, width = queries.shape
-    block = pl.BlockSpec((whole, LANES), lambda p: (0, p))
-    table = pl.BlockSpec((whole, LANES), lambda p: (0, 0))
-    return pl.pallas_call(
-        functools.partial(attend_back_kernel, reach),
-        grid=(width // LANES,),
-        in_specs=[pl.BlockSpec((8, whole), lambda p: (0, 0)), table, table, block, block, block, block],
-        out_specs=[block] * 3,
-        out_shape=[jax.ShapeDtypeStruct((whole, width), jnp.bfloat16)] * 3,
+def attend_back(pair, start_row, cos, sin, projected, grad_mixed, so_far, reach):
+    count, whole, width = projected.shape
+
+    def block(c):
+        return pl.BlockSpec((None, whole, LANES), lambda i: (c, 0, pair))
+
+    table = pl.BlockSpec((whole, LANES), lambda i: (0, 0))
+    begun = [] if so_far is None else [so_far]
+    kernel = attend_back_kernel if so_far is None else lambda reach, unused, *refs: attend_back_kernel(reach, *refs)
+    return pl.pallas_call(
+        functools.partial(kernel, reach),
+        grid=(1,),
+        in_specs=[pl.BlockSpec(memory_space=pl.ANY)] * len(begun)
+        + [
+            pl.BlockSpec((8, whole), lambda i: (0, 0)),
+            table,
+            table,
+            block(0),
+            block(1),
+            block(2),
+            pl.BlockSpec((whole, LANES), lambda i: (0, pair)),
+        ],
+        out_specs=pl.BlockSpec((count, whole, LANES), lambda i: (0, 0, pair)),
+        out_shape=jax.ShapeDtypeStruct((count, whole, width), jnp.bfloat16),
         scratch_shapes=[
             pltpu.VMEM((whole, LANES), jnp.float32),
             pltpu.VMEM((whole, LANES), jnp.float32),
             pltpu.VMEM((BLOCK, LANES), jnp.float32),
         ],
+        input_output_aliases={0: 0} if begun else {},
         compiler_params=pltpu.CompilerParams(vmem_limit_bytes=40 << 20),
         cost_estimate=pl.CostEstimate(
-            flops=10 * whole * width * 640, transcendentals=whole * 640 * 6, bytes_accessed=14 * whole * width
-        ),
-    )(start_row, cos, sin, queries, keys, values, grad_mixed)
+            flops=10 * whole * LANES * 640, transcendentals=whole * 640 * 2, bytes_accessed=14 * whole * LANES
+        ),
+    )(*begun, start_row, cos, sin, projected, projected, projected, grad_mixed)
 
 
 ROWS = 256
@@ -192,13 +214,6 @@
 
 def whole_spec(shape):
     return pl.BlockSpec(shape, lambda *at: (0,) * len(shape))
-
-
-def join_rows(flags, own, near, far, out):
-    half = near.shape[0]
-    for index, got in ((flags[2], near), (1 - flags[2], far)):
-        at = pl.ds(pl.multiple_of(index * half, half), half)
-        out[at, :] = jnp.where(flags[0] == 1, own[at, :], got[...])
 
 
 def turn(field, cos, sin):
@@ -209,7 +224,7 @@
 
 
 def project_kernel(
-    flags, rows_ref, gain_ref, shift_ref, cos_ref, sin_ref, w_own, w_near, w_far, out_ref, turned_ref,
+    flags, rows_ref, gain_ref, shift_ref, cos_ref, sin_ref, w_own, w_got, out_ref, turned_ref,
     weight_ref, norm_ref,
 ):
     whole = rows_ref.shape[0]
@@ -225,7 +240,7 @@
 
         row_blocks(whole, body)
 
-    join_rows(flags, w_own.at[0], w_near.at[0], w_far.at[0], weight_ref.at[0])
+    weight_ref[0] = jnp.where(flags[0] == 1, w_own[0], w_got[0])
 
     def body(i, at):
         field = dot(norm_ref[at, :], weight_ref[0])
@@ -245,11 +260,10 @@
     row_blocks(whole, body)
 
 
-def project(flags, rows, gain, shift, cos, sin, w_own, w_near, w_far):
+def project(flags, rows, gain, shift, cos, sin, w_own, w_got):
     whole, width = rows.shape
     count, unused, columns = w_own.shape
     weight = pl.BlockSpec((1, width, columns), lambda c, flags: (c, 0, 0))
-    part = pl.BlockSpec((1, width // 2, columns), lambda c, flags: (c, 0, 0))
     return pl.pallas_call(
         project_kernel,
         grid_spec=pltpu.PrefetchScalarGridSpec(
@@ -262,8 +276,7 @@
                 whole_spec((whole, LANES)),
                 whole_spec((whole, LANES)),
                 weight,
-                part,
-                part,
+                weight,
             ],
             out_specs=[
                 pl.BlockSpec((1, whole, columns), lambda c, flags: (c, 0, 0)),
@@ -283,7 +296,7 @@
             transcendentals=0,
             bytes_accessed=12 * whole * width,
         ),
-    )(flags, rows, gain, shift, cos, sin, w_own, w_near, w_far)
+    )(flags, rows, gain, shift, cos, sin, w_own, w_got)
 
 
 HIDDEN = 256
@@ -298,136 +311,167 @@
     return up * half, slope
 
 
-def feed_kernel(
-    flags, weight_ref, rows_ref, own_ref, got_ref, cot_ref, gain_ref, shift_ref, up_own, up_near,
-    up_far, down_own, down_near, down_far, down_ref, back_ref, keep_ref, send_ref, gdown_ref, norm, norm_t, grad, grad_t, act, slope, up_w, down_w,
-):
-    whole, width = rows_ref.shape
+def feed_kernel(early, flags, *refs):
+    if early:
+        weight_ref, rows_ref, own_ref, got_ref, cot_ref, gain_ref, shift_ref = refs[:7]
+        refs = refs[7:]
+        up_own, up_got, down_own, down_got, norm, norm_t, grad, grad_t = refs[:8]
+    else:
+        norm, norm_t, grad, grad_t, back_early, up_own, up_got, down_own, down_got = refs[:9]
+    back_ref, act_ref, gup_ref, gdown_ref, slope, up_w = refs[-6:]
+    whole, width = norm.shape
     step = pl.program_id(0)
-    last = pl.num_programs(0) - 1
-
-    @pl.when(step == 0)
+
+    if early:
+
+        @pl.when(step == 0)
+        def _():
+            def body(i, at):
+                unit, unused = norm_parts(wide(rows_ref, at) + wide(own_ref, at) + wide(got_ref, at))
+                field = unit * gain_ref[...] + shift_ref[...]
+                norm[at, :] = field.astype(jnp.bfloat16)
+                norm_t[:, at] = field.T.astype(jnp.bfloat16)
+                field = wide(cot_ref, at) * weight_ref[0]
+                grad[at, :] = field.astype(jnp.bfloat16)
+                grad_t[:, at] = field.T.astype(jnp.bfloat16)
+
+            row_blocks(whole, body)
+
+    hidden = pl.ds(pl.multiple_of(step * HIDDEN, HIDDEN), HIDDEN)
+    up_w[:, hidden] = jnp.where(flags[0] == 1, up_own[...], up_got[...])
+    up_block = up_w[:, hidden]
+    down_block = jnp.where(flags[0] == 1, down_own[...], down_got[...])
+
+    def body(i, at):
+        value, rise = gelu_both(dot(norm[at, :], up_block))
+        act_ref[at, :] = value.astype(jnp.bfloat16)
+        slope[at, hidden] = (dot(grad[at, :], down_block, NT) * rise).astype(jnp.bfloat16)
+
+    row_blocks(whole, body)
+
+    def grads(i, at):
+        gdown_ref[at, :] = dot(grad_t[at, :], act_ref[...]).astype(jnp.bfloat16)
+        gup_ref[at, :] = dot(norm_t[at, :], slope[:, hidden]).astype(jnp.bfloat16)
+
+    row_blocks(width, grads)
+
+    @pl.when(step == pl.num_programs(0) - 1)
     def _():
         def body(i, at):
-            unit, unused = norm_parts(wide(rows_ref, at) + wide(own_ref, at) + wide(got_ref, at))
-            field = unit * gain_ref[...] + shift_ref[...]
-            norm[at, :] = field.astype(jnp.bfloat16)
-            norm_t[:, at] = field.T.astype(jnp.bfloat16)
-            field = wide(cot_ref, at) * weight_ref[0]
-            grad[at, :] = field.astype(jnp.bfloat16)
-            grad_t[:, at] = field.T.astype(jnp.bfloat16)
+            back = dot(slope[at, :], up_w[...], NT)
+            if not early:
+                back = back + back_early[at, :]
+            back_ref[at, :] = back.astype(back_ref.dtype)
 
         row_blocks(whole, body)
 
-    hidden = pl.ds(pl.multiple_of(step * HIDDEN, HIDDEN), HIDDEN)
-    first = step < pl.num_programs(0) // 2
-    join_rows(flags, up_own, up_near, up_far, up_w.at[:, hidden])
-    down_w[hidden, :] = jnp.where(
-        flags[0] == 1, down_own[...], jnp.where(first, down_near[...], down_far[...])
-    )
-    up_block = up_w[:, hidden]
-    down_block = down_w[hidden, :]
-
-    def body(i, at):
-        value, rise = gelu_both(dot(norm[at, :], up_block))
-        act[at, hidden] = value.astype(jnp.bfloat16)
-        slope[at, hidden] = (dot(grad[at, :], down_block, NT) * rise).astype(jnp.bfloat16)
-
-    row_blocks(whole, body)
-
-    def grads(i, at):
-        gdown_ref[0, at, :] = dot(grad_t[at, :], act[:, hidden]).astype(jnp.bfloat16)
-        grad_up = dot(norm_t[at, :], slope[:, hidden]).astype(jnp.bfloat16)
-
-        @pl.when(first)
-        def _():
-            keep_ref[at, :] = grad_up
-
-        @pl.when(jnp.logical_not(first))
-        def _():
-            send_ref[at, :] = grad_up
-
-    row_blocks(width, grads)
-
-    @pl.when(step == last)
-    def _():
-        def body(i, at):
-            back_ref[at, :] = dot(slope[at, :], up_w[...], NT).astype(jnp.bfloat16)
-            down_ref[at, :] = dot(act[at, :], down_w[...]).astype(jnp.bfloat16)
-
-        row_blocks(whole, body)
-
-
-def feed(flags, weight, rows, own, got, cot, gain, shift, up_own, up_near, up_far, down_own, down_near, down_far):
-    whole, width = rows.shape
-    hidden = up_own.shape[1]
+
+def feed(early, flags, head, up_own, up_got, down_own, down_got):
+    whole, width = head[1].shape if early else head[0].shape
+    hidden = up_got.shape[1]
     steps = hidden // HIDDEN
-    half = steps // 2
     tokens = whole_spec((whole, width))
+    turned = whole_spec((width, whole))
     vector = whole_spec((1, width))
 
     def at(j, flags):
-        return lax.rem(flags[2] * half + j, steps)
-
-    def early(j):
-        return jnp.minimum(j, half - 1)
-
-    def late(j):
-        return jnp.maximum(j - half, 0)
-
-    up_spec = pl.BlockSpec((width, HIDDEN), lambda j, flags: (0, at(j, flags)))
-    up_part = pl.BlockSpec((width // 2, HIDDEN), lambda j, flags: (0, at(j, flags)))
-    down_spec = pl.BlockSpec((HIDDEN, width), lambda j, flags: (at(j, flags), 0))
-    piece = pl.BlockSpec(
-        (1, width, HIDDEN), lambda j, flags: (at(j, flags) // half, 0, lax.rem(at(j, flags), half))
-    )
-    wide_bf16 = jax.ShapeDtypeStruct((whole, width), jnp.bfloat16)
-    part = jax.ShapeDtypeStruct((width, hidden // 2), jnp.bfloat16)
-    pieces = jax.ShapeDtypeStruct((2, width, hidden // 2), jnp.bfloat16)
-    return pl.pallas_call(
-        feed_kernel,
+        return ((1 - flags[2]) if early else flags[2]) * steps + j
+
+    low = jax.ShapeDtypeStruct((whole, width), jnp.bfloat16)
+    low_turned = jax.ShapeDtypeStruct((width, whole), jnp.bfloat16)
+    full = jax.ShapeDtypeStruct((whole, width), jnp.float32)
+    piece = jax.ShapeDtypeStruct((width, hidden), jnp.bfloat16)
+    if early:
+        head_specs = [pl.BlockSpec(memory_space=pltpu.SMEM)] + [tokens] * 4 + [vector] * 2
+    else:
+        head_specs = [tokens, turned, tokens, turned, tokens]
+    block = pl.BlockSpec((width, HIDDEN), lambda j, flags: (0, j))
+    return pl.pallas_call(
+        functools.partial(feed_kernel, early),
         grid_spec=pltpu.PrefetchScalarGridSpec(
             num_scalar_prefetch=1,
             grid=(steps,),
+            in_specs=head_specs
+            + [
+                pl.BlockSpec((width, HIDDEN), lambda j, flags: (0, at(j, flags))),
+                block,
+                pl.BlockSpec((HIDDEN, width), lambda j, flags: (at(j, flags), 0)),
+                pl.BlockSpec((HIDDEN, width), lambda j, flags: (j, 0)),
+            ],
+            out_specs=([tokens, turned, tokens, turned] if early else [])
+            + [tokens, pl.BlockSpec((whole, HIDDEN), lambda j, flags: (0, j)), block, block],
+            scratch_shapes=[
+                pltpu.VMEM((whole, hidden), jnp.bfloat16),
+                pltpu.VMEM((width, hidden), jnp.bfloat16),
+            ],
+        ),
+        out_shape=([low, low_turned, low, low_turned, full] if early else [low])
+        + [jax.ShapeDtypeStruct((whole, hidden), jnp.bfloat16), piece, piece],
+        compiler_params=pltpu.CompilerParams(vmem_limit_bytes=56 << 20),
+        cost_estimate=pl.CostEstimate(
+            flops=10 * whole * width * hidden,
+            transcendentals=whole * hidden,
+            bytes_accessed=24 * whole * width,
+        ),
+    )(flags, *head, up_own, up_got, down_own, down_got)
+
+
+def lower_kernel(flags, act_early, act_late, own_early, got_early, own_late, got_late, rows_ref, own_ref, got_ref, keep_ref, send_ref):
+    half = keep_ref.shape[0]
+    same = flags[0] == 1
+    first = jnp.where(same, own_early[...], got_early[...])
+    second = jnp.where(same, own_late[...], got_late[...])
+
+    def at_rows(near, i):
+        return pl.ds(pl.multiple_of(near * half + i * ROWS, ROWS), ROWS)
+
+    def send(i, at):
+        here = at_rows(1 - flags[1], i)
+        total = dot(act_early[here, :], first) + dot(act_late[here, :], second)
+        send_ref[at, :] = total.astype(jnp.bfloat16)
+
+    def keep(i, at):
+        here = at_rows(flags[1], i)
+        total = dot(act_early[here, :], first) + dot(act_late[here, :], second)
+        keep_ref[at, :] = total + wide(rows_ref, here) + wide(own_ref, here) + wide(got_ref, here)
+
+    row_blocks(half, send)
+    row_blocks(half, keep)
+
+
+def lower(flags, act_early, act_late, down_own, got_early, got_late, rows, own, got):
+    whole, hidden = act_early.shape
+    width = rows.shape[1]
+    tokens = whole_spec((whole, width))
+    half = whole_spec((whole // 2, width))
+    piece = whole_spec((hidden, width))
+    return pl.pallas_call(
+        lower_kernel,
+        grid_spec=pltpu.PrefetchScalarGridSpec(
+            num_scalar_prefetch=1,
+            grid=(1,),
             in_specs=[
-                pl.BlockSpec(memory_space=pltpu.SMEM),
+                whole_spec((whole, hidden)),
+                whole_spec((whole, hidden)),
+                pl.BlockSpec((hidden, width), lambda i, flags: (1 - flags[2], 0)),
+                piece,
+                pl.BlockSpec((hidden, width), lambda i, flags: (flags[2], 0)),
+                piece,
                 tokens,
                 tokens,
                 tokens,
-                tokens,
-                vector,
-                vector,
-                up_spec,
-                up_part,
-                up_part,
-                down_spec,
-                pl.BlockSpec((HIDDEN, width), lambda j, flags: (early(j), 0)),
-                pl.BlockSpec((HIDDEN, width), lambda j, flags: (late(j), 0)),
             ],
-            out_specs=[
-                tokens,
-                tokens,
-                pl.BlockSpec((width, HIDDEN), lambda j, flags: (0, early(j))),
-                pl.BlockSpec((width, HIDDEN), lambda j, flags: (0, late(j))),
-                piece,
-            ],
-            scratch_shapes=[
-                pltpu.VMEM((whole, width), jnp.bfloat16),
-                pltpu.VMEM((width, whole), jnp.bfloat16),
-                pltpu.VMEM((whole, width), jnp.bfloat16),
-                pltpu.VMEM((width, whole), jnp.bfloat16),
-                pltpu.VMEM((whole, hidden), jnp.bfloat16),
-                pltpu.VMEM((whole, hidden), jnp.bfloat16),
-                pltpu.VMEM((width, hidden), jnp.bfloat16),
-                pltpu.VMEM((hidden, width), jnp.bfloat16),
-            ],
-        ),
-        out_shape=[wide_bf16, wide_bf16, part, part, pieces],
+            out_specs=[half, half],
+        ),
+        out_shape=[
+            jax.ShapeDtypeStruct((whole // 2, width), jnp.float32),
+            jax.ShapeDtypeStruct((whole // 2, width), jnp.bfloat16),
+        ],
         compiler_params=pltpu.CompilerParams(vmem_limit_bytes=56 << 20),
         cost_estimate=pl.CostEstimate(
-            flops=12 * whole * width * hidden, transcendentals=whole * hidden, bytes_accessed=32 * whole * width
-        ),
-    )(flags, weight, rows, own, got, cot, gain, shift, up_own, up_near, up_far, down_own, down_near, down_far)
+            flops=4 * whole * width * hidden, transcendentals=0, bytes_accessed=18 * whole * width
+        ),
+    )(flags, act_early, act_late, down_own, got_early, down_own, got_late, rows, own, got)
 
 
 def middle_kernel(
@@ -494,17 +538,17 @@
     )(flags, weight, rows, own, got, cot, back_own, back_got, gain, mixed, w_out)
 
 
-def weigh_kernel(turned_ref, gq_ref, gk_ref, gv_ref, out_ref):
+def weigh_kernel(turned_ref, grad_ref, out_ref):
     def grads(i, at):
-        for c, ref in enumerate((gq_ref, gk_ref, gv_ref)):
-            out_ref[c, at, :] = dot(turned_ref[at, :], ref[...]).astype(jnp.bfloat16)
+        for c in range(grad_ref.shape[0]):
+            out_ref[c, at, :] = dot(turned_ref[at, :], grad_ref[c]).astype(jnp.bfloat16)
 
     row_blocks(turned_ref.shape[0], grads)
 
 
-def weigh(turned, gq, gk, gv):
+def weigh(turned, grad):
     width, whole = turned.shape
-    columns = gq.shape[1]
+    columns = grad.shape[2]
     return pl.pallas_call(
         weigh_kernel,
         out_shape=jax.ShapeDtypeStruct((3, width, columns), jnp.bfloat16),
@@ -512,18 +556,18 @@
         cost_estimate=pl.CostEstimate(
             flops=6 * whole * width * columns, transcendentals=0, bytes_accessed=6 * whole * width
         ),
-    )(turned, gq, gk, gv)
-
-
-def unproject_kernel(flags, gq_ref, gk_ref, gv_ref, weight, keep_ref, send_ref):
+    )(turned, grad)
+
+
+def unproject_kernel(flags, grad_ref, weight, keep_ref, send_ref):
     half = keep_ref.shape[0]
 
     def side(near, out_ref):
         def body(i, at):
             from_rows = pl.ds(pl.multiple_of(near * half + i * ROWS, ROWS), ROWS)
-            total = dot(gq_ref[from_rows, :], weight[0], NT)
-            total = total + dot(gk_ref[from_rows, :], weight[1], NT)
-            total = total + dot(gv_ref[from_rows, :], weight[2], NT)
+            total = dot(grad_ref[0, from_rows, :], weight[0], NT)
+            for c in range(1, grad_ref.shape[0]):
+                total = total + dot(grad_ref[c, from_rows, :], weight[c], NT)
             out_ref[at, :] = total.astype(out_ref.dtype)
 
         row_blocks(half, body)
@@ -532,17 +576,16 @@
     side(flags[1], keep_ref)
 
 
-def unproject(flags, gq, gk, gv, weight):
-    whole, columns = gq.shape
+def unproject(flags, grad, weight):
+    count, whole, columns = grad.shape
     width = weight.shape[1]
-    narrow = whole_spec((whole, columns))
     half = whole_spec((whole // 2, width))
     return pl.pallas_call(
         unproject_kernel,
         grid_spec=pltpu.PrefetchScalarGridSpec(
             num_scalar_prefetch=1,
             grid=(1,),
-            in_specs=[narrow, narrow, narrow, whole_spec((3, width, columns))],
+            in_specs=[whole_spec(grad.shape), whole_spec((count, width, columns))],
             out_specs=[half, half],
         ),
         out_shape=[
@@ -553,7 +596,7 @@
         cost_estimate=pl.CostEstimate(
             flops=6 * whole * width * columns, transcendentals=0, bytes_accessed=8 * whole * width
         ),
-    )(flags, gq, gk, gv, weight)
+    )(flags, grad, weight)
 
 
 def first_norm_kernel(flags, rows_ref, keep_ref, got_ref, resid_ref, gain_ref, out_ref, sums_ref):
@@ -755,15 +798,11 @@
 
     dps = lax.axis_size("dp")
     input_got = swap_diagonal(layer_input[0])
-    qkv_near = swap_diagonal(part_of(w_qkv, far, 1))
-    out_near = swap_diagonal(part_of(w_out, far, 0))
-    up_near = swap_diagonal(part_of(w_up, far, 0))
-    cot_got = swap_diagonal(cotangent[0])
-    down_near = swap_diagonal(part_of(w_down, far, 0))
-    qkv_far = swap_far_crossing(qkv_near)
-    out_far = swap_far_crossing(out_near)
-    up_far = swap_far_crossing(up_near)
-    down_far = swap_far_crossing(down_near)
+    qkv_got = swap_diagonal(w_qkv)
+    up_early = swap_diagonal(after(part_of(w_up, 1 - far, 1), input_got))
+    down_early = swap_diagonal(after(part_of(w_down, 1 - far, 0), qkv_got))
+    out_got = swap_diagonal(after(w_out, qkv_got))
+    cot_got = swap_diagonal(after(cotangent[0], qkv_got))
 
     own_lengths = jnp.where(same, lengths, swap_near(lengths))[0]
     seq_owner, token_place = positions(own_lengths, whole)
@@ -785,34 +824,35 @@
     gain_two, bias_two = gain_two[None], bias_two[None]
 
     projected, norm_one_t, weight_qkv = project(
-        flags, layer_rows, gain_one, bias_one, cos_table, sin_table, w_qkv, qkv_near, qkv_far
-    )
-    queries, keys, values = projected[0], projected[1], projected[2]
-    mixed = attend(start_column, queries, keys, values, LONGEST)
-    weight_out = jnp.where(same, w_out, ordered(out_near, out_far, far == 0))
+        flags, layer_rows, gain_one, bias_one, cos_table, sin_table, w_qkv, qkv_got
+    )
+    pairs = projected.shape[2] // LANES
+    mixed = attend(0, start_column, projected, None, LONGEST)
+    for pair in range(1, pairs):
+        if pair == 1:
+            up_late = swap_far_crossing(after(up_early, mixed))
+        mixed = attend(pair, start_column, projected, mixed, LONGEST)
+    down_late = swap_far_crossing(after(down_early, mixed))
+    weight_out = jnp.where(same, w_out, after(out_got, mixed))
     attn = jnp.dot(mixed, weight_out, preferred_element_type=jnp.float32).astype(jnp.bfloat16)
     attn_got = swap_near(attn)
     cot_half = jnp.where(same, cotangent[0], after(cot_got, mixed))
     cot_rows = ordered(cot_half, swap_near(cot_half), near == 0)
-    down, back, up_keep, up_send, grad_down = feed(
-        flags,
-        own_weight,
-        layer_rows,
-        attn,
-        attn_got,
-        cot_rows,
-        gain_two,
-        bias_two,
-        w_up,
-        up_near,
-        up_far,
-        w_down,
-        down_near,
-        down_far,
+    head = (own_weight, layer_rows, attn, attn_got, cot_rows, gain_two, bias_two)
+    *kept, act_early, up_send, down_first = feed(
+        True, flags, head, w_up, up_early, w_down, down_early
+    )
+    up_got = swap_far(up_send)
+    first_got = swap_diagonal(down_first)
+    back, act_late, up_keep, down_second = feed(
+        False, flags, kept, w_up, up_late, w_down, down_late
     )
     back_got = swap_near(back)
-    up_got = swap_far(up_send)
-    down_got = swap_diagonal(grad_down)
+    second_got = swap_diagonal(down_second)
+    block_keep, block_send = lower(
+        flags, act_early, act_late, w_down, down_early, down_late, layer_rows, attn, attn_got
+    )
+    block_got = swap_near(block_send)
     grad_attn, grad_mixed, grad_out, sums_two = middle(
         flags,
         own_weight,
@@ -820,15 +860,12 @@
         attn,
         attn_got,
         cot_rows,
-        back,
+        after(back, block_send),
         back_got,
         gain_two,
         mixed,
         weight_out,
     )
-    grad_queries, grad_keys, grad_values = attend_back(
-        start_row, cos_table, sin_table, queries, keys, values, grad_mixed, LONGEST
-    )
 
     def columns_of(pieces):
         return pieces.transpose(1, 0, 2).reshape(pieces.shape[1], -1)
@@ -836,58 +873,67 @@
     def by_dp(block):
         return block.reshape(dps, block.shape[0] // dps, block.shape[1])
 
-    up_pair = add(up_keep, after(up_got, grad_keys))
+    grad_qkv = attend_back(0, start_row, cos_table, sin_table, projected, grad_mixed, None, LONGEST)
+    up_pair = add(up_keep, after(up_got, grad_qkv))
     up_moved = swap_diagonal(up_pair)
-    down_pair = jnp.where(same, grad_down, after(down_got, grad_keys))
-    down_other = swap_near(take(down_pair, 1 - near))
-    grad_qkv = weigh(norm_one_t, grad_queries, grad_keys, grad_values)
-    mine = take(grad_qkv, far)
-    attn_got_far = swap_far(take(grad_qkv, 1 - far))
-    late_pieces = jnp.stack([grad_qkv[2], grad_out])
+    first_sum = jnp.where(same, down_first, after(first_got, grad_qkv))
+    second_sum = jnp.where(same, down_second, after(second_got, grad_qkv))
+    down_keep = jnp.where(near == far, second_sum, first_sum)
+    down_other = swap_near(jnp.where(near == far, first_sum, second_sum))
+    block_half = add(block_keep, after(block_got, grad_qkv))
+    block_moved = swap_diagonal(block_half)
+    grad_qkv = after(grad_qkv, up_pair, down_keep, block_half)
+    for pair in range(1, pairs):
+        grad_qkv = attend_back(
+            pair, start_row, cos_table, sin_table, projected, grad_mixed, grad_qkv, LONGEST
+        )
+        if pair == 1:
+            down_one = add(down_keep, after(down_other, grad_qkv))
+            down_blocks = move_rows(by_dp(down_one))
+            up_pair = jnp.where(same, up_pair, after(up_moved, grad_qkv))
+            up_other = swap_near(part_of(up_pair, 1 - near, 1))
+            grad_qkv = after(grad_qkv, down_one, up_pair)
+    up_one = add(part_of(up_pair, near, 1), after(up_other, grad_qkv))
+    up_blocks = move_rows(by_dp(up_one))
+    grad_weights = weigh(norm_one_t, grad_qkv)
+    mine = take(grad_weights, far)
+    key_got = swap_far(take(grad_weights, 1 - far))
+    late_pieces = jnp.stack([grad_weights[2], grad_out])
     late_got = swap_diagonal(late_pieces)
-    keep, send = unproject(flags, grad_queries, grad_keys, grad_values, weight_qkv)
+    keep, send = unproject(flags, after(grad_qkv, grad_weights), weight_qkv)
     send_got = swap_near(send)
-    down_one = add(take(down_pair, near), after(down_other, grad_qkv))
-    down_blocks = move_rows(by_dp(down_one))
+    output, sums_now = present(
+        flags, own_weight, past_sum, cotangent[0], block_half, after(block_moved, send)
+    )
     input_grad, sums_one = first_norm_back(flags, layer_rows, keep, send_got, grad_attn, gain_one)
     grad_input = swap_diagonal(input_grad)
-    up_pair = jnp.where(same, up_pair, after(up_moved, grad_qkv))
-    up_one = add(part_of(up_pair, near, 1), swap_near(part_of(up_pair, 1 - near, 1)))
-    up_blocks = move_rows(by_dp(up_one))
-
-    def half_of(field, index):
-        return lax.dynamic_slice_in_dim(field, index * rows, rows, 0)
-
-    down_half = after(half_of(down, 1 - near), input_grad)
-    block_half = add(
-        *[half_of(field, near) for field in (layer_rows, attn, attn_got, down)], swap_near(down_half)
-    )
-    output, sums_now = present(
-        flags, own_weight, past_sum, cotangent[0], block_half, swap_diagonal(block_half)
-    )
+    down_sum = add(*[after(block, input_grad) for block in down_blocks])
+    down_far = swap_far(down_sum)
     small = jnp.concatenate(
         [sums_one[:2], sums_two[:2], sums_past[:hist_count], sums_now[:1]], axis=0
     )
     small = sum_everywhere(small)
 
-    key_pair = add(mine, attn_got_far)
-    key_pair = by_dp(jnp.where(same, key_pair, swap_diagonal(key_pair)))
+    key_pair = add(mine, after(key_got, input_grad))
+    key_moved = swap_diagonal(key_pair)
+    late_pair = jnp.where(same, late_pieces, after(late_got, key_pair))
+    late_one = add(take(late_pair, near), swap_near(take(late_pair, 1 - near)))
+    late_blocks = move_rows(by_dp(late_one))
+    key_pair = by_dp(jnp.where(same, key_pair, key_moved))
     key_one = add(part_of(key_pair, near, 1), swap_near(part_of(key_pair, 1 - near, 1)))
-    late_pair = jnp.where(same, late_pieces, late_got)
-    late_one = add(take(late_pair, near), swap_near(take(late_pair, 1 - near)))
-    late_sum = add(*move_rows(by_dp(late_one)))
-    key_sum = add(*move_rows(key_one))
+    key_blocks = move_rows(key_one)
+    up_sum = add(*[after(block, key_one) for block in up_blocks])
+    up_half = ordered(up_sum, swap_near(up_sum), near == 0, axis=1)
+    up_far = swap_far(up_half)
+    down_sum = add(down_sum, down_far)
+    grad_w_down = ordered(down_sum[None], swap_near(down_sum)[None], near == 0)
+    late_sum = add(*late_blocks)
     late_sum = add(late_sum, swap_far(late_sum))
     grad_value_out = ordered(late_sum[None], swap_near(late_sum)[None], near == 0)
+    key_sum = add(*key_blocks)
     key_half = ordered(key_sum, swap_near(key_sum), near == 0)
     grad_query_key = ordered(key_half[None], swap_far(key_half)[None], far == 0)
-
-    down_sum = add(*down_blocks)
-    down_sum = add(down_sum, swap_far(down_sum))
-    grad_w_down = ordered(down_sum[None], swap_near(down_sum)[None], near == 0)
-    up_sum = add(*up_blocks)
-    up_half = ordered(up_sum, swap_near(up_sum), near == 0, axis=1)
-    grad_w_up = ordered(up_half[None], swap_far(up_half)[None], far == 0)
+    grad_w_up = ordered(up_half[None], up_far[None], far == 0)
     grad_w_qkv = jnp.concatenate([grad_query_key, grad_value_out[:1]], axis=0)
 
     return (

time: 338 us -> 331 us (0.979)
  Pallas kernels: 118 us -> 135 us
  starting transfers between devices: 86.2 us -> 71.9 us
  waiting for transfers between devices: 85.9 us -> 71.9 us
    ppermute x4 -> x2, waiting for transfers between devices: 21.7 us -> 0.01 us  [swap_far_crossing(): return lax.ppermute(field, AXES, crossing(lambda t, d, r: (t, d, r ^ 2)))]
    pallas_call x3 -> x9, Pallas kernels: 82.5 us -> 97.9 us  [the longest x2 42.5 us: feed(): pl.pallas_call(functools.partial(feed_kernel, early), grid_spec=pltpu.Pre...]
    ppermute x5, waiting for transfers between devices: 4.01 us -> 15 us  [sum_everywhere(): lax.ppermute(field, name, [(d, d ^ bit) for d in range(size)])]
    ppermute x12, waiting for transfers between devices: 35.2 us -> 25.8 us  [move_rows(): lax.ppermute(sent, 'dp', [(d, (d + step) % dps) for d in range(dps)])]
    ppermute x12, starting transfers between devices: 18.3 us -> 11.4 us  [move_rows(): lax.ppermute(sent, 'dp', [(d, (d + step) % dps) for d in range(dps)])]
    ppermute x4 -> x2, starting transfers between devices: 10.7 us -> 5.27 us  [swap_far_crossing(): return lax.ppermute(field, AXES, crossing(lambda t, d, r: (t, d, r ^ 2)))]
    ppermute x12 -> x13, waiting for transfers between devices: 22.3 us -> 25.4 us  [swap_diagonal(): lax.ppermute(field, AXES, crossing(lambda t, d, r: (r % 2, d, r - r % 2 +...]
    unnamed x80 -> x88, local copies, waits for them, and re-layouts: 10.1 us -> 12.6 us
  transfers between devices with their start and end apart: 54 -> 53, of which waited for: 24 -> 20; matrix products, arithmetic and copies ran while one was open for 9% -> 9% of each run, Pallas kernels for 24% -> 36%
where the time goes in v2:
time: 331 us; the launch traced here: 325 us
  Pallas kernels  135 us (41%)
  starting transfers between devices  71.9 us (22%)
  waiting for transfers between devices  71.9 us (22%)
  local copies, waits for them, and re-layouts  24.9 us (8%)
  other arithmetic  18 us (5%)
    ppermute x13, starting transfers between devices, swap_diagonal(): lax.ppermute(field, AXES, crossing(lambda t, d, r: (r % 2, d, r - r % 2 +...  42.6 us
    pallas_call x2, Pallas kernels, feed(): pl.pallas_call(functools.partial(feed_kernel, early), grid_spec=pltpu.Pre...  42.5 us
    pallas_call x3, Pallas kernels, attend_back(): pl.pallas_call(functools.partial(kernel, reach), grid=(1,), in_specs=[pl....  28.4 us
    ppermute x12, waiting for transfers between devices, move_rows(): lax.ppermute(sent, 'dp', [(d, (d + step) % dps) for d in range(dps)])  25.8 us
    ppermute x13, waiting for transfers between devices, swap_diagonal(): lax.ppermute(field, AXES, crossing(lambda t, d, r: (r % 2, d, r - r % 2 +...  25.4 us
    pallas_call x3, Pallas kernels, attend(): pl.pallas_call(functools.partial(kernel, reach), grid=(1,), in_specs=[pl....  17.1 us
    ppermute x5, waiting for transfers between devices, sum_everywhere(): lax.ppermute(field, name, [(d, d ^ bit) for d in range(size)])  15 us
    unnamed x88, local copies, waits for them, and re-layouts  12.6 us
  transfers between devices with their start and end apart: 53, of which 20 were waited for; matrix products, arithmetic and copies ran while one was open for 9% of the time, Pallas kernels for 36%

profile of v2, /device:TPU:9, one launch (start us, length us, event | category | flops | bytes accessed | tf_op | source)
XLA Modules:
  0.0 325.0 jit_solution(11327478601420410741)
XLA Ops:
  0.6 3.7 %collective-permute-start.3 = (bf16[3,768,384]{2,1,0:T(8,128)(2,1)}, bf16[3,768,384]{2,1,0:T(8,128)(2,1)S(1)}, u32[]{:S(2)}, u32[]{:S(2)}) collective-permute-start(bf16[3,768,384]{2,1,0:T(8,128)(2,1)} %w_own.1), channel_id=1, source_target_pairs={{1,16},{3,18},{5,20},{7,22},{9,24},{11,26},{13,28},{15,30},{16,1},... | collective-permute-start | bytes 5308424 | tf_op jit(solution)/shard_map/ppermute | solution.py:714
  4.4 1.9 collective-permute-start
  9.0 1.9 copy-done.11
  11.5 3.0 shard_map.220
  15.7 1.5 copy-done.28
  18.6 14.6 %collective-permute-done = bf16[512,768]{1,0:T(8,128)(2,1)S(1)} collective-permute-done((bf16[512,768]{1,0:T(8,128)(2,1)}, bf16[512,768]{1,0:T(8,128)(2,1)S(1)}, u32[]{:S(2)}, u32[]{:S(2)}) %collective-permute-start) | collective-permute-done | bytes 786464 | tf_op jit(solution)/shard_map/ppermute | solution.py:714
  34.1 3.6 %collective-permute-start.8 = (bf16[768,768]{1,0:T(8,128)(2,1)}, bf16[768,768]{1,0:T(8,128)(2,1)}, u32[]{:S(2)}, u32[]{:S(2)}) collective-permute-start(bf16[768,768]{1,0:T(8,128)(2,1)} %constant_dynamic-slice_fusion.3), channel_id=1, source_target_pairs={{1,16},{3,18},{5,20},{7,22},{9,24},{11,26},{13,28},{15,30},{16,1},... | collective-permute-start | bytes 3538952 | tf_op jit(solution)/shard_map/ppermute | solution.py:714
  37.7 1.5 broadcast_select_fusion.7
  39.4 1.9 collective-permute-start.4
  41.3 1.9 fusion.2
  44.8 3.8 %collective-permute-start.6 = (bf16[512,768]{1,0:T(8,128)(2,1)S(1)}, bf16[512,768]{1,0:T(8,128)(2,1)S(1)}, u32[]{:S(2)}, u32[]{:S(2)}) collective-permute-start(bf16[512,768]{1,0:T(8,128)(2,1)S(1)} %bitcast.102), channel_id=1, source_target_pairs={{1,16},{3,18},{5,20},{7,22},{9,24},{11,26},{13,28},{15,30},{16,1},... | collective-permute-start | bytes 2359304 | tf_op jit(solution)/shard_map/ppermute | solution.py:714
  48.5 2.4 collective-permute-start.9
  51.1 1.5 copy-done.23
  52.5 9.4 %shard_map.221 = (bf16[3,1024,384]{2,1,0:T(8,128)(2,1)S(1)}, bf16[768,1024]{1,0:T(8,128)(2,1)S(1)}, bf16[3,768,384]{2,1,0:T(8,128)(2,1)S(1)}) custom-call(s32[3]{0:T(128)S(1)} %pad_add_fusion.flags, bf16[1024,768]{1,0:T(8,128)(2,1)S(1)} %maximum_select_fusion.rows_ref.refs_1_, f32[1,768]{1,0:T(1,128)S(1)} %broadcast_in_dim.73.gain_ref, ...), custom_call_target="tpu_custom_call" | custom-call | flops 1811939328 | bytes 9437184 | tf_op jit(solution)/shard_map/pallas_call | solution.py:267
  62.0 5.7 %shard_map.222.unused = bf16[1024,384]{1,0:T(8,128)(2,1)S(1)} custom-call(s32[1024,128]{1,0:T(8,128)S(1)} %broadcast_in_dim.71.start_ref.refs_0_, bf16[3,1024,384]{2,1,0:T(8,128)(2,1)S(1)} %get-tuple-element.75.q_ref.k_ref.v_ref.refs_1_.refs_2_.refs_3_.refs_4_.refs_5_, ...), custom_call_target="tpu_custom_call" | custom-call | flops 335544320 | bytes 1048576 | tf_op jit(solution)/shard_map/pallas_call | solution.py:83
  67.7 5.7 %shard_map.223.unused = bf16[1024,384]{1,0:T(8,128)(2,1)S(1)} custom-call(bf16[1024,384]{1,0:T(8,128)(2,1)S(1)} %shard_map.222.unused, s32[1024,128]{1,0:T(8,128)S(1)} %broadcast_in_dim.71.start_ref.refs_0_, bf16[3,1024,384]{2,1,0:T(8,128)(2,1)S(1)} %get-tuple-element.75.q_ref.k_ref.v_ref.refs_1_.refs_2_.refs_3_.refs_4_.refs_5_, ...), custom_call_target="tpu_custom_call", output_to_operand_aliasing={{}: (0, {})} | custom-call | flops 335544320 | bytes 1048576 | tf_op jit(solution)/shard_map/pallas_call | solution.py:83
  73.5 5.7 %shard_map.224.mixed_ref = bf16[1024,384]{1,0:T(8,128)(2,1)S(1)} custom-call(bf16[1024,384]{1,0:T(8,128)(2,1)S(1)} %shard_map.223.unused, s32[1024,128]{1,0:T(8,128)S(1)} %broadcast_in_dim.71.start_ref.refs_0_, bf16[3,1024,384]{2,1,0:T(8,128)(2,1)S(1)} %get-tuple-element.75.q_ref.k_ref.v_ref.refs_1_.refs_2_.refs_3_.refs_4_.refs_5_, ...), custom_call_target="tpu_custom_call", output_to_operand_aliasing={{}: (0, {})} | custom-call | flops 335544320 | bytes 1048576 | tf_op jit(solution)/shard_map/pallas_call | solution.py:83
  82.0 3.1 collective-permute-start.10
  85.2 2.2 collective-permute-start.11
  89.1 1.8 maximum_select_fusion.1.refs_4_.cot_ref
  92.1 23.5 %shard_map.225 = (bf16[1024,768]{1,0:T(8,128)(2,1)}, bf16[768,1024]{1,0:T(8,128)(2,1)}, bf16[1024,768]{1,0:T(8,128)(2,1)}, bf16[768,1024]{1,0:T(8,128)(2,1)}, f3...) custom-call(s32[3]{0:T(128)} %copy-done.17, ...), custom_call_target="tpu_custom_call" | custom-call | flops 6039797760 | bytes 18874368 | tf_op jit(solution)/shard_map/pallas_call | solution.py:389
  115.6 19.0 %shard_map.226 = (bf16[1024,768]{1,0:T(8,128)(2,1)}, bf16[1024,768]{1,0:T(8,128)(2,1)}, bf16[768,768]{1,0:T(8,128)(2,1)}, bf16[768,768]{1,0:T(8,128)(2,1)}) custom-call(s32[3]{0:T(128)} %copy-done.17, bf16[1024,768]{1,0:T(8,128)(2,1)} %get-tuple-element.83.refs_0_, bf16[768,1024]{1,0:T(8,128)(2,1)} %get-tuple-element.84.refs_1_, ...), custom_call_target="tpu_custom_call" | custom-call | flops 6039797760 | bytes 18874368 | tf_op jit(solution)/shard_map/pallas_call | solution.py:389
  134.6 4.2 %collective-permute-start.17 = (bf16[768,768]{1,0:T(8,128)(2,1)}, bf16[768,768]{1,0:T(8,128)(2,1)}, u32[]{:S(2)}, u32[]{:S(2)}) collective-permute-start(bf16[768,768]{1,0:T(8,128)(2,1)} %get-tuple-element.102), channel_id=1, source_target_pairs={{1,16},{3,18},{5,20},{7,22},{9,24},{11,26},{13,28},{15,30},{16,1},... | collective-permute-start | bytes 3538952 | tf_op jit(solution)/shard_map/ppermute | solution.py:714
  138.8 2.1 collective-permute-start.16
  142.2 9.9 %shard_map.227 = (f32[512,768]{1,0:T(8,128)}, bf16[512,768]{1,0:T(8,128)(2,1)}) custom-call(s32[3]{0:T(128)} %copy-done.17, bf16[1024,768]{1,0:T(8,128)(2,1)} %get-tuple-element.82.act_early, bf16[1024,768]{1,0:T(8,128)(2,1)} %get-tuple-element.90.act_late, bf16[1536,768]{1,0:T(8,128)(2,1)} %own_late.1, bf16[768,768]{1,0:T(8,128)(2,1)} %copy-done.35, ...), custom_call_target="tpu_custom_call" | custom-call | flops 2415919104 | bytes 14155776 | tf_op jit(solution)/shard_map/pallas_call | solution.py:448
  152.2 12.3 %shard_map.228 = (bf16[1024,768]{1,0:T(8,128)(2,1)}, bf16[1024,384]{1,0:T(8,128)(2,1)}, bf16[768,384]{1,0:T(8,128)(2,1)}, f32[8,768]{1,0:T(8,128)}) custom-call(s32[3]{0:T(128)} %copy-done.17, f32[1]{0:T(128)} %slice.39.refs_0_.weight_ref, bf16[1024,768]{1,0:T(8,128)(2,1)} %copy-done, bf16[1024,768]{1,0:T(8,128)(2,1)} %copy-done.29, ...), custom_call_target="tpu_custom_call" | custom-call | flops 1207959552 | bytes 14155776 | tf_op jit(solution)/shard_map/pallas_call | solution.py:517
  165.6 9.5 %shard_map.229.unused = bf16[3,1024,384]{2,1,0:T(8,128)(2,1)S(1)} custom-call(s32[8,1024]{1,0:T(8,128)S(1)} %broadcast_in_dim.72.start_ref.refs_0_, f32[1024,128]{1,0:T(8,128)S(1)} %copy-done.6, f32[1024,128]{1,0:T(8,128)S(1)} %copy-done.4, bf16[3,1024,384]{2,1,0:T(8,128)(2,1)S(1)} %get-tuple-element.75.q_ref.k_ref.v_ref.refs_1_.refs_2_.refs_3_.refs_4_.refs_5_, ...), custom_call_target="tpu_custom_call" | custom-call | flops 838860800 | bytes 1835008 | tf_op jit(solution)/shard_map/pallas_call | solution.py:166
  175.2 1.6 add_convert_fusion.1
  176.8 4.1 %collective-permute-start.19 = (bf16[768,768]{1,0:T(8,128)(2,1)S(1)}, bf16[768,768]{1,0:T(8,128)(2,1)S(1)}, u32[]{:S(2)}, u32[]{:S(2)}) collective-permute-start(bf16[768,768]{1,0:T(8,128)(2,1)S(1)} %add_convert_fusion.1), channel_id=1, source_target_pairs={{1,16},{3,18},{5,20},{7,22},{9,24},{11,26},{13,28},{15,30},{16,1},... | collective-permute-start | bytes 3538952 | tf_op jit(solution)/shard_map/ppermute | solution.py:714
  180.9 1.9 broadcast_select_fusion.4
  183.1 2.1 collective-permute-start.14
  185.2 9.5 %shard_map.230.unused = bf16[3,1024,384]{2,1,0:T(8,128)(2,1)S(1)} custom-call(bf16[3,1024,384]{2,1,0:T(8,128)(2,1)S(1)} %shard_map.229.unused, s32[8,1024]{1,0:T(8,128)S(1)} %broadcast_in_dim.72.start_ref.refs_0_, f32[1024,128]{1,0:T(8,128)S(1)} %copy-done.6, f32[1024,128]{1,0:T(8,128)S(1)} %copy-done.4, ...), custom_call_target="tpu_custom_call", output_to_operand_aliasing={{}: (0, {})} | custom-call | flops 838860800 | bytes 1835008 | tf_op jit(solution)/shard_map/pallas_call | solution.py:166
  197.2 9.5 %shard_map.231.grad_ref = bf16[3,1024,384]{2,1,0:T(8,128)(2,1)S(1)} custom-call(bf16[3,1024,384]{2,1,0:T(8,128)(2,1)S(1)} %shard_map.230.unused, s32[8,1024]{1,0:T(8,128)S(1)} %broadcast_in_dim.72.start_ref.refs_0_, f32[1024,128]{1,0:T(8,128)S(1)} %copy-done.6, f32[1024,128]{1,0:T(8,128)S(1)} %copy-done.4, ...), custom_call_target="tpu_custom_call", output_to_operand_aliasing={{}: (0, {})} | custom-call | flops 838860800 | bytes 1835008 | tf_op jit(solution)/shard_map/pallas_call | solution.py:166
  206.7 2.9 shard_map.232
  209.7 3.8 %shard_map.233 = (f32[512,768]{1,0:T(8,128)S(1)}, bf16[512,768]{1,0:T(8,128)(2,1)}) custom-call(s32[3]{0:T(128)S(1)} %copy-done.18, bf16[3,1024,384]{2,1,0:T(8,128)(2,1)S(1)} %shard_map.231.grad_ref, bf16[3,768,384]{2,1,0:T(8,128)(2,1)S(1)} %copy-done.25), custom_call_target="tpu_custom_call" | custom-call | flops 1811939328 | bytes 6291456 | tf_op jit(solution)/shard_map/pallas_call | solution.py:583
  215.4 1.5 dynamic-slice_bitcast_fusion.5
  216.9 1.3 collective-permute-start.48
  219.3 1.4 collective-permute-start.50
  222.0 1.4 collective-permute-start.42
  223.3 2.8 shard_map.234
  226.2 3.0 shard_map.235
  232.3 1.6 collective-permute-done.23
  233.8 4.7 %collective-permute-start.35 = (bf16[2,768,384]{2,1,0:T(8,128)(2,1)S(1)}, bf16[2,768,384]{2,1,0:T(8,128)(2,1)S(1)}, u32[]{:S(2)}, u32[]{:S(2)}) collective-permute-start(bf16[2,768,384]{2,1,0:T(8,128)(2,1)S(1)} %pad_maximum_fusion), channel_id=1, source_target_pairs={{1,16},{3,18},{5,20},{7,22},{9,24},{11,26},{13,28},{15,30},{16,1},... | collective-permute-start | bytes 3538952 | tf_op jit(solution)/shard_map/ppermute | solution.py:714
  238.9 4.1 %collective-permute-done.49 = bf16[192,768]{1,0:T(8,128)(2,1)S(1)} collective-permute-done((bf16[192,768]{1,0:T(8,128)(2,1)S(1)}, bf16[192,768]{1,0:T(8,128)(2,1)S(1)}, u32[]{:S(2)}, u32[]{:S(2)}) %collective-permute-start.49) | collective-permute-done | bytes 294944 | tf_op jit(solution)/shard_map/ppermute | solution.py:761
  243.3 2.4 collective-permute-done.50
  246.5 6.3 %collective-permute-done.24 = f32[9,768]{1,0:T(8,128)S(1)} collective-permute-done((f32[9,768]{1,0:T(8,128)S(1)}, f32[9,768]{1,0:T(8,128)S(1)}, u32[]{:S(2)}, u32[]{:S(2)}) %collective-permute-start.24) | collective-permute-done | bytes 27680 | tf_op jit(solution)/shard_map/ppermute | solution.py:770
  254.1 2.7 collective-permute-done.25
  257.0 3.6 %collective-permute-done.26 = f32[9,768]{1,0:T(8,128)S(1)} collective-permute-done((f32[9,768]{1,0:T(8,128)S(1)}, f32[9,768]{1,0:T(8,128)S(1)}, u32[]{:S(2)}, u32[]{:S(2)}) %collective-permute-start.26) | collective-permute-done | bytes 27680 | tf_op jit(solution)/shard_map/ppermute | solution.py:770
  260.6 2.4 collective-permute-start.45
  264.3 6.1 %collective-permute-start.28 = (bf16[768,384]{1,0:T(8,128)(2,1)S(1)}, bf16[768,384]{1,0:T(8,128)(2,1)S(1)}, u32[]{:S(2)}, u32[]{:S(2)}) collective-permute-start(bf16[768,384]{1,0:T(8,128)(2,1)S(1)} %fusion.1), channel_id=1, source_target_pairs={{1,16},{3,18},{5,20},{7,22},{9,24},{11,26},{13,28},{15,30},{16,1},... | collective-permute-start | bytes 1769480 | tf_op jit(solution)/shard_map/ppermute | solution.py:714
  270.5 1.9 collective-permute-start.21
  272.7 5.3 %collective-permute-done.28 = bf16[768,384]{1,0:T(8,128)(2,1)S(1)} collective-permute-done((bf16[768,384]{1,0:T(8,128)(2,1)S(1)}, bf16[768,384]{1,0:T(8,128)(2,1)S(1)}, u32[]{:S(2)}, u32[]{:S(2)}) %collective-permute-start.28) | collective-permute-done | bytes 589856 | tf_op jit(solution)/shard_map/ppermute | solution.py:714
  278.1 1.5 collective-permute-done.52
  281.0 5.4 %collective-permute-done.21 = bf16[512,768]{1,0:T(8,128)(2,1)S(1)} collective-permute-done((bf16[512,768]{1,0:T(8,128)(2,1)S(1)}, bf16[512,768]{1,0:T(8,128)(2,1)S(1)}, u32[]{:S(2)}, u32[]{:S(2)}) %collective-permute-start.21) | collective-permute-done | bytes 786464 | tf_op jit(solution)/shard_map/ppermute | solution.py:714
  287.6 1.8 collective-permute-start.31
  290.8 1.8 collective-permute-done.31
  292.6 4.2 %collective-permute-done.32 = bf16[96,384]{1,0:T(8,128)(2,1)S(1)} collective-permute-done((bf16[96,384]{1,0:T(8,128)(2,1)S(1)}, bf16[96,384]{1,0:T(8,128)(2,1)S(1)}, u32[]{:S(2)}, u32[]{:S(2)}) %collective-permute-start.32) | collective-permute-done | bytes 73760 | tf_op jit(solution)/shard_map/ppermute | solution.py:761
  297.8 1.8 collective-permute-start.38
  300.3 2.9 collective-permute-done.37
  303.2 7.5 %collective-permute-done.38 = bf16[192,384]{1,0:T(8,128)(2,1)S(1)} collective-permute-done((bf16[192,384]{1,0:T(8,128)(2,1)S(1)}, bf16[192,384]{1,0:T(8,128)(2,1)S(1)}, u32[]{:S(2)}, u32[]{:S(2)}) %collective-permute-start.38) | collective-permute-done | bytes 147488 | tf_op jit(solution)/shard_map/ppermute | solution.py:761
  310.7 2.7 collective-permute-done.39
  313.6 1.5 collective-permute-start.34
  315.1 3.4 %collective-permute-done.40 = bf16[192,384]{1,0:T(8,128)(2,1)S(1)} collective-permute-done((bf16[192,384]{1,0:T(8,128)(2,1)S(1)}, bf16[192,384]{1,0:T(8,128)(2,1)S(1)}, u32[]{:S(2)}, u32[]{:S(2)}) %collective-permute-start.40) | collective-permute-done | bytes 147488 | tf_op jit(solution)/shard_map/ppermute | solution.py:726
  318.5 2.3 collective-permute-start.41
  (221 shorter events, 41.0 us)
Async XLA Ops:
  0.6 38.7 %collective-permute-start.3 = (bf16[3,768,384]{2,1,0:T(8,128)(2,1)}, bf16[3,768,384]{2,1,0:T(8,128)(2,1)S(1)}, u32[]{:S(2)}, u32[]{:S(2)}) collective-permute-start(bf16[3,768,384]{2,1,0:T(8,128)(2,1)} %w_own.1), channel_id=1, source_target_pairs={{1,16},{3,18},{5,20},{7,22},{9,24},{11,26},{13,28},{15,30},{16,1},... | collective-permute-start | bytes 5308424 | tf_op jit(solution)/shard_map/ppermute | solution.py:714
  4.4 28.8 %collective-permute-start = (bf16[512,768]{1,0:T(8,128)(2,1)}, bf16[512,768]{1,0:T(8,128)(2,1)S(1)}, u32[]{:S(2)}, u32[]{:S(2)}) collective-permute-start(bf16[512,768]{1,0:T(8,128)(2,1)} %bitcast.117), channel_id=1, source_target_pairs={{1,16},{3,18},{5,20},{7,22},{9,24},{11,26},{13,28},{15,30},{16,1},... | collective-permute-start | bytes 2359304 | tf_op jit(solution)/shard_map/ppermute | solution.py:714
  6.3 12.0 %collective-permute-start.2 = (s32[1,3]{1,0:T(1,128)}, s32[1,3]{1,0:T(1,128)S(1)}, u32[]{:S(2)}, u32[]{:S(2)}) collective-permute-start(s32[1,3]{1,0:T(1,128)} %param.16), channel_id=1, source_target_pairs={{0,1},{1,0},{2,3},{3,2},{4,5},{5,4},{6,7},{7,6},{8,9},{9,8},{10,11... | collective-permute-start | bytes 44 | tf_op jit(solution)/shard_map/ppermute | solution.py:722
  6.5 44.5 %copy-start.17 = (s32[3]{0:T(128)}, s32[3]{0:T(128)S(1)}, u32[]{:S(2)}) copy-start(s32[3]{0:T(128)S(1)} %pad_add_fusion.flags) | copy-start | bytes 40
  34.1 33.7 %collective-permute-start.8 = (bf16[768,768]{1,0:T(8,128)(2,1)}, bf16[768,768]{1,0:T(8,128)(2,1)}, u32[]{:S(2)}, u32[]{:S(2)}) collective-permute-start(bf16[768,768]{1,0:T(8,128)(2,1)} %constant_dynamic-slice_fusion.3), channel_id=1, source_target_pairs={{1,16},{3,18},{5,20},{7,22},{9,24},{11,26},{13,28},{15,30},{16,1},... | collective-permute-start | bytes 3538952 | tf_op jit(solution)/shard_map/ppermute | solution.py:714
  39.2 4.1 %collective-permute-start.1 = (bf16[512,768]{1,0:T(8,128)(2,1)S(1)}, bf16[512,768]{1,0:T(8,128)(2,1)S(1)}, u32[]{:S(2)}, u32[]{:S(2)}) collective-permute-start(bf16[512,768]{1,0:T(8,128)(2,1)S(1)} %broadcast_select_fusion.7), channel_id=1, source_target_pairs={{0,1},{1,0},{2,3},{3,2},{4,5},{5,4},{6,7},{7,6},{8,9},{9,8},{10,11... | collective-permute-start | bytes 2359304 | tf_op jit(solution)/shard_map/ppermute | solution.py:722
  39.4 39.8 %collective-permute-start.4 = (bf16[384,768]{1,0:T(8,128)(2,1)}, bf16[384,768]{1,0:T(8,128)(2,1)S(1)}, u32[]{:S(2)}, u32[]{:S(2)}) collective-permute-start(bf16[384,768]{1,0:T(8,128)(2,1)} %param.21), channel_id=1, source_target_pairs={{1,16},{3,18},{5,20},{7,22},{9,24},{11,26},{13,28},{15,30},{16,1},... | collective-permute-start | bytes 1769480 | tf_op jit(solution)/shard_map/ppermute | solution.py:714
  43.2 7.8 %copy-start.3 = (f32[1024,128]{1,0:T(8,128)}, f32[1024,128]{1,0:T(8,128)S(1)}, u32[]{:S(2)}) copy-start(f32[1024,128]{1,0:T(8,128)S(1)} %get-tuple-element.206.sin_ref.refs_2_) | copy-start | bytes 1572868
  44.0 18.0 %copy-start = (bf16[1024,768]{1,0:T(8,128)(2,1)}, bf16[1024,768]{1,0:T(8,128)(2,1)S(1)}, u32[]{:S(2)}) copy-start(bf16[1024,768]{1,0:T(8,128)(2,1)S(1)} %maximum_select_fusion.rows_ref.refs_1_) | copy-start | bytes 4718596
  44.8 36.6 %collective-permute-start.6 = (bf16[512,768]{1,0:T(8,128)(2,1)S(1)}, bf16[512,768]{1,0:T(8,128)(2,1)S(1)}, u32[]{:S(2)}, u32[]{:S(2)}) collective-permute-start(bf16[512,768]{1,0:T(8,128)(2,1)S(1)} %bitcast.102), channel_id=1, source_target_pairs={{1,16},{3,18},{5,20},{7,22},{9,24},{11,26},{13,28},{15,30},{16,1},... | collective-permute-start | bytes 2359304 | tf_op jit(solution)/shard_map/ppermute | solution.py:714
  48.5 36.6 %collective-permute-start.9 = (bf16[768,768]{1,0:T(8,128)(2,1)S(1)}, bf16[768,768]{1,0:T(8,128)(2,1)S(1)}, u32[]{:S(2)}, u32[]{:S(2)}) collective-permute-start(bf16[768,768]{1,0:T(8,128)(2,1)S(1)} %copy-done.37), channel_id=1, source_target_pairs={{1,16},{3,18},{5,20},{7,22},{9,24},{11,26},{13,28},{15,30},{16,1},... | collective-permute-start | bytes 3538952 | tf_op jit(solution)/shard_map/ppermute | solution.py:714
  81.2 9.7 %copy-start.29 = (bf16[1024,768]{1,0:T(8,128)(2,1)}, bf16[1024,768]{1,0:T(8,128)(2,1)S(1)}, u32[]{:S(2)}) copy-start(bf16[1024,768]{1,0:T(8,128)(2,1)S(1)} %convolution_convert_fusion.refs_2_.own_ref) | copy-start | bytes 4718596
  81.3 9.6 %collective-permute-start.5 = (bf16[1024,768]{1,0:T(8,128)(2,1)S(1)}, bf16[1024,768]{1,0:T(8,128)(2,1)S(1)}, u32[]{:S(2)}, u32[]{:S(2)}) collective-permute-start(bf16[1024,768]{1,0:T(8,128)(2,1)S(1)} %convolution_convert_fusion.refs_2_.own_ref), channel_id=1, source_target_pairs={{0,1},{1,0},{2,3},{3,2},{4,5},{5,4},{6,7},{7,6},{8,9},{9,8},{10,11... | collective-permute-start | bytes 4718600 | tf_op jit(solution)/shard_map/ppermute | solution.py:722
  81.5 7.6 %collective-permute-start.7 = (bf16[512,768]{1,0:T(8,128)(2,1)S(1)}, bf16[512,768]{1,0:T(8,128)(2,1)S(1)}, u32[]{:S(2)}, u32[]{:S(2)}) collective-permute-start(bf16[512,768]{1,0:T(8,128)(2,1)S(1)} %broadcast_select_fusion.6), channel_id=1, source_target_pairs={{0,1},{1,0},{2,3},{3,2},{4,5},{5,4},{6,7},{7,6},{8,9},{9,8},{10,11... | collective-permute-start | bytes 2359304 | tf_op jit(solution)/shard_map/ppermute | solution.py:722
  82.0 33.6 %collective-permute-start.10 = (bf16[768,768]{1,0:T(8,128)(2,1)}, bf16[768,768]{1,0:T(8,128)(2,1)}, u32[]{:S(2)}, u32[]{:S(2)}) collective-permute-start(bf16[768,768]{1,0:T(8,128)(2,1)} %collective-permute-done.8.refs_8_), channel_id=1, source_target_pairs={{1,3},{3,1},{5,7},{7,5},{9,11},{11,9},{13,15},{15,13},{16,18},{18,... | collective-permute-start | bytes 3538952 | tf_op jit(solution)/shard_map/ppermute | solution.py:718
  85.2 30.5 %collective-permute-start.11 = (bf16[768,768]{1,0:T(8,128)(2,1)S(1)}, bf16[768,768]{1,0:T(8,128)(2,1)}, u32[]{:S(2)}, u32[]{:S(2)}) collective-permute-start(bf16[768,768]{1,0:T(8,128)(2,1)S(1)} %collective-permute-done.9.refs_10_.got_early), channel_id=1, source_target_pairs={{1,3},{3,1},{5,7},{7,5},{9,11},{11,9},{13,15},{15,13},{16,18},{18,... | collective-permute-start | bytes 3538952 | tf_op jit(solution)/shard_map/ppermute | solution.py:718
  134.6 17.6 %collective-permute-start.13 = (bf16[1024,768]{1,0:T(8,128)(2,1)}, bf16[1024,768]{1,0:T(8,128)(2,1)}, u32[]{:S(2)}, u32[]{:S(2)}) collective-permute-start(bf16[1024,768]{1,0:T(8,128)(2,1)} %get-tuple-element.94.back_own), channel_id=1, source_target_pairs={{0,1},{1,0},{2,3},{3,2},{4,5},{5,4},{6,7},{7,6},{8,9},{9,8},{10,11... | collective-permute-start | bytes 4718600 | tf_op jit(solution)/shard_map/ppermute | solution.py:722
  134.6 40.5 %collective-permute-start.17 = (bf16[768,768]{1,0:T(8,128)(2,1)}, bf16[768,768]{1,0:T(8,128)(2,1)}, u32[]{:S(2)}, u32[]{:S(2)}) collective-permute-start(bf16[768,768]{1,0:T(8,128)(2,1)} %get-tuple-element.102), channel_id=1, source_target_pairs={{1,16},{3,18},{5,20},{7,22},{9,24},{11,26},{13,28},{15,30},{16,1},... | collective-permute-start | bytes 3538952 | tf_op jit(solution)/shard_map/ppermute | solution.py:714
  138.8 36.3 %collective-permute-start.16 = (bf16[768,768]{1,0:T(8,128)(2,1)}, bf16[768,768]{1,0:T(8,128)(2,1)}, u32[]{:S(2)}, u32[]{:S(2)}) collective-permute-start(bf16[768,768]{1,0:T(8,128)(2,1)} %get-tuple-element.100), channel_id=1, source_target_pairs={{1,16},{3,18},{5,20},{7,22},{9,24},{11,26},{13,28},{15,30},{16,1},... | collective-permute-start | bytes 3538952 | tf_op jit(solution)/shard_map/ppermute | solution.py:714
  140.9 34.2 %collective-permute-start.15 = (bf16[768,768]{1,0:T(8,128)(2,1)}, bf16[768,768]{1,0:T(8,128)(2,1)}, u32[]{:S(2)}, u32[]{:S(2)}) collective-permute-start(bf16[768,768]{1,0:T(8,128)(2,1)} %get-tuple-element.98), channel_id=1, source_target_pairs={{0,2},{1,3},{2,0},{3,1},{4,6},{5,7},{6,4},{7,5},{8,10},{9,11},{10,... | collective-permute-start | bytes 3538952 | tf_op jit(solution)/shard_map/ppermute | solution.py:726
  152.1 12.4 %copy-start.4 = (f32[1024,128]{1,0:T(8,128)S(1)}, f32[1024,128]{1,0:T(8,128)}, u32[]{:S(2)}) copy-start(f32[1024,128]{1,0:T(8,128)} %copy-done.3) | copy-start | bytes 1572868
  152.1 12.4 %copy-start.6 = (f32[1024,128]{1,0:T(8,128)S(1)}, f32[1024,128]{1,0:T(8,128)}, u32[]{:S(2)}) copy-start(f32[1024,128]{1,0:T(8,128)} %copy-done.5) | copy-start | bytes 1572868
  152.1 30.8 %collective-permute-start.12 = (bf16[512,768]{1,0:T(8,128)(2,1)}, bf16[512,768]{1,0:T(8,128)(2,1)S(1)}, u32[]{:S(2)}, u32[]{:S(2)}) collective-permute-start(bf16[512,768]{1,0:T(8,128)(2,1)} %get-tuple-element.92), channel_id=1, source_target_pairs={{0,1},{1,0},{2,3},{3,2},{4,5},{5,4},{6,7},{7,6},{8,9},{9,8},{10,11... | collective-permute-start | bytes 2359304 | tf_op jit(solution)/shard_map/ppermute | solution.py:722
  165.6 9.5 %copy-start.36 = (bf16[768,768]{1,0:T(8,128)(2,1)S(1)}, bf16[768,768]{1,0:T(8,128)(2,1)}, u32[]{:S(2)}) copy-start(bf16[768,768]{1,0:T(8,128)(2,1)} %get-tuple-element.97) | copy-start | bytes 3538948
  176.8 17.9 %collective-permute-start.19 = (bf16[768,768]{1,0:T(8,128)(2,1)S(1)}, bf16[768,768]{1,0:T(8,128)(2,1)S(1)}, u32[]{:S(2)}, u32[]{:S(2)}) collective-permute-start(bf16[768,768]{1,0:T(8,128)(2,1)S(1)} %add_convert_fusion.1), channel_id=1, source_target_pairs={{1,16},{3,18},{5,20},{7,22},{9,24},{11,26},{13,28},{15,30},{16,1},... | collective-permute-start | bytes 3538952 | tf_op jit(solution)/shard_map/ppermute | solution.py:714
  182.8 13.1 %collective-permute-start.18 = (bf16[768,768]{1,0:T(8,128)(2,1)S(1)}, bf16[768,768]{1,0:T(8,128)(2,1)S(1)}, u32[]{:S(2)}, u32[]{:S(2)}) collective-permute-start(bf16[768,768]{1,0:T(8,128)(2,1)S(1)} %get-tuple-element.186), channel_id=1, source_target_pairs={{0,1},{1,0},{2,3},{3,2},{4,5},{5,4},{6,7},{7,6},{8,9},{9,8},{10,11... | collective-permute-start | bytes 3538952 | tf_op jit(solution)/shard_map/ppermute | solution.py:722
  183.1 38.9 %collective-permute-start.14 = (bf16[512,768]{1,0:T(8,128)(2,1)S(1)}, bf16[512,768]{1,0:T(8,128)(2,1)}, u32[]{:S(2)}, u32[]{:S(2)}) collective-permute-start(bf16[512,768]{1,0:T(8,128)(2,1)S(1)} %add_convert_fusion.2.own_ref), channel_id=1, source_target_pairs={{1,16},{3,18},{5,20},{7,22},{9,24},{11,26},{13,28},{15,30},{16,1},... | collective-permute-start | bytes 2359304 | tf_op jit(solution)/shard_map/ppermute | solution.py:714
  197.2 9.5 %copy-start.27 = (bf16[768,1024]{1,0:T(8,128)(2,1)S(1)}, bf16[768,1024]{1,0:T(8,128)(2,1)}, u32[]{:S(2)}) copy-start(bf16[768,1024]{1,0:T(8,128)(2,1)} %copy-done.26) | copy-start | bytes 4718596
  214.6 11.6 %collective-permute-start.20 = (bf16[512,768]{1,0:T(8,128)(2,1)}, bf16[512,768]{1,0:T(8,128)(2,1)}, u32[]{:S(2)}, u32[]{:S(2)}) collective-permute-start(bf16[512,768]{1,0:T(8,128)(2,1)} %get-tuple-element.111), channel_id=1, source_target_pairs={{0,1},{1,0},{2,3},{3,2},{4,5},{5,4},{6,7},{7,6},{8,9},{9,8},{10,11... | collective-permute-start | bytes 2359304 | tf_op jit(solution)/shard_map/ppermute | solution.py:722
  215.4 7.9 %copy-start.9 = (bf16[1,512,768]{2,1,0:T(8,128)(2,1)S(1)}, bf16[1,512,768]{2,1,0:T(8,128)(2,1)}, u32[]{:S(2)}) copy-start(bf16[1,512,768]{2,1,0:T(8,128)(2,1)} %param.15) | copy-start | bytes 2359300
  215.4 7.9 %copy-start.13 = (f32[512,768]{1,0:T(8,128)S(1)}, f32[512,768]{1,0:T(8,128)}, u32[]{:S(2)}) copy-start(f32[512,768]{1,0:T(8,128)} %copy-done.12) | copy-start | bytes 4718596
  216.9 21.9 %collective-permute-start.48 = (bf16[192,768]{1,0:T(8,128)(2,1)S(1)}, bf16[192,768]{1,0:T(8,128)(2,1)S(1)}, u32[]{:S(2)}, u32[]{:S(2)}) collective-permute-start(bf16[192,768]{1,0:T(8,128)(2,1)S(1)} %get-tuple-element.193), channel_id=1, source_target_pairs={{0,4},{4,8},{8,12},{12,0},{1,5},{5,9},{9,13},{13,1},{2,6},{6,10},{... | collective-permute-start | bytes 884744 | tf_op jit(solution)/shard_map/ppermute | solution.py:761
  218.2 24.9 %collective-permute-start.49 = (bf16[192,768]{1,0:T(8,128)(2,1)S(1)}, bf16[192,768]{1,0:T(8,128)(2,1)S(1)}, u32[]{:S(2)}, u32[]{:S(2)}) collective-permute-start(bf16[192,768]{1,0:T(8,128)(2,1)S(1)} %get-tuple-element.192), channel_id=1, source_target_pairs={{0,8},{4,12},{8,0},{12,4},{1,9},{5,13},{9,1},{13,5},{2,10},{6,14},... | collective-permute-start | bytes 884744 | tf_op jit(solution)/shard_map/ppermute | solution.py:761
  219.3 26.4 %collective-permute-start.50 = (bf16[192,768]{1,0:T(8,128)(2,1)S(1)}, bf16[192,768]{1,0:T(8,128)(2,1)S(1)}, u32[]{:S(2)}, u32[]{:S(2)}) collective-permute-start(bf16[192,768]{1,0:T(8,128)(2,1)S(1)} %get-tuple-element.191), channel_id=1, source_target_pairs={{0,12},{4,0},{8,4},{12,8},{1,13},{5,1},{9,5},{13,9},{2,14},{6,2},{... | collective-permute-start | bytes 884744 | tf_op jit(solution)/shard_map/ppermute | solution.py:761
  222.0 9.1 %collective-permute-start.42 = (bf16[768,384]{1,0:T(8,128)(2,1)S(1)}, bf16[768,384]{1,0:T(8,128)(2,1)S(1)}, u32[]{:S(2)}, u32[]{:S(2)}) collective-permute-start(bf16[768,384]{1,0:T(8,128)(2,1)S(1)} %constant_dynamic-slice_fusion), channel_id=1, source_target_pairs={{0,1},{1,0},{2,3},{3,2},{4,5},{5,4},{6,7},{7,6},{8,9},{9,8},{10,11... | collective-permute-start | bytes 1769480 | tf_op jit(solution)/shard_map/ppermute | solution.py:722
  229.2 1.3 collective-permute-start.22
  229.7 8.9 %copy-start.31 = (bf16[768,768]{1,0:T(8,128)(2,1)S(1)}, bf16[768,768]{1,0:T(8,128)(2,1)}, u32[]{:S(2)}) copy-start(bf16[768,768]{1,0:T(8,128)(2,1)} %broadcast_select_fusion.1) | copy-start | bytes 3538948
  230.5 3.3 %collective-permute-start.23 = (f32[9,768]{1,0:T(8,128)S(1)}, f32[9,768]{1,0:T(8,128)S(1)}, u32[]{:S(2)}, u32[]{:S(2)}) collective-permute-start(f32[9,768]{1,0:T(8,128)S(1)} %fusion.15), channel_id=1, source_target_pairs={{0,2},{1,3},{2,0},{3,1},{4,6},{5,7},{6,4},{7,5},{8,10},{9,11},{10,... | collective-permute-start | bytes 82952 | tf_op jit(solution)/shard_map/ppermute | solution.py:770
  231.0 23.0 %collective-permute-start.27 = (bf16[768,384]{1,0:T(8,128)(2,1)S(1)}, bf16[768,384]{1,0:T(8,128)(2,1)S(1)}, u32[]{:S(2)}, u32[]{:S(2)}) collective-permute-start(bf16[768,384]{1,0:T(8,128)(2,1)S(1)} %get-tuple-element.188), channel_id=1, source_target_pairs={{0,2},{1,3},{2,0},{3,1},{4,6},{5,7},{6,4},{7,5},{8,10},{9,11},{10,... | collective-permute-start | bytes 1769480 | tf_op jit(solution)/shard_map/ppermute | solution.py:726
  233.8 36.7 %collective-permute-start.35 = (bf16[2,768,384]{2,1,0:T(8,128)(2,1)S(1)}, bf16[2,768,384]{2,1,0:T(8,128)(2,1)S(1)}, u32[]{:S(2)}, u32[]{:S(2)}) collective-permute-start(bf16[2,768,384]{2,1,0:T(8,128)(2,1)S(1)} %pad_maximum_fusion), channel_id=1, source_target_pairs={{1,16},{3,18},{5,20},{7,22},{9,24},{11,26},{13,28},{15,30},{16,1},... | collective-permute-start | bytes 3538952 | tf_op jit(solution)/shard_map/ppermute | solution.py:714
  238.8 14.0 %collective-permute-start.24 = (f32[9,768]{1,0:T(8,128)S(1)}, f32[9,768]{1,0:T(8,128)S(1)}, u32[]{:S(2)}, u32[]{:S(2)}) collective-permute-start(f32[9,768]{1,0:T(8,128)S(1)} %add.186), channel_id=1, source_target_pairs={{0,16},{16,0},{1,17},{17,1},{2,18},{18,2},{3,19},{19,3},{4,20},{20... | collective-permute-start | bytes 82952 | tf_op jit(solution)/shard_map/ppermute | solution.py:770
  243.1 44.4 %collective-permute-start.43 = (bf16[192,384]{1,0:T(8,128)(2,1)S(1)}, bf16[192,384]{1,0:T(8,128)(2,1)S(1)}, u32[]{:S(2)}, u32[]{:S(2)}) collective-permute-start(bf16[192,384]{1,0:T(8,128)(2,1)S(1)} %get-tuple-element.197), channel_id=1, source_target_pairs={{0,4},{4,8},{8,12},{12,0},{1,5},{5,9},{9,13},{13,1},{2,6},{6,10},{... | collective-permute-start | bytes 442376 | tf_op jit(solution)/shard_map/ppermute | solution.py:761
  245.7 41.8 %collective-permute-start.44 = (bf16[192,384]{1,0:T(8,128)(2,1)S(1)}, bf16[192,384]{1,0:T(8,128)(2,1)S(1)}, u32[]{:S(2)}, u32[]{:S(2)}) collective-permute-start(bf16[192,384]{1,0:T(8,128)(2,1)S(1)} %get-tuple-element.196), channel_id=1, source_target_pairs={{0,8},{4,12},{8,0},{12,4},{1,9},{5,13},{9,1},{13,5},{2,10},{6,14},... | collective-permute-start | bytes 442376 | tf_op jit(solution)/shard_map/ppermute | solution.py:761
  252.8 4.0 %collective-permute-start.25 = (f32[9,768]{1,0:T(8,128)S(1)}, f32[9,768]{1,0:T(8,128)S(1)}, u32[]{:S(2)}, u32[]{:S(2)}) collective-permute-start(f32[9,768]{1,0:T(8,128)S(1)} %add.187), channel_id=1, source_target_pairs={{0,4},{4,0},{8,12},{12,8},{1,5},{5,1},{9,13},{13,9},{2,6},{6,2},{1... | collective-permute-start | bytes 82952 | tf_op jit(solution)/shard_map/ppermute | solution.py:770
  254.0 10.3 %collective-permute-start.51 = (bf16[192,768]{1,0:T(8,128)(2,1)S(1)}, bf16[192,768]{1,0:T(8,128)(2,1)S(1)}, u32[]{:S(2)}, u32[]{:S(2)}) collective-permute-start(bf16[192,768]{1,0:T(8,128)(2,1)S(1)} %add_convert_fusion.5), channel_id=1, source_target_pairs={{0,2},{1,3},{2,0},{3,1},{4,6},{5,7},{6,4},{7,5},{8,10},{9,11},{10,... | collective-permute-start | bytes 884744 | tf_op jit(solution)/shard_map/ppermute | solution.py:726
  256.8 3.8 %collective-permute-start.26 = (f32[9,768]{1,0:T(8,128)S(1)}, f32[9,768]{1,0:T(8,128)S(1)}, u32[]{:S(2)}, u32[]{:S(2)}) collective-permute-start(f32[9,768]{1,0:T(8,128)S(1)} %add.188), channel_id=1, source_target_pairs={{0,8},{4,12},{8,0},{12,4},{1,9},{5,13},{9,1},{13,5},{2,10},{6,14},... | collective-permute-start | bytes 82952 | tf_op jit(solution)/shard_map/ppermute | solution.py:770
  260.6 26.8 %collective-permute-start.45 = (bf16[192,384]{1,0:T(8,128)(2,1)S(1)}, bf16[192,384]{1,0:T(8,128)(2,1)S(1)}, u32[]{:S(2)}, u32[]{:S(2)}) collective-permute-start(bf16[192,384]{1,0:T(8,128)(2,1)S(1)} %get-tuple-element.195), channel_id=1, source_target_pairs={{0,12},{4,0},{8,4},{12,8},{1,13},{5,1},{9,5},{13,9},{2,14},{6,2},{... | collective-permute-start | bytes 442376 | tf_op jit(solution)/shard_map/ppermute | solution.py:761
  264.3 13.7 %collective-permute-start.28 = (bf16[768,384]{1,0:T(8,128)(2,1)S(1)}, bf16[768,384]{1,0:T(8,128)(2,1)S(1)}, u32[]{:S(2)}, u32[]{:S(2)}) collective-permute-start(bf16[768,384]{1,0:T(8,128)(2,1)S(1)} %fusion.1), channel_id=1, source_target_pairs={{1,16},{3,18},{5,20},{7,22},{9,24},{11,26},{13,28},{15,30},{16,1},... | collective-permute-start | bytes 1769480 | tf_op jit(solution)/shard_map/ppermute | solution.py:714
  270.5 15.9 %collective-permute-start.21 = (bf16[512,768]{1,0:T(8,128)(2,1)S(1)}, bf16[512,768]{1,0:T(8,128)(2,1)S(1)}, u32[]{:S(2)}, u32[]{:S(2)}) collective-permute-start(bf16[512,768]{1,0:T(8,128)(2,1)S(1)} %get-tuple-element.116), channel_id=1, source_target_pairs={{1,16},{3,18},{5,20},{7,22},{9,24},{11,26},{13,28},{15,30},{16,1},... | collective-permute-start | bytes 2359304 | tf_op jit(solution)/shard_map/ppermute | solution.py:714
  278.0 1.6 collective-permute-start.52
  279.6 7.8 %collective-permute-start.29 = (bf16[4,96,384]{2,1,0:T(8,128)(2,1)S(1)}, bf16[4,96,384]{2,1,0:T(8,128)(2,1)S(1)}, u32[]{:S(2)}, u32[]{:S(2)}) collective-permute-start(bf16[4,96,384]{2,1,0:T(8,128)(2,1)S(1)} %constant_dynamic-slice_fusion.1), channel_id=1, source_target_pairs={{0,1},{1,0},{2,3},{3,2},{4,5},{5,4},{6,7},{7,6},{8,9},{9,8},{10,11... | collective-permute-start | bytes 884744 | tf_op jit(solution)/shard_map/ppermute | solution.py:722
  286.4 11.1 %collective-permute-start.36 = (bf16[768,384]{1,0:T(8,128)(2,1)S(1)}, bf16[768,384]{1,0:T(8,128)(2,1)S(1)}, u32[]{:S(2)}, u32[]{:S(2)}) collective-permute-start(bf16[768,384]{1,0:T(8,128)(2,1)S(1)} %dynamic-slice_bitcast_fusion), channel_id=1, source_target_pairs={{0,1},{1,0},{2,3},{3,2},{4,5},{5,4},{6,7},{7,6},{8,9},{9,8},{10,11... | collective-permute-start | bytes 1769480 | tf_op jit(solution)/shard_map/ppermute | solution.py:722
  287.5 3.3 %collective-permute-start.30 = (bf16[96,384]{1,0:T(8,128)(2,1)S(1)}, bf16[96,384]{1,0:T(8,128)(2,1)S(1)}, u32[]{:S(2)}, u32[]{:S(2)}) collective-permute-start(bf16[96,384]{1,0:T(8,128)(2,1)S(1)} %get-tuple-element.203), channel_id=1, source_target_pairs={{0,4},{4,8},{8,12},{12,0},{1,5},{5,9},{9,13},{13,1},{2,6},{6,10},{... | collective-permute-start | bytes 221192 | tf_op jit(solution)/shard_map/ppermute | solution.py:761
  287.6 5.0 %collective-permute-start.31 = (bf16[96,384]{1,0:T(8,128)(2,1)S(1)}, bf16[96,384]{1,0:T(8,128)(2,1)S(1)}, u32[]{:S(2)}, u32[]{:S(2)}) collective-permute-start(bf16[96,384]{1,0:T(8,128)(2,1)S(1)} %get-tuple-element.205), channel_id=1, source_target_pairs={{0,8},{4,12},{8,0},{12,4},{1,9},{5,13},{9,1},{13,5},{2,10},{6,14},... | collective-permute-start | bytes 221192 | tf_op jit(solution)/shard_map/ppermute | solution.py:761
  289.4 7.5 %collective-permute-start.32 = (bf16[96,384]{1,0:T(8,128)(2,1)S(1)}, bf16[96,384]{1,0:T(8,128)(2,1)S(1)}, u32[]{:S(2)}, u32[]{:S(2)}) collective-permute-start(bf16[96,384]{1,0:T(8,128)(2,1)S(1)} %get-tuple-element.204), channel_id=1, source_target_pairs={{0,12},{4,0},{8,4},{12,8},{1,13},{5,1},{9,5},{13,9},{2,14},{6,2},{... | collective-permute-start | bytes 221192 | tf_op jit(solution)/shard_map/ppermute | solution.py:761
  289.5 10.5 %collective-permute-start.46 = (bf16[192,384]{1,0:T(8,128)(2,1)S(1)}, bf16[192,384]{1,0:T(8,128)(2,1)S(1)}, u32[]{:S(2)}, u32[]{:S(2)}) collective-permute-start(bf16[192,384]{1,0:T(8,128)(2,1)S(1)} %add_convert_fusion.7), channel_id=1, source_target_pairs={{0,1},{1,0},{2,3},{3,2},{4,5},{5,4},{6,7},{7,6},{8,9},{9,8},{10,11... | collective-permute-start | bytes 442376 | tf_op jit(solution)/shard_map/ppermute | solution.py:722
  296.9 16.6 %collective-permute-start.33 = (bf16[96,384]{1,0:T(8,128)(2,1)S(1)}, bf16[96,384]{1,0:T(8,128)(2,1)S(1)}, u32[]{:S(2)}, u32[]{:S(2)}) collective-permute-start(bf16[96,384]{1,0:T(8,128)(2,1)S(1)} %fusion.8), channel_id=1, source_target_pairs={{0,1},{1,0},{2,3},{3,2},{4,5},{5,4},{6,7},{7,6},{8,9},{9,8},{10,11... | collective-permute-start | bytes 221192 | tf_op jit(solution)/shard_map/ppermute | solution.py:722
  297.7 5.5 %collective-permute-start.37 = (bf16[192,384]{1,0:T(8,128)(2,1)S(1)}, bf16[192,384]{1,0:T(8,128)(2,1)S(1)}, u32[]{:S(2)}, u32[]{:S(2)}) collective-permute-start(bf16[192,384]{1,0:T(8,128)(2,1)S(1)} %get-tuple-element.198), channel_id=1, source_target_pairs={{0,4},{4,8},{8,12},{12,0},{1,5},{5,9},{9,13},{13,1},{2,6},{6,10},{... | collective-permute-start | bytes 442376 | tf_op jit(solution)/shard_map/ppermute | solution.py:761
  297.8 12.9 %collective-permute-start.38 = (bf16[192,384]{1,0:T(8,128)(2,1)S(1)}, bf16[192,384]{1,0:T(8,128)(2,1)S(1)}, u32[]{:S(2)}, u32[]{:S(2)}) collective-permute-start(bf16[192,384]{1,0:T(8,128)(2,1)S(1)} %get-tuple-element.200), channel_id=1, source_target_pairs={{0,8},{4,12},{8,0},{12,4},{1,9},{5,13},{9,1},{13,5},{2,10},{6,14},... | collective-permute-start | bytes 442376 | tf_op jit(solution)/shard_map/ppermute | solution.py:761
  299.5 13.9 %collective-permute-start.39 = (bf16[192,384]{1,0:T(8,128)(2,1)S(1)}, bf16[192,384]{1,0:T(8,128)(2,1)S(1)}, u32[]{:S(2)}, u32[]{:S(2)}) collective-permute-start(bf16[192,384]{1,0:T(8,128)(2,1)S(1)} %get-tuple-element.199), channel_id=1, source_target_pairs={{0,12},{4,0},{8,4},{12,8},{1,13},{5,1},{9,5},{13,9},{2,14},{6,2},{... | collective-permute-start | bytes 442376 | tf_op jit(solution)/shard_map/ppermute | solution.py:761
  300.1 21.6 %collective-permute-start.47 = (bf16[192,768]{1,0:T(8,128)(2,1)S(1)}, bf16[192,768]{1,0:T(8,128)(2,1)S(1)}, u32[]{:S(2)}, u32[]{:S(2)}) collective-permute-start(bf16[192,768]{1,0:T(8,128)(2,1)S(1)} %maximum_select_fusion.7), channel_id=1, source_target_pairs={{0,2},{1,3},{2,0},{3,1},{4,6},{5,7},{6,4},{7,5},{8,10},{9,11},{10,... | collective-permute-start | bytes 884744 | tf_op jit(solution)/shard_map/ppermute | solution.py:726
  313.5 5.0 %collective-permute-start.40 = (bf16[192,384]{1,0:T(8,128)(2,1)S(1)}, bf16[192,384]{1,0:T(8,128)(2,1)S(1)}, u32[]{:S(2)}, u32[]{:S(2)}) collective-permute-start(bf16[192,384]{1,0:T(8,128)(2,1)S(1)} %fusion.5), channel_id=1, source_target_pairs={{0,2},{1,3},{2,0},{3,1},{4,6},{5,7},{6,4},{7,5},{8,10},{9,11},{10,... | collective-permute-start | bytes 442376 | tf_op jit(solution)/shard_map/ppermute | solution.py:726
  313.6 8.1 %collective-permute-start.34 = (bf16[192,384]{1,0:T(8,128)(2,1)S(1)}, bf16[192,384]{1,0:T(8,128)(2,1)S(1)}, u32[]{:S(2)}, u32[]{:S(2)}) collective-permute-start(bf16[192,384]{1,0:T(8,128)(2,1)S(1)} %maximum_select_fusion.9), channel_id=1, source_target_pairs={{0,2},{1,3},{2,0},{3,1},{4,6},{5,7},{6,4},{7,5},{8,10},{9,11},{10,... | collective-permute-start | bytes 442376 | tf_op jit(solution)/shard_map/ppermute | solution.py:726
  318.5 4.5 %collective-permute-start.41 = (bf16[192,384]{1,0:T(8,128)(2,1)S(1)}, bf16[192,384]{1,0:T(8,128)(2,1)S(1)}, u32[]{:S(2)}, u32[]{:S(2)}) collective-permute-start(bf16[192,384]{1,0:T(8,128)(2,1)S(1)} %add_convert_fusion.8), channel_id=1, source_target_pairs={{0,1},{1,0},{2,3},{3,2},{4,5},{5,4},{6,7},{7,6},{8,9},{9,8},{10,11... | collective-permute-start | bytes 442376 | tf_op jit(solution)/shard_map/ppermute | solution.py:722
  (33 other events, 122.6 us)
